TPU v7x, 32 devices: a whole 2x2x4 slice. The times are simulated.
32 devices in a mesh: phys: 8 (over y, x, core), ang: 4 (over z).
Axes of the slice: x: 2, y: 2, z: 4, core: 2. Of those that a mesh axis runs over, the one named last changes fastest.
Arguments:
- vorticity: float32 [96, 4, 256, 256], P('ang', None, 'phys'), may hold values from -200 to 200
- forcing_mode: int32 [1], replicated, may hold values from 4 to 85
- time_step: float32 [1], replicated, may hold values from 0.003 to 0.005
- rotation: float32 [1], replicated, may hold values from 0.5 to 3
Outputs:
- residual_modes: float32 [2, 88, 256, 384], P(None, 'phys', 'ang')
All inputs are finite; a program needn't handle non-finite values.
Results may differ from a plain program's by a relative error of at most 0.000075.
Values sent between devices are 32-bit elements; how exact they have to be, the bound alone decides.
No kernel may reach another device: no remote copies, remote signals or barrier semaphores. Data moves between devices by JAX's collectives and lax.ppermute only.
A program may use at most 192 MiB of HBM per device.

v0:
```python
import math

import jax
import jax.numpy as jnp
from jax import lax
from jax.sharding import PartitionSpec as P

VISCOSITY = 1.0 / 40.0
HIGHEST = lax.Precision.HIGHEST


def signed(values, length):
    return jnp.where(values < length // 2, values, values - length)


def column_values(positions, plus_rows, minus_rows, drop_rows, half_total, grid_width):
    per_device = plus_rows + minus_rows + drop_rows
    holder = positions // per_device
    offset = positions % per_device
    positive = holder * plus_rows + offset
    negative = -(holder * plus_rows + (offset - plus_rows) + 1)
    drop_total = grid_width - 2 * half_total
    drop_index = holder * drop_rows + offset - plus_rows - minus_rows
    drop_value = jnp.where(
        drop_index < drop_total // 2,
        half_total + drop_index,
        drop_index - drop_total // 2 - grid_width // 2,
    )
    return jnp.where(
        offset < plus_rows,
        positive,
        jnp.where(offset < plus_rows + minus_rows, negative, drop_value),
    )


def dft_tables(positions, mode_vals, length):
    product = jnp.mod(positions[:, None] * mode_vals[None, :], length)
    turning = 2.0 * math.pi / length * product.astype(jnp.float32)
    return (jnp.cos(turning), jnp.sin(turning))


def times_i(values_in, wave_num):
    return jnp.stack([-wave_num * values_in[1], wave_num * values_in[0]])


def flatten_last(values_in):
    return values_in.reshape(
        values_in.shape[0],
        values_in.shape[1],
        values_in.shape[2],
        values_in.shape[3] * values_in.shape[4],
    )


def local(vorticity, forcing_mode, time_step, rotation):
    angle_local, samples, row_count, grid_width = vorticity.shape
    phys_count = lax.axis_size("phys")
    ang_count = lax.axis_size("ang")
    angle_total = angle_local * ang_count
    field_count = angle_local * samples
    plus_rows = (grid_width // 3 + phys_count) // phys_count
    half_total = plus_rows * phys_count
    drop_rows = (grid_width - 2 * half_total) // phys_count
    local_rows = plus_rows + plus_rows + drop_rows
    phys_index = lax.axis_index("phys")
    grid_index = jnp.arange(grid_width, dtype=jnp.int32)
    all_columns = column_values(
        jnp.arange(local_rows * phys_count, dtype=jnp.int32),
        plus_rows,
        plus_rows,
        drop_rows,
        half_total,
        grid_width,
    )
    local_columns = column_values(
        phys_index * local_rows + jnp.arange(local_rows, dtype=jnp.int32),
        plus_rows,
        plus_rows,
        drop_rows,
        half_total,
        grid_width,
    )
    inv_width = 1.0 / grid_width
    x_cos, x_sin = dft_tables(grid_index, all_columns, grid_width)
    fwd_x_cos = x_cos * inv_width
    fwd_x_sin = x_sin * inv_width
    column_weight = jnp.ones(all_columns.shape, jnp.float32)
    back_x_cos = x_cos * column_weight[None, :]
    back_x_sin = x_sin * column_weight[None, :]
    y_modes = signed(grid_index, grid_width)
    y_cos, y_sin = dft_tables(grid_index, y_modes, grid_width)
    fwd_y_cos = y_cos * inv_width
    fwd_y_sin = y_sin * inv_width
    wave_x = local_columns.astype(jnp.float32)[:, None]
    wave_y = y_modes.astype(jnp.float32)[None, :]
    mode_limit = grid_width // 3
    keep_mask = ((jnp.abs(wave_x) <= mode_limit) & (jnp.abs(wave_y) <= mode_limit)).astype(
        jnp.float32
    )
    wave_sq = wave_x * wave_x + wave_y * wave_y
    inverse_sq = jnp.where(wave_sq > 0, 1.0 / jnp.where(wave_sq > 0, wave_sq, 1.0), 0.0)
    forcing = forcing_mode[0].astype(jnp.float32)
    rows_global = (phys_index * row_count + jnp.arange(row_count, dtype=jnp.int32)).astype(
        jnp.float32
    )
    force_rows = (-forcing * jnp.cos(forcing * (2 * jnp.pi * rows_global / grid_width)))[:, None]

    def along_y(pieces):
        real_in = pieces[0]
        imag_in = pieces[1]
        out_real = jnp.einsum("fky,yq->fkq", real_in, fwd_y_cos, precision=HIGHEST) + jnp.einsum(
            "fky,yq->fkq", imag_in, fwd_y_sin, precision=HIGHEST
        )
        out_imag = jnp.einsum("fky,yq->fkq", imag_in, fwd_y_cos, precision=HIGHEST) - jnp.einsum(
            "fky,yq->fkq", real_in, fwd_y_sin, precision=HIGHEST
        )
        return jnp.stack([out_real, out_imag])

    def to_modes(grid_fields):
        real_part = jnp.einsum("fyx,xk->fky", grid_fields, fwd_x_cos, precision=HIGHEST)
        imag_part = -jnp.einsum("fyx,xk->fky", grid_fields, fwd_x_sin, precision=HIGHEST)
        stacked = jnp.stack([real_part, imag_part])
        modes_out = along_y(
            lax.all_to_all(stacked, "phys", split_axis=2, concat_axis=3, tiled=True)
        )
        return modes_out * keep_mask

    def along_x(pieces):
        return jnp.einsum("gky,xk->gyx", pieces[0], back_x_cos, precision=HIGHEST) - jnp.einsum(
            "gky,xk->gyx", pieces[1], back_x_sin, precision=HIGHEST
        )

    def to_grid(spectra):
        real_in = spectra[0]
        imag_in = spectra[1]
        grid_real = jnp.einsum("gkq,yq->gky", real_in, y_cos, precision=HIGHEST) - jnp.einsum(
            "gkq,yq->gky", imag_in, y_sin, precision=HIGHEST
        )
        grid_imag = jnp.einsum("gkq,yq->gky", imag_in, y_cos, precision=HIGHEST) + jnp.einsum(
            "gkq,yq->gky", real_in, y_sin, precision=HIGHEST
        )
        stacked = jnp.stack([grid_real, grid_imag])
        return along_x(lax.all_to_all(stacked, "phys", split_axis=3, concat_axis=2, tiled=True))

    def tendency(spectrum):
        stream = spectrum * inverse_sq
        fields = jnp.concatenate(
            [
                times_i(stream, wave_y),
                -times_i(stream, wave_x),
                times_i(spectrum, wave_x),
                times_i(spectrum, wave_y),
            ],
            axis=1,
        )
        grid_fields = to_grid(fields)
        vel_x = grid_fields[:field_count]
        vel_y = grid_fields[field_count : 2 * field_count]
        grad_x = grid_fields[2 * field_count : 3 * field_count]
        grad_y = grid_fields[3 * field_count :]
        return (
            to_modes(force_rows - (vel_x * grad_x + vel_y * grad_y))
            - VISCOSITY * wave_sq * spectrum
        )

    angle_index = jnp.arange(angle_total, dtype=jnp.int32)
    angle_cos, angle_sin = dft_tables(angle_index, angle_index, angle_total)
    angle_factor = 1.0 / math.sqrt(angle_total)
    angle_cos = angle_cos * angle_factor
    angle_sin = angle_sin * angle_factor
    signed_angle = signed(angle_index, angle_total).astype(jnp.float32)
    turn_cos = jnp.cos(signed_angle * rotation[0])
    turn_sin = jnp.sin(signed_angle * rotation[0])

    def angle_raw(pieces):
        real_in = pieces[0]
        imag_in = pieces[1]
        out_real = jnp.einsum("jskq,jm->kqsm", real_in, angle_cos, precision=HIGHEST) + jnp.einsum(
            "jskq,jm->kqsm", imag_in, angle_sin, precision=HIGHEST
        )
        out_imag = jnp.einsum("jskq,jm->kqsm", imag_in, angle_cos, precision=HIGHEST) - jnp.einsum(
            "jskq,jm->kqsm", real_in, angle_sin, precision=HIGHEST
        )
        return jnp.stack([out_real, out_imag])

    def arrange(values_in):
        return values_in[:, :, :plus_rows].reshape(2, angle_local, samples, plus_rows, grid_width)

    spectrum = to_modes(vorticity.reshape(field_count, row_count, grid_width))
    time_value = time_step[0]
    section_one = tendency(spectrum)
    second = tendency(spectrum + 0.5 * time_value * section_one)
    advanced = spectrum + time_value * second
    pieces = (
        lax.all_to_all(arrange(advanced), "ang", split_axis=4, concat_axis=1, tiled=True),
        lax.all_to_all(arrange(spectrum), "ang", split_axis=4, concat_axis=1, tiled=True),
    )
    turned_pieces = pieces[1]
    plain = angle_raw(turned_pieces)
    return flatten_last(
        angle_raw(pieces[0])
        - jnp.stack(
            [turn_cos * plain[0] - turn_sin * plain[1], turn_sin * plain[0] + turn_cos * plain[1]]
        )
    )


def solution(mesh):
    in_specs = (P("ang", None, "phys", None), P(), P(), P())
    out_specs = P(None, "phys", "ang", None)
    return jax.shard_map(local, mesh=mesh, in_specs=in_specs, out_specs=out_specs, check_vma=False)
```

profile of v0, /device:TPU:0, one launch (start us, length us, event | category | flops | bytes accessed | tf_op | source)
XLA Modules:
  0.0 1904.2 jit_solution(5813040505058667416)
XLA Ops:
  1.9 5.1 negate_bitcast_fusion.2
  7.0 5.1 fusion.53
  15.6 9.4 copy.154
  25.0 5.4 all-to-all-start
  32.6 92.3 %all-to-all-done = f32[2,96,256,32]{1,3,0,2:T(8,128)} async-done(((f32[2,96,256,32]{1,3,0,2:T(8,128)}), f32[2,96,256,32]{1,3,0,2:T(8,128)}, u32[]{:S(2)}, u32[]{:S(2)}) %all-to-all-start) | async-done | bytes 6291488 | tf_op jit(solution)/shard_map/all_to_all | solution.py:124
  143.5 5.1 copy.157
  159.9 5.7 add_bitcast_fusion.4
  169.6 9.4 slice_multiply_fusion.16
  182.5 15.6 maximum_maximum_fusion
  198.1 14.8 slice_bitcast_fusion.3
  212.8 19.7 %fusion.16 = f32[384,32,256]{2,0,1:T(8,128)} fusion(f32[384,32,256]{2,1,0:T(8,128)S(1)} %get-tuple-element.16, s32[256]{0:T(256)S(1)} %compare_select_fusion), kind=kOutput, calls=%fused_computation.28 | convolution fusion | flops 9664593920 | bytes 25166848 | tf_op jit(solution)/shard_map/gkq,yq->gky/dot_general | solution.py:139
  232.5 19.8 %fusion.18 = f32[384,32,256]{2,0,1:T(8,128)} fusion(f32[384,32,256]{2,1,0:T(8,128)S(1)} %get-tuple-element.16, s32[256]{0:T(256)S(1)} %compare_select_fusion), kind=kOutput, calls=%fused_computation.30 | convolution fusion | flops 9664593920 | bytes 25166848 | tf_op jit(solution)/shard_map/gkq,yq->gky/dot_general | solution.py:136
  252.3 26.1 %add_bitcast_fusion.1 = f32[1,384,32,256]{3,1,2,0:T(8,128)} fusion(f32[384,32,256]{2,0,1:T(8,128)} %fusion.16, f32[384,32,256]{2,1,0:T(8,128)} %get-tuple-element.15, s32[256]{0:T(256)S(1)} %compare_select_fusion), kind=kOutput, calls=%fused_computation.18 | convolution fusion | flops 9667739648 | bytes 37749760 | tf_op jit(solution)/shard_map/gkq,yq->gky/dot_general | solution.py:139
  278.4 26.3 %subtract_bitcast_fusion.1 = f32[1,384,32,256]{3,1,2,0:T(8,128)} fusion(f32[384,32,256]{2,0,1:T(8,128)} %fusion.18, f32[384,32,256]{2,1,0:T(8,128)} %get-tuple-element.15, s32[256]{0:T(256)S(1)} %compare_select_fusion), kind=kOutput, calls=%fused_computation.19 | convolution fusion | flops 9667739648 | bytes 37749760 | tf_op jit(solution)/shard_map/gkq,yq->gky/dot_general | solution.py:136
  304.7 17.4 pad_maximum_fusion
  322.1 25.1 %copy.166 = f32[2,384,32,256]{1,2,0,3:T(8,128)} copy(f32[2,384,32,256]{3,1,2,0:T(8,128)} %pad_maximum_fusion) | data formatting | bytes 50331648 | tf_op jit(solution)/shard_map/stack | solution.py:142
  347.2 278.2 %all_to_all.105 = f32[2,384,32,256]{1,2,0,3:T(8,128)S(1)} all-to-all(f32[2,384,32,256]{1,2,0,3:T(8,128)} %copy.166), channel_id=1, replica_groups=mesh['phys'=8,'ang'=4] {'phys'}, dimensions={3} | all-to-all | bytes 50331648 | tf_op jit(solution)/shard_map/all_to_all | solution.py:143
  625.4 16.7 copy.167
  642.1 19.8 %fusion.407 = (f32[1,384,8,32,32]{1,4,2,3,0:T(8,128)}, f32[1,384,8,32,32]{1,4,2,3,0:T(8,128)}) fusion(f32[2,384,8,32,32]{1,4,2,3,0:T(8,128)} %bitcast.217), kind=kLoop, calls=%fused_computation.447 | loop fusion | bytes 50331648 | tf_op jit(solution)/shard_map/slice | solution.py:129
  661.9 11.0 copy.170
  672.9 30.5 %fusion.4 = f32[384,32,256]{2,0,1:T(8,128)} fusion(f32[384,256,32]{0,2,1:T(8,128)} %bitcast.223, s32[256]{0:T(256)S(1)} %copy-done.22), kind=kOutput, calls=%fused_computation.12 | convolution fusion | flops 9664593920 | bytes 25166848 | tf_op jit(solution)/shard_map/gky,xk->gyx/dot_general | solution.py:129
  703.5 11.0 copy.168
  714.5 32.7 %fusion.35 = f32[384,32,256]{2,0,1:T(8,128)} fusion(f32[384,32,256]{2,0,1:T(8,128)} %fusion.4, f32[384,256,32]{0,2,1:T(8,128)} %bitcast.225, s32[256]{0:T(256)S(1)} %copy-done.22), kind=kOutput, calls=%fused_computation.46 | convolution fusion | flops 9667739648 | bytes 37749760 | tf_op jit(solution)/shard_map/gky,xk->gyx/dot_general | solution.py:129
  747.2 6.3 fusion.48
  764.6 9.4 copy.172
  779.6 93.4 %all-to-all-done.2 = f32[2,96,256,32]{1,3,0,2:T(8,128)} async-done(((f32[2,96,256,32]{1,3,0,2:T(8,128)}), f32[2,96,256,32]{1,3,0,2:T(8,128)}, u32[]{:S(2)}, u32[]{:S(2)}) %all-to-all-start.2) | async-done | bytes 6291488 | tf_op jit(solution)/shard_map/all_to_all | solution.py:124
  886.8 5.3 fusion.86
  894.7 5.5 copy.175
  900.3 5.7 fusion.88
  916.0 9.4 slice_multiply_fusion.8
  928.9 15.6 maximum_maximum_fusion.1
  944.4 14.8 slice_bitcast_fusion.1
  959.2 19.5 %fusion.8 = f32[384,32,256]{2,0,1:T(8,128)} fusion(f32[384,32,256]{2,1,0:T(8,128)S(1)} %get-tuple-element.12, s32[256]{0:T(256)S(1)} %compare_select_fusion), kind=kOutput, calls=%fused_computation.20 | convolution fusion | flops 9664593920 | bytes 25166848 | tf_op jit(solution)/shard_map/gkq,yq->gky/dot_general | solution.py:139
  978.7 19.8 %fusion.10 = f32[384,32,256]{2,0,1:T(8,128)} fusion(f32[384,32,256]{2,1,0:T(8,128)S(1)} %get-tuple-element.12, s32[256]{0:T(256)S(1)} %compare_select_fusion), kind=kOutput, calls=%fused_computation.22 | convolution fusion | flops 9664593920 | bytes 25166848 | tf_op jit(solution)/shard_map/gkq,yq->gky/dot_general | solution.py:136
  998.5 26.3 %add_bitcast_fusion = f32[1,384,32,256]{3,1,2,0:T(8,128)} fusion(f32[384,32,256]{2,0,1:T(8,128)} %fusion.8, f32[384,32,256]{2,1,0:T(8,128)} %get-tuple-element.11, s32[256]{0:T(256)S(1)} %compare_select_fusion), kind=kOutput, calls=%fused_computation.16 | convolution fusion | flops 9667739648 | bytes 37749760 | tf_op jit(solution)/shard_map/gkq,yq->gky/dot_general | solution.py:139
  1024.8 26.0 %subtract_bitcast_fusion = f32[1,384,32,256]{3,1,2,0:T(8,128)} fusion(f32[384,32,256]{2,0,1:T(8,128)} %fusion.10, f32[384,32,256]{2,1,0:T(8,128)} %get-tuple-element.11, s32[256]{0:T(256)S(1)} %compare_select_fusion), kind=kOutput, calls=%fused_computation.17 | convolution fusion | flops 9667739648 | bytes 37749760 | tf_op jit(solution)/shard_map/gkq,yq->gky/dot_general | solution.py:136
  1050.8 17.4 pad_maximum_fusion.1
  1068.2 25.1 %copy.184 = f32[2,384,32,256]{1,2,0,3:T(8,128)} copy(f32[2,384,32,256]{3,1,2,0:T(8,128)} %pad_maximum_fusion.1) | data formatting | bytes 50331648 | tf_op jit(solution)/shard_map/stack | solution.py:142
  1093.3 278.2 %all_to_all.106 = f32[2,384,32,256]{1,2,0,3:T(8,128)S(1)} all-to-all(f32[2,384,32,256]{1,2,0,3:T(8,128)} %copy.184), channel_id=1, replica_groups=mesh['phys'=8,'ang'=4] {'phys'}, dimensions={3} | all-to-all | bytes 50331648 | tf_op jit(solution)/shard_map/all_to_all | solution.py:143
  1371.5 16.7 copy.185
  1388.2 19.8 %fusion.406 = (f32[1,384,8,32,32]{1,4,2,3,0:T(8,128)}, f32[1,384,8,32,32]{1,4,2,3,0:T(8,128)}) fusion(f32[2,384,8,32,32]{1,4,2,3,0:T(8,128)} %bitcast.218), kind=kLoop, calls=%fused_computation.446 | loop fusion | bytes 50331648 | tf_op jit(solution)/shard_map/slice | solution.py:129
  1408.0 11.0 copy.188
  1419.0 30.7 %fusion = f32[384,32,256]{2,0,1:T(8,128)} fusion(f32[384,256,32]{0,2,1:T(8,128)} %bitcast.224, s32[256]{0:T(256)S(1)} %copy-done.23), kind=kOutput, calls=%fused_computation.8 | convolution fusion | flops 9664593920 | bytes 25166848 | tf_op jit(solution)/shard_map/gky,xk->gyx/dot_general | solution.py:129
  1449.8 11.0 copy.186
  1460.8 32.7 %fusion.38 = f32[384,32,256]{2,0,1:T(8,128)} fusion(f32[384,32,256]{2,0,1:T(8,128)} %fusion, f32[384,256,32]{0,2,1:T(8,128)} %bitcast.226, s32[256]{0:T(256)S(1)} %copy-done.23), kind=kOutput, calls=%fused_computation.47 | convolution fusion | flops 9667739648 | bytes 37749760 | tf_op jit(solution)/shard_map/gky,xk->gyx/dot_general | solution.py:129
  1493.5 6.3 fusion.46
  1510.9 9.4 copy.190
  1525.4 94.0 %all-to-all-done.4 = f32[2,96,256,32]{1,3,0,2:T(8,128)} async-done(((f32[2,96,256,32]{1,3,0,2:T(8,128)}), f32[2,96,256,32]{1,3,0,2:T(8,128)}, u32[]{:S(2)}, u32[]{:S(2)}) %all-to-all-start.4) | async-done | bytes 6291488 | tf_op jit(solution)/shard_map/all_to_all | solution.py:124
  1633.3 5.3 fusion.82
  1641.1 5.3 copy.193
  1646.5 5.7 fusion.84
  1652.2 6.6 subtract_bitcast_fusion.2
  1666.0 14.1 copy.198
  1680.1 17.8 reshape.362
  1697.9 5.7 all-to-all-start.5
  1703.6 13.5 copy.208
  1717.1 17.8 reshape.364
  1734.9 15.4 all-to-all-done.5
  1756.4 7.3 reduce
  1763.7 19.6 %reshape.363 = f32[256,2,11,4,24]{4,3,2,1,0:T(4,128)} reshape(f32[4,135168]{1,0:T(4,128)S(1)} %reduce) | data formatting | bytes 4325376
  1783.3 11.4 copy.218
  1817.6 7.5 reduce.1
  1825.2 19.6 %reshape.365 = f32[256,2,11,4,24]{4,3,2,1,0:T(4,128)} reshape(f32[4,135168]{1,0:T(4,128)S(1)} %reduce.1) | data formatting | bytes 4325376
  1844.8 11.2 copy.219
  (167 shorter events, 205.4 us)
Async XLA Ops:
  0.0 1.9 copy-start
  1.9 5.1 copy-start.21
  25.0 99.9 %all-to-all-start = ((f32[2,96,256,32]{1,3,0,2:T(8,128)}), f32[2,96,256,32]{1,3,0,2:T(8,128)}, u32[]{:S(2)}, u32[]{:S(2)}) async-start(f32[2,96,256,32]{1,3,0,2:T(8,128)} %copy.154), calls=%async_computation | async-start | bytes 16777216 | tf_op jit(solution)/shard_map/all_to_all | solution.py:124
  31.2 138.3 %copy-start.32 = (f32[32]{0:T(128)}, f32[32]{0:T(128)S(1)}, u32[]{:S(2)}) copy-start(f32[32]{0:T(128)S(1)} %fusion.225) | copy-start | bytes 388
  31.2 138.3 %copy-start.28 = (f32[256]{0:T(256)}, f32[256]{0:T(256)S(1)}, u32[]{:S(2)}) copy-start(f32[256]{0:T(256)S(1)} %fusion.230) | copy-start | bytes 3076
  31.3 138.3 %copy-start.30 = (f32[256]{0:T(256)}, f32[256]{0:T(256)S(1)}, u32[]{:S(2)}) copy-start(f32[256]{0:T(256)S(1)} %fusion.228) | copy-start | bytes 3076
  31.9 137.7 %copy-start.26 = (f32[32]{0:T(128)}, f32[32]{0:T(128)S(1)}, u32[]{:S(2)}) copy-start(f32[32]{0:T(128)S(1)} %get-tuple-element.58) | copy-start | bytes 388
  31.9 133.7 %copy-start.15 = (f32[32,256]{1,0:T(8,128)}, f32[32,256]{1,0:T(8,128)S(1)}, u32[]{:S(2)}) copy-start(f32[32,256]{1,0:T(8,128)S(1)} %and_convert_fusion) | copy-start | bytes 98308
  32.6 133.0 %copy-start.17 = (f32[32,256]{1,0:T(8,128)}, f32[32,256]{1,0:T(8,128)S(1)}, u32[]{:S(2)}) copy-start(f32[32,256]{1,0:T(8,128)S(1)} %get-tuple-element.56) | copy-start | bytes 98308
  148.7 3.7 copy-start.4
  169.5 9.4 copy-start.2
  661.9 11.0 copy-start.22
  714.5 32.7 %copy-start.24 = (f32[32]{0:T(128)S(1)}, f32[32]{0:T(128)}, u32[]{:S(2)}) copy-start(f32[32]{0:T(128)} %get-tuple-element.57) | copy-start | bytes 388
  774.0 99.0 %all-to-all-start.2 = ((f32[2,96,256,32]{1,3,0,2:T(8,128)}), f32[2,96,256,32]{1,3,0,2:T(8,128)}, u32[]{:S(2)}, u32[]{:S(2)}) async-start(f32[2,96,256,32]{1,3,0,2:T(8,128)} %copy.172), calls=%async_computation.2 | async-start | bytes 16777216 | tf_op jit(solution)/shard_map/all_to_all | solution.py:124
  886.8 5.3 copy-start.6
  900.3 5.8 copy-start.5
  900.3 5.8 copy-start.8
  906.0 7.8 slice-start
  909.9 3.9 slice-start.1
  909.9 3.9 copy-start.16
  909.9 3.9 copy-start.18
  909.9 3.9 copy-start.19
  913.9 2.1 copy-start.27
  913.9 2.1 copy-start.29
  913.9 2.1 copy-start.31
  913.9 2.1 copy-start.33
  915.9 9.4 copy-start.3
  1408.0 11.0 copy-start.23
  1460.8 32.7 %copy-start.25 = (f32[32]{0:T(128)S(1)}, f32[32]{0:T(128)}, u32[]{:S(2)}) copy-start(f32[32]{0:T(128)} %get-tuple-element.57) | copy-start | bytes 388
  1520.3 5.1 copy-start.20
  1520.3 99.1 %all-to-all-start.4 = ((f32[2,96,256,32]{1,3,0,2:T(8,128)}), f32[2,96,256,32]{1,3,0,2:T(8,128)}, u32[]{:S(2)}, u32[]{:S(2)}) async-start(f32[2,96,256,32]{1,3,0,2:T(8,128)} %copy.190), calls=%async_computation.4 | async-start | bytes 16777216 | tf_op jit(solution)/shard_map/all_to_all | solution.py:124
  1633.2 5.3 copy-start.7
  1646.4 16.1 slice-start.4
  1652.2 10.4 slice-start.2
  1652.2 10.4 slice-start.5
  1658.8 3.8 slice-start.3
  1658.8 3.8 slice-start.6
  1697.9 52.4 %all-to-all-start.5 = ((f32[4,1,135168]{2,1,0:T(1,128)}), f32[4,1,135168]{2,1,0:T(1,128)}, u32[]{:S(2)}, u32[]{:S(2)}) async-start(f32[4,1,135168]{2,1,0:T(1,128)} %reshape.362), calls=%async_computation.5 | async-start | bytes 4325376 | tf_op jit(solution)/shard_map/all_to_all | solution.py:195
  1750.3 67.3 %all-to-all-start.6 = ((f32[4,1,135168]{2,1,0:T(1,128)}), f32[4,1,135168]{2,1,0:T(1,128)}, u32[]{:S(2)}, u32[]{:S(2)}) async-start(f32[4,1,135168]{2,1,0:T(1,128)} %reshape.364), calls=%async_computation.6 | async-start | bytes 4325376 | tf_op jit(solution)/shard_map/all_to_all | solution.py:196
  1863.6 4.1 copy-start.9
  1871.1 5.2 copy-start.13
  1871.1 5.2 copy-start.14
  1876.7 5.0 copy-start.12
  1883.2 5.2 copy-start.10
  1892.1 2.7 copy-start.11
  1896.8 6.9 copy-start.1
where the time goes:
time: 1920 us; the launch traced here: 1900 us
  blocking collectives  556 us (29%)
  local copies, waits for them, and re-layouts  461 us (24%)
  matrix products  412 us (21%)
  waiting for transfers between devices  295 us (15%)
  other arithmetic  150 us (8%)
  starting transfers between devices  26 us (1%)
    all_to_all x2, blocking collectives, to_grid(): lax.all_to_all(stacked, 'phys', split_axis=3, concat_axis=2, tiled=True)  556 us
    all_to_all x3, waiting for transfers between devices, to_modes(): lax.all_to_all(stacked, 'phys', split_axis=2, concat_axis=3, tiled=True)  280 us
    unnamed x84, local copies, waits for them, and re-layouts  77 us
    dot_general x2, matrix products, along_x(): jnp.einsum('gky,xk->gyx', pieces[0], back_x_cos, precision=HIGHEST)  65.4 us
    slice x4, local copies, waits for them, and re-layouts, along_x(): pieces[0]  61.6 us
    dot_general x2, matrix products, along_x(): jnp.einsum('gky,xk->gyx', pieces[1], back_x_sin, precision=HIGHEST)  61.2 us
    dot_general x2, matrix products, to_grid(): jnp.einsum('gkq,yq->gky', real_in, y_sin, precision=HIGHEST)  52.4 us
    dot_general x2, matrix products, to_grid(): jnp.einsum('gkq,yq->gky', real_in, y_cos, precision=HIGHEST)  52.3 us
  transfers between devices with their start and end apart: 5, of which 4 were waited for; matrix products, arithmetic and copies ran while one was open for 5% of the time, Pallas kernels for 0%

commit v1 on v0

v1 whole, which is shorter than its diff:
```python
import functools
import math

import jax
import jax.numpy as jnp
import ml_dtypes
import numpy as np
from jax import lax
from jax.experimental import pallas as pl
from jax.experimental.pallas import tpu as pltpu
from jax.sharding import PartitionSpec as P

VISCOSITY = 1.0 / 40.0
F32 = jnp.float32
BF16 = jnp.bfloat16


def split_table(table):
    table = np.asarray(table, np.float32)
    high = table.astype(ml_dtypes.bfloat16)
    low = (table - high.astype(np.float32)).astype(ml_dtypes.bfloat16)
    return high, low


def signed(values, length):
    return np.where(values < length // 2, values, values - length)


def make_tables(width, phys, ang):
    limit = width // 3
    half = width // 2
    plus = (limit + phys) // phys
    slots = plus
    while (slots * phys) % 16 or (phys == 8 and slots * 12 % 8):
        slots += 1
    slot = np.arange(slots * phys)
    kx = np.where(slot % slots < plus, (slot // slots) * plus + slot % slots, -1)
    kx_keep = ((kx >= 0) & (kx <= limit)).astype(np.float64)
    kx = np.maximum(kx, 0)
    block = width // ang
    lane = np.arange(width)
    owner = lane // block
    part = (lane % block) // (block // 2)
    even_index = owner * block + 2 * (lane % (block // 2))
    turn = 2.0 * math.pi / width
    grid = np.arange(width)

    def angle(left, right):
        return turn * np.mod(left[:, None] * right[None, :], width)

    x_turn = angle(kx, grid)
    fwd_x = np.concatenate([np.cos(x_turn), -np.sin(x_turn)]) / width
    fwd_x = fwd_x * np.concatenate([kx_keep, kx_keep])[:, None]
    weight = (np.where(kx == 0, 1.0, 2.0) * kx_keep)[:, None]
    inv_x = np.concatenate([weight * np.cos(x_turn), -weight * np.sin(x_turn)]).T
    inv_kx = np.concatenate(
        [-weight * kx[:, None] * np.sin(x_turn), -weight * kx[:, None] * np.cos(x_turn)]
    ).T
    fwd_y, inv_y, lane_ky = [], [], []
    for parity in (0, 1):
        ky = signed(even_index + parity, width)
        keep = (np.abs(ky) <= limit).astype(np.float64)
        lane_ky.append(ky)
        y_turn = angle(np.arange(half), ky)
        cos_y, sin_y = np.cos(y_turn) * keep, np.sin(y_turn) * keep
        real_out = part == 0
        from_real = np.where(real_out, cos_y, -sin_y)
        from_imag = np.where(real_out, sin_y, cos_y)
        fwd_y.append(np.concatenate([from_real, from_imag]) / width)
        real_back = np.where(real_out, cos_y, -sin_y).T
        imag_back = np.where(real_out, sin_y, cos_y).T
        scale = ky[:, None]
        inv_y.append(
            np.concatenate(
                [real_back, imag_back, -scale * imag_back, scale * real_back], axis=1
            )
        )
    lanes = np.concatenate(lane_ky).astype(np.float32)
    wave_sq = kx.astype(np.float32)[:, None] ** 2 + lanes[None, :] ** 2
    inverse_sq = np.where(wave_sq > 0, 1.0 / np.where(wave_sq > 0, wave_sq, 1.0), 0.0)
    return dict(
        plus=plus,
        slots=slots,
        fwd_x=split_table(fwd_x),
        inv_x=split_table(inv_x),
        inv_kx=split_table(inv_kx),
        fwd_y=[split_table(t) for t in fwd_y],
        inv_y=[split_table(t) for t in inv_y],
        inverse_sq=inverse_sq.astype(np.float32),
        damping=(np.float32(VISCOSITY) * wave_sq).astype(np.float32),
    )


def split(values):
    high = values.astype(BF16)
    low = (values - high.astype(F32)).astype(BF16)
    return high, low


def right_mul(values, high_ref, low_ref):
    high, low = split(values)
    left = jnp.concatenate([high, low, high], axis=1)
    right = jnp.concatenate([high_ref[...], high_ref[...], low_ref[...]], axis=0)
    return jnp.dot(left, right, preferred_element_type=F32)


def left_mul(high_ref, low_ref, values):
    high, low = split(values)
    left = jnp.concatenate([high_ref[...], low_ref[...], high_ref[...]], axis=1)
    right = jnp.concatenate([high, high, low], axis=0)
    return jnp.dot(left, right, preferred_element_type=F32)


def forward_y(rows, tables):
    count = rows.shape[0] // 2
    half = rows.shape[1] // 2
    real, imag = rows[:count], rows[count:]
    even = jnp.concatenate(
        [real[:, :half] + real[:, half:], imag[:, :half] + imag[:, half:]], axis=1
    )
    odd = jnp.concatenate(
        [real[:, :half] - real[:, half:], imag[:, :half] - imag[:, half:]], axis=1
    )
    return jnp.concatenate(
        [right_mul(even, tables[0], tables[1]), right_mul(odd, tables[2], tables[3])], axis=1
    )


def store_send(send_ref, modes, field, field_count, interleave):
    count = modes.shape[0]
    pieces = [modes[:, 128 * b : 128 * (b + 1)] for b in range(4)]
    if interleave:
        low_lane = lax.broadcasted_iota(jnp.int32, pieces[0].shape, 1) < 64
        out = []
        for b in range(2):
            even, odd = pieces[b], pieces[b + 2]
            out.append(jnp.where(low_lane, even, pltpu.roll(odd, 64, 1)))
            out.append(jnp.where(low_lane, pltpu.roll(even, 64, 1), odd))
        pieces = out
    for b in range(4):
        send_ref[b, pl.ds(field, count, stride=field_count), :] = pieces[b]


def spectrum_kernel(interleave, field_count, x_ref, fx_hi, fx_lo, e_hi, e_lo, o_hi, o_lo, s_ref, send_ref):
    width = x_ref.shape[3]
    grid_field = x_ref[:, 0].reshape(width, width)
    high, low = split(grid_field)
    left = jnp.concatenate([fx_hi[...], fx_lo[...], fx_hi[...]], axis=1)
    right = jnp.concatenate([high, high, low], axis=1)
    rows = lax.dot_general(left, right, (((1,), (1,)), ((), ())), preferred_element_type=F32)
    modes = forward_y(rows, (e_hi, e_lo, o_hi, o_lo))
    s_ref[0] = modes
    store_send(send_ref, modes, pl.program_id(0), field_count, interleave)


def advance_kernel(
    interleave,
    field_count,
    dt_ref,
    s_ref,
    force_ref,
    isq_ref,
    damp_ref,
    fx_hi,
    fx_lo,
    e_hi,
    e_lo,
    o_hi,
    o_lo,
    bx_hi,
    bx_lo,
    bk_hi,
    bk_lo,
    ye_hi,
    ye_lo,
    yo_hi,
    yo_lo,
    send_ref,
):
    spectrum = s_ref[0]
    count = spectrum.shape[0]
    width = spectrum.shape[1] // 2
    half = width // 2

    def tendency(modes):
        both = jnp.concatenate([modes * isq_ref[...], modes], axis=0)
        even = right_mul(both[:, :width], ye_hi, ye_lo)
        odd = right_mul(both[:, width:], yo_hi, yo_lo)
        first, second = even + odd, even - odd

        def columns(row, block):
            rows = slice(row * count, (row + 1) * count)
            real = slice(2 * block * half, (2 * block + 1) * half)
            imag = slice((2 * block + 1) * half, (2 * block + 2) * half)
            return jnp.concatenate(
                [
                    jnp.concatenate([first[rows, real], second[rows, real]], axis=1),
                    jnp.concatenate([first[rows, imag], second[rows, imag]], axis=1),
                ],
                axis=0,
            )

        vel_x = left_mul(bx_hi, bx_lo, columns(0, 1))
        grad_x = left_mul(bk_hi, bk_lo, columns(1, 0))
        total = vel_x * grad_x
        minus_vel_y = left_mul(bk_hi, bk_lo, columns(0, 0))
        grad_y = left_mul(bx_hi, bx_lo, columns(1, 1))
        total = force_ref[...] - (total - minus_vel_y * grad_y)
        rows = left_mul(fx_hi, fx_lo, total)
        return forward_y(rows, (e_hi, e_lo, o_hi, o_lo)) - damp_ref[...] * modes

    step = dt_ref[0]
    middle = spectrum + (0.5 * step) * tendency(spectrum)
    advanced = spectrum + step * tendency(middle)
    store_send(send_ref, advanced, pl.program_id(0), field_count, interleave)


def angle_kernel(field_count, slots, adv_ref, start_ref, mat_hi, mat_lo, turn_ref, out_ref, rows_ref):
    sources = adv_ref.shape[0] // (slots * field_count)
    base = pl.program_id(0) * field_count

    def gather(ref):
        rows = [
            ref[pl.ds(base + f, sources, stride=slots * field_count), :] for f in range(field_count)
        ]
        return jnp.concatenate(rows, axis=0).T

    both = jnp.concatenate([gather(adv_ref), gather(start_ref)], axis=0)
    result = right_mul(both, mat_hi, mat_lo)
    lanes = adv_ref.shape[1]
    quarter = lanes // 4
    merged = result.shape[1] // 2
    turn_cos, turn_sin = turn_ref[0:1], turn_ref[1:2]

    def modes(row):
        real = result[row : row + quarter]
        imag = result[row + quarter : row + 2 * quarter]
        return (
            real[:, :merged] + imag[:, merged:],
            imag[:, :merged] - real[:, merged:],
        )

    blocks = merged // 128
    for parity in range(2):
        adv_real, adv_imag = modes(parity * 2 * quarter)
        real, imag = modes(lanes + parity * 2 * quarter)
        pair = (
            adv_real - (turn_cos * real - turn_sin * imag),
            adv_imag - (turn_sin * real + turn_cos * imag),
        )
        for part in range(2):
            for b in range(blocks):
                rows_ref[part * blocks + b, pl.ds(parity, quarter, stride=2), :] = pair[part][
                    :, 128 * b : 128 * (b + 1)
                ]
    for part in range(2):
        out_ref[part, 0] = jnp.concatenate(
            [rows_ref[part * blocks + b] for b in range(blocks)], axis=1
        )


def whole_spec(shape):
    zeros = (0,) * len(shape)
    return pl.BlockSpec(tuple(shape), lambda *_: zeros)


def local(tables, vorticity, forcing_mode, time_step, rotation):
    angle_local, samples, row_count, width = vorticity.shape
    phys = lax.axis_size("phys")
    ang = lax.axis_size("ang")
    angle_total = angle_local * ang
    group_fields = angle_local * samples
    field_count = -(-group_fields // phys)
    slots, plus = tables["slots"], tables["plus"]
    count = slots * phys
    block = width // ang
    interleave = block == 64

    forcing = forcing_mode[0].astype(F32)
    rows_global = jnp.arange(width, dtype=jnp.int32).astype(F32)
    force = (-forcing * jnp.cos(forcing * (2 * jnp.pi * rows_global / width)))[None, :]

    fields = vorticity.reshape(group_fields, row_count, width)
    if field_count * phys != group_fields:
        fields = jnp.pad(fields, ((0, field_count * phys - group_fields), (0, 0), (0, 0)))
    fields = fields.reshape(phys, field_count, row_count, width)
    fields = lax.all_to_all(fields, "phys", split_axis=0, concat_axis=0, tiled=True)

    fwd = list(tables["fwd_x"]) + list(tables["fwd_y"][0]) + list(tables["fwd_y"][1])
    fwd = [jnp.asarray(t) for t in fwd]
    inv = list(tables["inv_x"]) + list(tables["inv_kx"]) + list(tables["inv_y"][0]) + list(tables["inv_y"][1])
    inv = [jnp.asarray(t) for t in inv]
    params = pltpu.CompilerParams(
        dimension_semantics=("arbitrary",), vmem_limit_bytes=56 * 1024 * 1024
    )
    send_shape = (4, count * field_count, 128)
    start_modes, start_send = pl.pallas_call(
        functools.partial(spectrum_kernel, interleave, field_count),
        grid=(field_count,),
        in_specs=[pl.BlockSpec((phys, 1, row_count, width), lambda f: (0, f, 0, 0))]
        + [whole_spec(t.shape) for t in fwd],
        out_specs=[
            pl.BlockSpec((1, count, 2 * width), lambda f: (f, 0, 0)),
            whole_spec(send_shape),
        ],
        out_shape=[
            jax.ShapeDtypeStruct((field_count, count, 2 * width), F32),
            jax.ShapeDtypeStruct(send_shape, F32),
        ],
        compiler_params=params,
        name="spectrum",
    )(fields, *fwd)

    def exchange(send):
        rows = slots * field_count
        if interleave:
            send = send.reshape(ang * phys, rows, 128)
        else:
            send = send.reshape(2, 2, phys, rows, 128 // block, block)
            send = send.transpose(1, 4, 2, 3, 0, 5).reshape(ang * phys, rows, 2 * block)
        got = lax.all_to_all(send, ("ang", "phys"), split_axis=0, concat_axis=0, tiled=True)
        return got.reshape(ang * phys * rows, 2 * block)

    start = exchange(start_send)

    extra = [force, jnp.asarray(tables["inverse_sq"]), jnp.asarray(tables["damping"])]
    adv_send = pl.pallas_call(
        functools.partial(advance_kernel, interleave, field_count),
        grid=(field_count,),
        in_specs=[
            pl.BlockSpec(memory_space=pltpu.SMEM),
            pl.BlockSpec((1, count, 2 * width), lambda f: (f, 0, 0)),
        ]
        + [whole_spec(t.shape) for t in extra + fwd + inv],
        out_specs=whole_spec(send_shape),
        out_shape=jax.ShapeDtypeStruct(send_shape, F32),
        compiler_params=params,
        name="advance",
    )(time_step, start_modes, *extra, *fwd, *inv)
    advanced = exchange(adv_send)

    index = np.arange(field_count)[:, None] + field_count * np.arange(phys)[None, :]
    index = np.broadcast_to(index[:, None, :], (field_count, ang, phys))
    first = np.arange(ang)[None, :, None] * angle_local + index // samples
    valid = index < group_fields
    turn = 2.0 * math.pi / angle_total * np.mod(
        first[..., None] * np.arange(angle_total), angle_total
    )
    scale = 1.0 / math.sqrt(angle_total)
    pair = scale * np.stack([np.cos(turn), np.sin(turn)], axis=-2)
    pick = ((index % samples)[..., None] == np.arange(samples)) & valid[..., None]
    pick = jnp.asarray(pick.reshape(-1, 1, samples, 1).astype(ml_dtypes.bfloat16))
    mat_hi, mat_lo = [
        (jnp.asarray(part.reshape(-1, 2, 1, angle_total)) * pick).reshape(
            -1, 2 * samples * angle_total
        )
        for part in split_table(pair)
    ]
    signed_angle = jnp.asarray(signed(np.arange(angle_total), angle_total).astype(np.float32))
    turns = jnp.stack(
        [
            jnp.tile(jnp.cos(signed_angle * rotation[0]), samples),
            jnp.tile(jnp.sin(signed_angle * rotation[0]), samples),
        ]
    )
    merged = samples * angle_total
    return pl.pallas_call(
        functools.partial(angle_kernel, field_count, slots),
        grid=(plus,),
        in_specs=[
            whole_spec(t.shape) for t in (advanced, start, mat_hi, mat_lo, turns)
        ],
        out_specs=pl.BlockSpec((2, 1, block, merged), lambda k: (0, k, 0, 0)),
        out_shape=jax.ShapeDtypeStruct((2, plus, block, merged), F32),
        scratch_shapes=[pltpu.VMEM((2 * merged // 128, block, 128), F32)],
        compiler_params=params,
        name="angle",
    )(advanced, start, mat_hi, mat_lo, turns)


def solution(mesh):
    in_specs = (P("ang", None, "phys", None), P(), P(), P())
    out_specs = P(None, "phys", "ang", None)

    def program(vorticity, forcing_mode, time_step, rotation):
        tables = make_tables(vorticity.shape[3], mesh.shape["phys"], mesh.shape["ang"])
        return jax.shard_map(
            functools.partial(local, tables),
            mesh=mesh,
            in_specs=in_specs,
            out_specs=out_specs,
            check_vma=False,
        )(vorticity, forcing_mode, time_step, rotation)

    return program
```

time: 1920 us -> 230 us (0.12)
  blocking collectives: 556 us -> 59.8 us
  local copies, waits for them, and re-layouts: 461 us -> 5.44 us
  matrix products: 412 us -> 0 us
  waiting for transfers between devices: 295 us -> 85.7 us
  other arithmetic: 150 us -> 2.36 us
  Pallas kernels: 0 us -> 66 us
    all_to_all x2 -> x1, blocking collectives: 556 us -> 59.8 us  [exchange(): lax.all_to_all(send, ('ang', 'phys'), split_axis=0, concat_axis=0, tiled=...]
    dot_general x30 -> x0, matrix products: 392 us -> none  [the longest x2 65.4 us: along_x(): jnp.einsum('gky,xk->gyx', pieces[0], back_x_cos, precision=HIGHEST)]
    all_to_all x5 -> x2, waiting for transfers between devices: 295 us -> 85.7 us  [the longest x1 49.8 us: exchange(): lax.all_to_all(send, ('ang', 'phys'), split_axis=0, concat_axis=0, tiled=...]
    slice x24 -> x0, local copies, waits for them, and re-layouts: 126 us -> none  [the longest x4 61.6 us: along_x(): pieces[0]]
    another operation x9 -> x4, local copies, waits for them, and re-layouts: 89.2 us -> 0.18 us  [the longest x2 0.17 us: local(): jnp.stack([jnp.tile(jnp.cos(signed_angle * rotation[0]), samples), jnp.ti...]
    unnamed x84 -> x8, local copies, waits for them, and re-layouts: 77 us -> 3.06 us
    all_to_all x8 -> x0, local copies, waits for them, and re-layouts: 69.6 us -> none  [the longest x2 33.4 us: to_grid(): lax.all_to_all(stacked, 'phys', split_axis=3, concat_axis=2, tiled=True)]
    pallas_call x0 -> x3, Pallas kernels: none -> 66 us  [the longest x1 41.1 us: local(): pl.pallas_call(functools.partial(advance_kernel, interleave, field_count)...]
  transfers between devices with their start and end apart: 5 -> 2, of which waited for: 4 -> 2; matrix products, arithmetic and copies ran while one was open for 5% -> 2% of each run, Pallas kernels for 0% -> 0%
where the time goes in v1:
time: 230 us; the launch traced here: 229 us
  waiting for transfers between devices  85.7 us (37%)
  Pallas kernels  66 us (29%)
  blocking collectives  59.8 us (26%)
  starting transfers between devices  8.07 us (4%)
  local copies, waits for them, and re-layouts  5.44 us (2%)
  other arithmetic  2.36 us (1%)
    all_to_all x1, blocking collectives, exchange(): lax.all_to_all(send, ('ang', 'phys'), split_axis=0, concat_axis=0, tiled=...  59.8 us
    all_to_all x1, waiting for transfers between devices, exchange(): lax.all_to_all(send, ('ang', 'phys'), split_axis=0, concat_axis=0, tiled=...  49.8 us
    pallas_call x1, Pallas kernels, local(): pl.pallas_call(functools.partial(advance_kernel, interleave, field_count)...  41.1 us
    all_to_all x1, waiting for transfers between devices, local(): lax.all_to_all(fields, 'phys', split_axis=0, concat_axis=0, tiled=True)  36 us
    pallas_call x1, Pallas kernels, local(): pl.pallas_call(functools.partial(spectrum_kernel, interleave, field_count...  12.8 us
    pallas_call x1, Pallas kernels, local(): pl.pallas_call(functools.partial(angle_kernel, field_count, slots), grid=...  12.1 us
    all_to_all x1, starting transfers between devices, local(): lax.all_to_all(fields, 'phys', split_axis=0, concat_axis=0, tiled=True)  5.17 us
  transfers between devices with their start and end apart: 2, of which 2 were waited for; matrix products, arithmetic and copies ran while one was open for 2% of the time, Pallas kernels for 0%

profile of v1, /device:TPU:0, one launch (start us, length us, event | category | flops | bytes accessed | tf_op | source)
XLA Modules:
  0.0 229.5 jit_solution(7089758236045041022)
XLA Ops:
  0.0 5.2 %all-to-all-start = ((f32[8,12,32,256]{3,2,1,0:T(8,128)}), f32[8,12,32,256]{3,2,1,0:T(8,128)S(1)}, u32[]{:S(2)}, u32[]{:S(2)}) async-start(f32[8,12,32,256]{3,2,1,0:T(8,128)} %bitcast.14), calls=%async_computation | async-start | bytes 6291456 | tf_op jit(solution)/shard_map/all_to_all | solution.py:287
  6.5 0.6 cosine_multiply_fusion.force_ref
  7.1 36.0 %all-to-all-done.x_ref = f32[8,12,32,256]{3,2,1,0:T(8,128)S(1)} async-done(((f32[8,12,32,256]{3,2,1,0:T(8,128)}), f32[8,12,32,256]{3,2,1,0:T(8,128)S(1)}, u32[]{:S(2)}, u32[]{:S(2)}) %all-to-all-start) | async-done | bytes 3145760 | tf_op jit(solution)/shard_map/all_to_all | solution.py:287
  43.1 0.0 copy-start
  43.1 1.6 copy-done
  44.7 12.8 %spectrum.1 = (f32[12,96,512]{2,1,0:T(8,128)}, f32[4,1152,128]{2,1,0:T(8,128)}) custom-call(f32[8,12,32,256]{3,2,1,0:T(8,128)} %copy-done, bf16[192,256]{1,0:T(8,128)(2,1)} %constant.46.clone.fx_hi, bf16[192,256]{1,0:T(8,128)(2,1)} %constant.47.clone.fx_lo, bf16[256,256]{1,0:T(8,128)(2,1)} %constant.48.clone.e_hi, bf16[256,256]{1,0:T(8,128)(2,1)} %constant.49.clone.e_lo, ...), custom_call_target="tpu_custom_call" | custom-call | tf_op jit(solution)/shard_map/spectrum/pallas_call | solution.py:297
  57.5 41.1 %advance.1 = f32[4,1152,128]{2,1,0:T(8,128)} custom-call(f32[1]{0:T(128)S(6)} %copy.28.dt_ref, f32[12,96,512]{2,1,0:T(8,128)} %get-tuple-element.7.s_ref, f32[1,256]{1,0:T(1,128)} %cosine_multiply_fusion.force_ref, f32[96,512]{1,0:T(8,128)} %constant.60.clone.isq_ref, f32[96,512]{1,0:T(8,128)} %constant.61.clone.damp_ref, ...), custom_call_target="tpu_custom_call" | custom-call | tf_op jit(solution)/shard_map/advance/pallas_call | solution.py:327
  98.6 59.8 %all_to_all.15 = f32[32,144,128]{2,1,0:T(8,128)} all-to-all(f32[32,144,128]{2,1,0:T(8,128)} %bitcast.13), channel_id=1, replica_groups=mesh['phys'=8,'ang'=4] {'ang','phys'}, dimensions={0} | all-to-all | bytes 4718592 | tf_op jit(solution)/shard_map/all_to_all | solution.py:321
  158.5 0.0 copy-start.3
  158.5 0.0 copy-start.2
  158.5 2.9 %all-to-all-start.2 = ((f32[32,144,128]{2,1,0:T(8,128)}), f32[32,144,128]{2,1,0:T(8,128)S(1)}, u32[]{:S(2)}, u32[]{:S(2)}) async-start(f32[32,144,128]{2,1,0:T(8,128)} %bitcast.17), calls=%async_computation.2 | async-start | bytes 4718592 | tf_op jit(solution)/shard_map/all_to_all | solution.py:321
  162.0 0.0 copy-done.3
  162.1 0.1 stack_tile.6
  162.2 0.1 stack_tile.7
  162.3 0.0 copy-done.2
  162.3 1.1 broadcast_multiply_fusion
  163.4 1.1 copy.25.mat_hi
  164.5 1.1 copy.26.mat_lo
  165.6 0.6 pad_maximum_fusion.turn_ref
  166.2 49.8 %all-to-all-done.2 = f32[32,144,128]{2,1,0:T(8,128)S(1)} async-done(((f32[32,144,128]{2,1,0:T(8,128)}), f32[32,144,128]{2,1,0:T(8,128)S(1)}, u32[]{:S(2)}, u32[]{:S(2)}) %all-to-all-start.2) | async-done | bytes 2359328 | tf_op jit(solution)/shard_map/all_to_all | solution.py:321
  215.9 0.0 copy-start.1
  215.9 1.4 copy-done.1
  217.4 12.1 %angle.1 = f32[2,11,64,384]{3,2,1,0:T(8,128)} custom-call(f32[4608,128]{1,0:T(8,128)} %bitcast.11, f32[4608,128]{1,0:T(8,128)} %bitcast.12, bf16[384,768]{1,0:T(8,128)(2,1)} %copy.25.mat_hi, bf16[384,768]{1,0:T(8,128)(2,1)} %copy.26.mat_lo, f32[2,384]{1,0:T(2,128)} %pad_maximum_fusion.turn_ref), custom_call_target="tpu_custom_call" | custom-call | tf_op jit(solution)/shard_map/angle/pallas_call | solution.py:367
  (3 shorter events, 0.0 us)
Async XLA Ops:
  0.0 43.1 %all-to-all-start = ((f32[8,12,32,256]{3,2,1,0:T(8,128)}), f32[8,12,32,256]{3,2,1,0:T(8,128)S(1)}, u32[]{:S(2)}, u32[]{:S(2)}) async-start(f32[8,12,32,256]{3,2,1,0:T(8,128)} %bitcast.14), calls=%async_computation | async-start | bytes 6291456 | tf_op jit(solution)/shard_map/all_to_all | solution.py:287
  43.1 1.7 copy-start
  158.5 3.6 %copy-start.3 = (f32[96]{0:T(128)S(1)}, f32[96]{0:T(128)}, u32[]{:S(2)}) copy-start(f32[96]{0:T(128)} %constant.65.clone) | copy-start | bytes 1156
  158.5 3.8 %copy-start.2 = (bf16[384,4]{0,1:T(4,128)(2,1)S(1)}, bf16[384,4]{0,1:T(4,128)(2,1)}, u32[]{:S(2)}) copy-start(bf16[384,4]{0,1:T(4,128)(2,1)} %constant.67) | copy-start | bytes 9220
  158.5 57.5 %all-to-all-start.2 = ((f32[32,144,128]{2,1,0:T(8,128)}), f32[32,144,128]{2,1,0:T(8,128)S(1)}, u32[]{:S(2)}, u32[]{:S(2)}) async-start(f32[32,144,128]{2,1,0:T(8,128)} %bitcast.17), calls=%async_computation.2 | async-start | bytes 4718592 | tf_op jit(solution)/shard_map/all_to_all | solution.py:321
  215.9 1.4 copy-start.1

commit v2 on v1

--- a/solution.py
+++ b/solution.py
@@ -259,6 +259,10 @@
         )
 
 
+def cost(flops):
+    return pl.CostEstimate(flops=int(flops), bytes_accessed=8 * 1024 * 1024, transcendentals=0)
+
+
 def whole_spec(shape):
     zeros = (0,) * len(shape)
     return pl.BlockSpec(tuple(shape), lambda *_: zeros)
@@ -307,6 +311,7 @@
             jax.ShapeDtypeStruct((field_count, count, 2 * width), F32),
             jax.ShapeDtypeStruct(send_shape, F32),
         ],
+        cost_estimate=cost(field_count * 4 * count * 6 * width * width),
         compiler_params=params,
         name="spectrum",
     )(fields, *fwd)
@@ -334,9 +339,11 @@
         + [whole_spec(t.shape) for t in extra + fwd + inv],
         out_specs=whole_spec(send_shape),
         out_shape=jax.ShapeDtypeStruct(send_shape, F32),
+        cost_estimate=cost(field_count * 24 * count * 6 * width * width),
         compiler_params=params,
         name="advance",
     )(time_step, start_modes, *extra, *fwd, *inv)
+    adv_send, start = lax.optimization_barrier((adv_send, start))
     advanced = exchange(adv_send)
 
     index = np.arange(field_count)[:, None] + field_count * np.arange(phys)[None, :]
@@ -373,6 +380,7 @@
         out_specs=pl.BlockSpec((2, 1, block, merged), lambda k: (0, k, 0, 0)),
         out_shape=jax.ShapeDtypeStruct((2, plus, block, merged), F32),
         scratch_shapes=[pltpu.VMEM((2 * merged // 128, block, 128), F32)],
+        cost_estimate=cost(plus * 4 * block * 6 * advanced.shape[0] // (slots) * merged // 100),
         compiler_params=params,
         name="angle",
     )(advanced, start, mat_hi, mat_lo, turns)

time: 230 us -> 188 us (0.82)
  waiting for transfers between devices: 85.7 us -> 62.3 us
  blocking collectives: 59.8 us -> 43.1 us
    all_to_all x1 -> x0, waiting for transfers between devices: 36 us -> none  [local(): lax.all_to_all(fields, 'phys', split_axis=0, concat_axis=0, tiled=True)]
    all_to_all x1, blocking collectives: 59.8 us -> 43.1 us  [local(): lax.all_to_all(fields, 'phys', split_axis=0, concat_axis=0, tiled=True)]
    all_to_all x1 -> x2, waiting for transfers between devices: 49.8 us -> 62.3 us  [exchange(): lax.all_to_all(send, ('ang', 'phys'), split_axis=0, concat_axis=0, tiled=...]
    all_to_all x1 -> x2, starting transfers between devices: 2.9 us -> 8.69 us  [exchange(): lax.all_to_all(send, ('ang', 'phys'), split_axis=0, concat_axis=0, tiled=...]
    all_to_all x1 -> x0, starting transfers between devices: 5.17 us -> none  [local(): lax.all_to_all(fields, 'phys', split_axis=0, concat_axis=0, tiled=True)]
  transfers between devices with their start and end apart: 2 -> 2, of which waited for: 2 -> 2; matrix products, arithmetic and copies ran while one was open for 2% -> 2% of each run, Pallas kernels for 0% -> 22%
where the time goes in v2:
time: 188 us; the launch traced here: 187 us
  Pallas kernels  66 us (35%)
  waiting for transfers between devices  62.3 us (33%)
  blocking collectives  43.1 us (23%)
  starting transfers between devices  8.69 us (5%)
  local copies, waits for them, and re-layouts  3.79 us (2%)
  between operations  2.01 us (1%)
    all_to_all x2, waiting for transfers between devices, exchange(): lax.all_to_all(send, ('ang', 'phys'), split_axis=0, concat_axis=0, tiled=...  62.3 us
    all_to_all x1, blocking collectives, local(): lax.all_to_all(fields, 'phys', split_axis=0, concat_axis=0, tiled=True)  43.1 us
    pallas_call x1, Pallas kernels, local(): pl.pallas_call(functools.partial(advance_kernel, interleave, field_count)...  41 us
    pallas_call x1, Pallas kernels, local(): pl.pallas_call(functools.partial(spectrum_kernel, interleave, field_count...  12.8 us
    pallas_call x1, Pallas kernels, local(): pl.pallas_call(functools.partial(angle_kernel, field_count, slots), grid=...  12.1 us
    all_to_all x2, starting transfers between devices, exchange(): lax.all_to_all(send, ('ang', 'phys'), split_axis=0, concat_axis=0, tiled=...  8.69 us
  transfers between devices with their start and end apart: 2, of which 2 were waited for; matrix products, arithmetic and copies ran while one was open for 2% of the time, Pallas kernels for 22%

profile of v2, /device:TPU:0, one launch (start us, length us, event | category | flops | bytes accessed | tf_op | source)
XLA Modules:
  0.0 187.2 jit_solution(7344101655949518898)
XLA Ops:
  0.0 43.1 %all_to_all.15.x_ref = f32[8,12,32,256]{3,2,1,0:T(8,128)} all-to-all(f32[8,12,32,256]{3,2,1,0:T(8,128)} %bitcast.12), channel_id=1, replica_groups=mesh['phys'=8,'ang'=4] {'phys'}, dimensions={0} | all-to-all | bytes 6291456 | tf_op jit(solution)/shard_map/all_to_all | solution.py:291
  43.1 12.8 %spectrum.1 = (f32[12,96,512]{2,1,0:T(8,128)}, f32[4,1152,128]{2,1,0:T(8,128)}) custom-call(f32[8,12,32,256]{3,2,1,0:T(8,128)} %all_to_all.15.x_ref, bf16[192,256]{1,0:T(8,128)(2,1)} %constant.46.clone.fx_hi, bf16[192,256]{1,0:T(8,128)(2,1)} %constant.47.clone.fx_lo, bf16[256,256]{1,0:T(8,128)(2,1)} %constant.48.clone.e_hi, ...), custom_call_target="tpu_custom_call" | custom-call | flops 1811939328 | bytes 8388608 | tf_op jit(solution)/shard_map/spectrum/pallas_call | solution.py:301
  55.9 4.6 %all-to-all-start.1 = ((f32[32,144,128]{2,1,0:T(8,128)}), f32[32,144,128]{2,1,0:T(8,128)S(1)}, u32[]{:S(2)}, u32[]{:S(2)}) async-start(f32[32,144,128]{2,1,0:T(8,128)} %bitcast.16), calls=%async_computation.1 | async-start | bytes 4718592 | tf_op jit(solution)/shard_map/all_to_all | solution.py:326
  61.8 0.6 cosine_multiply_fusion.force_ref
  62.4 41.0 %advance.1 = f32[4,1152,128]{2,1,0:T(8,128)} custom-call(f32[1]{0:T(128)S(6)} %copy.28.dt_ref, f32[12,96,512]{2,1,0:T(8,128)} %get-tuple-element.9.s_ref, f32[1,256]{1,0:T(1,128)} %cosine_multiply_fusion.force_ref, f32[96,512]{1,0:T(8,128)} %constant.60.clone.isq_ref, f32[96,512]{1,0:T(8,128)} %constant.61.clone.damp_ref, ...), custom_call_target="tpu_custom_call" | custom-call | flops 10871635968 | bytes 8388608 | tf_op jit(solution)/shard_map/advance/pallas_call | solution.py:332
  103.5 11.6 %all-to-all-done.1 = f32[32,144,128]{2,1,0:T(8,128)S(1)} async-done(((f32[32,144,128]{2,1,0:T(8,128)}), f32[32,144,128]{2,1,0:T(8,128)S(1)}, u32[]{:S(2)}, u32[]{:S(2)}) %all-to-all-start.1) | async-done | bytes 2359328 | tf_op jit(solution)/shard_map/all_to_all | solution.py:326
  115.0 0.0 copy-start
  115.0 0.0 copy-start.4
  115.0 0.0 copy-start.1
  115.0 0.0 copy-start.2
  115.0 0.0 copy-start.3
  115.0 1.4 copy-done
  116.4 4.1 %all-to-all-start.2 = ((f32[32,144,128]{2,1,0:T(8,128)}), f32[32,144,128]{2,1,0:T(8,128)}, u32[]{:S(2)}, u32[]{:S(2)}) async-start(f32[32,144,128]{2,1,0:T(8,128)} %bitcast.15), calls=%async_computation.2 | async-start | bytes 4718592 | tf_op jit(solution)/shard_map/all_to_all | solution.py:326
  121.2 0.0 copy-done.4
  121.3 0.1 stack_tile.6
  121.4 0.1 stack_tile.7
  121.5 0.0 copy-done.1
  121.5 0.0 copy-done.2
  121.5 0.0 copy-done.3
  121.5 0.1 broadcast_multiply_fusion
  121.6 1.1 copy.25.mat_hi
  122.7 1.1 copy.26.mat_lo
  123.8 0.6 pad_maximum_fusion.turn_ref
  124.4 50.7 %all-to-all-done.2 = f32[32,144,128]{2,1,0:T(8,128)} async-done(((f32[32,144,128]{2,1,0:T(8,128)}), f32[32,144,128]{2,1,0:T(8,128)}, u32[]{:S(2)}, u32[]{:S(2)}) %all-to-all-start.2) | async-done | bytes 2359328 | tf_op jit(solution)/shard_map/all_to_all | solution.py:326
  175.1 12.1 %angle.1 = f32[2,11,64,384]{3,2,1,0:T(8,128)} custom-call(f32[4608,128]{1,0:T(8,128)} %bitcast.6.adv_ref, f32[4608,128]{1,0:T(8,128)} %bitcast.11, bf16[384,768]{1,0:T(8,128)(2,1)} %copy.25.mat_hi, bf16[384,768]{1,0:T(8,128)(2,1)} %copy.26.mat_lo, f32[2,384]{1,0:T(2,128)} %pad_maximum_fusion.turn_ref), custom_call_target="tpu_custom_call" | custom-call | flops 24914164 | bytes 8388608 | tf_op jit(solution)/shard_map/angle/pallas_call | solution.py:374
  (3 shorter events, 0.0 us)
Async XLA Ops:
  55.9 59.1 %all-to-all-start.1 = ((f32[32,144,128]{2,1,0:T(8,128)}), f32[32,144,128]{2,1,0:T(8,128)S(1)}, u32[]{:S(2)}, u32[]{:S(2)}) async-start(f32[32,144,128]{2,1,0:T(8,128)} %bitcast.16), calls=%async_computation.1 | async-start | bytes 4718592 | tf_op jit(solution)/shard_map/all_to_all | solution.py:326
  115.0 1.4 copy-start
  115.0 6.2 %copy-start.4 = (f32[96]{0:T(128)S(1)}, f32[96]{0:T(128)}, u32[]{:S(2)}) copy-start(f32[96]{0:T(128)} %constant.65.clone) | copy-start | bytes 1156
  115.0 6.4 %copy-start.1 = (bf16[384,2,96]{0,2,1:T(8,128)(2,1)S(1)}, bf16[384,2,96]{0,2,1:T(8,128)(2,1)}, u32[]{:S(2)}) copy-start(bf16[384,2,96]{0,2,1:T(8,128)(2,1)} %constant.66) | copy-start | bytes 442372
  115.0 6.4 %copy-start.2 = (bf16[384,2,96]{0,2,1:T(8,128)(2,1)S(1)}, bf16[384,2,96]{0,2,1:T(8,128)(2,1)}, u32[]{:S(2)}) copy-start(bf16[384,2,96]{0,2,1:T(8,128)(2,1)} %constant.68) | copy-start | bytes 442372
  115.0 6.4 %copy-start.3 = (bf16[384,4]{0,1:T(4,128)(2,1)S(1)}, bf16[384,4]{0,1:T(4,128)(2,1)}, u32[]{:S(2)}) copy-start(bf16[384,4]{0,1:T(4,128)(2,1)} %constant.67) | copy-start | bytes 9220
  116.4 58.7 %all-to-all-start.2 = ((f32[32,144,128]{2,1,0:T(8,128)}), f32[32,144,128]{2,1,0:T(8,128)}, u32[]{:S(2)}, u32[]{:S(2)}) async-start(f32[32,144,128]{2,1,0:T(8,128)} %bitcast.15), calls=%async_computation.2 | async-start | bytes 4718592 | tf_op jit(solution)/shard_map/all_to_all | solution.py:326

commit v3 on v2

v3 whole, which is shorter than its diff:
```python
import functools
import math

import jax
import jax.numpy as jnp
import ml_dtypes
import numpy as np
from jax import lax
from jax.experimental import pallas as pl
from jax.experimental.pallas import tpu as pltpu
from jax.sharding import PartitionSpec as P

VISCOSITY = 1.0 / 40.0
F32 = jnp.float32
BF16 = jnp.bfloat16


def split_table(table):
    table = np.asarray(table, np.float32)
    high = table.astype(ml_dtypes.bfloat16)
    low = (table - high.astype(np.float32)).astype(ml_dtypes.bfloat16)
    return high, low


def signed(values, length):
    return np.where(values < length // 2, values, values - length)


def make_tables(width, phys, ang):
    limit = width // 3
    half = width // 2
    plus = (limit + phys) // phys
    count = plus * phys
    full = 8 * phys * (plus // 8)
    row = np.arange(count)
    rest = plus % 8
    kx = np.where(
        row < full,
        (row % max(full, 1)) // 8 // max(plus // 8, 1) * plus + row % (8 * max(plus // 8, 1)),
        (row - full) // max(rest, 1) * plus + plus - rest + (row - full) % max(rest, 1),
    )
    kx_keep = (kx <= limit).astype(np.float64)
    block = width // ang
    lane = np.arange(width)
    owner = lane // block
    part = (lane % block) // (block // 2)
    even_index = owner * block + 2 * (lane % (block // 2))
    turn = 2.0 * math.pi / width
    grid = np.arange(width)

    def angle(left, right):
        return turn * np.mod(left[:, None] * right[None, :], width)

    x_turn = angle(kx, grid)
    fwd_x = np.concatenate([np.cos(x_turn), -np.sin(x_turn)]) / width
    fwd_x = fwd_x * np.concatenate([kx_keep, kx_keep])[:, None]
    weight = (np.where(kx == 0, 1.0, 2.0) * kx_keep)[:, None]
    inv_x = np.concatenate([weight * np.cos(x_turn), -weight * np.sin(x_turn)]).T
    inv_kx = np.concatenate(
        [-weight * kx[:, None] * np.sin(x_turn), -weight * kx[:, None] * np.cos(x_turn)]
    ).T
    fwd_y, inv_y, lane_ky = [], [], []
    for parity in (0, 1):
        ky = signed(even_index + parity, width)
        keep = (np.abs(ky) <= limit).astype(np.float64)
        lane_ky.append(ky)
        y_turn = angle(np.arange(half), ky)
        cos_y, sin_y = np.cos(y_turn) * keep, np.sin(y_turn) * keep
        real_out = part == 0
        from_real = np.where(real_out, cos_y, -sin_y)
        from_imag = np.where(real_out, sin_y, cos_y)
        fwd_y.append(np.concatenate([from_real, from_imag]) / width)
        real_back = np.where(real_out, cos_y, -sin_y).T
        imag_back = np.where(real_out, sin_y, cos_y).T
        scale = ky[:, None]
        inv_y.append(
            np.concatenate(
                [real_back, imag_back, -scale * imag_back, scale * real_back], axis=1
            )
        )
    return dict(
        plus=plus,
        fwd_x=split_table(fwd_x),
        inv_x=split_table(inv_x),
        inv_kx=split_table(inv_kx),
        fwd_y=[split_table(t) for t in fwd_y],
        inv_y=[split_table(t) for t in inv_y],
        wave_x=kx.astype(np.float32)[:, None],
        wave_y=np.concatenate(lane_ky).astype(np.float32)[None, :],
    )


def split(values):
    high = values.astype(BF16)
    low = (values - high.astype(F32)).astype(BF16)
    return high, low


def right_mul(values, high_ref, low_ref):
    high, low = split(values)
    left = jnp.concatenate([high, low, high], axis=1)
    right = jnp.concatenate([high_ref[...], high_ref[...], low_ref[...]], axis=0)
    return jnp.dot(left, right, preferred_element_type=F32)


def left_mul(high_ref, low_ref, values):
    high, low = split(values)
    left = jnp.concatenate([high_ref[...], low_ref[...], high_ref[...]], axis=1)
    right = jnp.concatenate([high, high, low], axis=0)
    return jnp.dot(left, right, preferred_element_type=F32)


def forward_y(rows, tables):
    count = rows.shape[0] // 2
    half = rows.shape[1] // 2
    real, imag = rows[:count], rows[count:]
    even = jnp.concatenate(
        [real[:, :half] + real[:, half:], imag[:, :half] + imag[:, half:]], axis=1
    )
    odd = jnp.concatenate(
        [real[:, :half] - real[:, half:], imag[:, :half] - imag[:, half:]], axis=1
    )
    return jnp.concatenate(
        [right_mul(even, tables[0], tables[1]), right_mul(odd, tables[2], tables[3])], axis=1
    )


def store_send(send_ref, modes, field, field_count, plus, interleave):
    pieces = [modes[:, 128 * b : 128 * (b + 1)] for b in range(4)]
    if interleave:
        low_lane = lax.broadcasted_iota(jnp.int32, pieces[0].shape, 1) < 64
        out = []
        for b in range(2):
            even, odd = pieces[b], pieces[b + 2]
            out.append(jnp.where(low_lane, even, pltpu.roll(odd, 64, 1)))
            out.append(jnp.where(low_lane, pltpu.roll(even, 64, 1), odd))
        pieces = out
    phys = modes.shape[0] // plus
    chunk = send_ref.shape[1] // phys
    whole, rest = 8 * (plus // 8), plus % 8
    for owner in range(phys):
        parts = [(owner * whole, whole, 0), (phys * whole + owner * rest, rest, whole)]
        for start, size, first in parts:
            if not size:
                continue
            place = pl.ds(owner * chunk + first * field_count + field, size, stride=field_count)
            for b in range(4):
                send_ref[b, place, :] = pieces[b][start : start + size]


def rows_kernel(x_ref, fx_hi, fx_lo, out_ref):
    width = x_ref.shape[2]
    high, low = split(x_ref[...].reshape(-1, width))
    left = jnp.concatenate([fx_hi[...], fx_lo[...], fx_hi[...]], axis=1)
    right = jnp.concatenate([high, high, low], axis=1)
    rows = lax.dot_general(left, right, (((1,), (1,)), ((), ())), preferred_element_type=F32)
    for group in range(out_ref.shape[0]):
        out_ref[group] = rows[:, 128 * group : 128 * (group + 1)]


def swap_lanes(first, second, width):
    lane = lax.broadcasted_iota(jnp.int32, first.shape, 1)
    keep = (lane // width) % 2 == 0
    return (
        jnp.where(keep, first, pltpu.roll(second, width, 1)),
        jnp.where(keep, pltpu.roll(first, 128 - width, 1), second),
    )


def gather_rows(pieces):
    left = swap_lanes(pieces[0], pieces[2], 64)
    right = swap_lanes(pieces[1], pieces[3], 64)
    return swap_lanes(left[0], right[0], 32) + swap_lanes(left[1], right[1], 32)


def columns_kernel(
    interleave, field_count, plus, x_ref, e_hi, e_lo, o_hi, o_lo, s_ref, send_ref
):
    halves = [gather_rows([x_ref[4 * h + q, 0] for q in range(4)]) for h in range(2)]
    fields = [jnp.concatenate([halves[0][i], halves[1][i]], axis=1) for i in range(4)]
    count = fields[0].shape[0] // 2
    rows = jnp.concatenate([f[:count] for f in fields] + [f[count:] for f in fields], axis=0)
    modes = forward_y(rows, (e_hi, e_lo, o_hi, o_lo))
    for i in range(4):
        own = modes[i * count : (i + 1) * count]
        s_ref[i] = own
        store_send(send_ref, own, pl.program_id(0) * 4 + i, field_count, plus, interleave)


def spectrum_kernel(interleave, field_count, plus, x_ref, fx_hi, fx_lo, e_hi, e_lo, o_hi, o_lo, s_ref, send_ref):
    width = x_ref.shape[3]
    grid_field = x_ref[:, 0].reshape(width, width)
    high, low = split(grid_field)
    left = jnp.concatenate([fx_hi[...], fx_lo[...], fx_hi[...]], axis=1)
    right = jnp.concatenate([high, high, low], axis=1)
    rows = lax.dot_general(left, right, (((1,), (1,)), ((), ())), preferred_element_type=F32)
    modes = forward_y(rows, (e_hi, e_lo, o_hi, o_lo))
    s_ref[0] = modes
    store_send(send_ref, modes, pl.program_id(0), field_count, plus, interleave)


def advance_kernel(
    interleave,
    field_count,
    plus,
    dt_ref,
    s_ref,
    force_ref,
    wave_x_ref,
    wave_y_ref,
    fx_hi,
    fx_lo,
    e_hi,
    e_lo,
    o_hi,
    o_lo,
    bx_hi,
    bx_lo,
    bk_hi,
    bk_lo,
    ye_hi,
    ye_lo,
    yo_hi,
    yo_lo,
    send_ref,
):
    stack, count = s_ref.shape[:2]
    width = s_ref.shape[2] // 2
    half = width // 2
    wave_x, wave_y = wave_x_ref[...], wave_y_ref[...]
    wave_sq = wave_x * wave_x + wave_y * wave_y
    inverse_sq = jnp.where(wave_sq > 0, 1.0 / jnp.where(wave_sq > 0, wave_sq, 1.0), 0.0)
    damping = VISCOSITY * wave_sq

    def tendency(modes):
        both = jnp.concatenate([m * inverse_sq for m in modes] + modes, axis=0)
        even = right_mul(both[:, :width], ye_hi, ye_lo)
        odd = right_mul(both[:, width:], yo_hi, yo_lo)
        first, second = even + odd, even - odd

        def columns(row, block):
            rows = slice(row * count, (row + 1) * count)
            real = slice(2 * block * half, (2 * block + 1) * half)
            imag = slice((2 * block + 1) * half, (2 * block + 2) * half)
            return jnp.concatenate(
                [
                    jnp.concatenate([first[rows, real], second[rows, real]], axis=1),
                    jnp.concatenate([first[rows, imag], second[rows, imag]], axis=1),
                ],
                axis=0,
            )

        rows = []
        for i in range(stack):
            vel_x = left_mul(bx_hi, bx_lo, columns(i, 1))
            grad_x = left_mul(bk_hi, bk_lo, columns(stack + i, 0))
            total = vel_x * grad_x
            minus_vel_y = left_mul(bk_hi, bk_lo, columns(i, 0))
            grad_y = left_mul(bx_hi, bx_lo, columns(stack + i, 1))
            total = force_ref[...] - (total - minus_vel_y * grad_y)
            rows.append(left_mul(fx_hi, fx_lo, total))
        rows = jnp.concatenate([r[:count] for r in rows] + [r[count:] for r in rows], axis=0)
        out = forward_y(rows, (e_hi, e_lo, o_hi, o_lo))
        return [out[i * count : (i + 1) * count] - damping * modes[i] for i in range(stack)]

    step = dt_ref[0]
    spectra = [s_ref[i] for i in range(stack)]
    middle = [s + (0.5 * step) * t for s, t in zip(spectra, tendency(spectra))]
    second = tendency(middle)
    for i in range(stack):
        field = pl.program_id(0) * stack + i
        advanced = spectra[i] + step * second[i]
        store_send(send_ref, advanced, field, field_count, plus, interleave)


def angle_kernel(
    plus, field_count, samples, chunk, got_ref, mat_hi, mat_lo, last_ref, out_ref, rows_ref
):
    sources = got_ref.shape[0] // chunk
    lanes = got_ref.shape[1]
    modes = mat_hi.shape[1] // 2
    quarter = lanes // 4
    merged = samples * modes
    blocks = merged // 128
    turning = len(last_ref.shape) == 2
    for k in range(plus):
        cos_rows, sin_rows = [], []
        for s in range(samples):
            if field_count < samples:
                picks, table = range(field_count), s
            else:
                picks, table = range(s, field_count, samples), 0
            values = jnp.concatenate(
                [got_ref[pl.ds(k * field_count + f, sources, stride=chunk), :] for f in picks],
                axis=0,
            )
            result = left_mul(mat_hi.at[table], mat_lo.at[table], values)
            cos_rows.append(result[:modes])
            sin_rows.append(result[modes:])
        cosine = jnp.concatenate(cos_rows, axis=0).T
        sine = jnp.concatenate(sin_rows, axis=0).T
        for parity in range(2):
            row = parity * 2 * quarter
            near, far = slice(row, row + quarter), slice(row + quarter, row + 2 * quarter)
            real = cosine[near] + sine[far]
            imag = cosine[far] - sine[near]
            if turning:
                turn_cos, turn_sin = last_ref[0:1], last_ref[1:2]
                pair = (turn_sin * imag - turn_cos * real, -(turn_sin * real + turn_cos * imag))
            else:
                pair = (real, imag)
            for part in range(2):
                for b in range(blocks):
                    place = (k * 2 + part) * blocks + b
                    rows_ref[place, pl.ds(parity, quarter, stride=2), :] = pair[part][
                        :, 128 * b : 128 * (b + 1)
                    ]
        for part in range(2):
            place = (k * 2 + part) * blocks
            joined = jnp.concatenate([rows_ref[place + b] for b in range(blocks)], axis=1)
            out_ref[part, k] = joined if turning else joined + last_ref[part, k]


def cost(flops):
    return pl.CostEstimate(flops=int(flops), bytes_accessed=8 * 1024 * 1024, transcendentals=0)


def whole_spec(shape):
    zeros = (0,) * len(shape)
    return pl.BlockSpec(tuple(shape), lambda *_: zeros)


def local(tables, vorticity, forcing_mode, time_step, rotation):
    angle_local, samples, row_count, width = vorticity.shape
    phys = lax.axis_size("phys")
    ang = lax.axis_size("ang")
    angle_total = angle_local * ang
    group_fields = angle_local * samples
    field_count = -(-group_fields // phys)
    plus = tables["plus"]
    count = plus * phys
    chunk = -(-plus * field_count // 8) * 8
    block = width // ang
    interleave = block == 64

    forcing = forcing_mode[0].astype(F32)
    rows_global = jnp.arange(width, dtype=jnp.int32).astype(F32)
    force = (-forcing * jnp.cos(forcing * (2 * jnp.pi * rows_global / width)))[None, :]

    fields = vorticity.reshape(group_fields, row_count, width)
    fwd = list(tables["fwd_x"]) + list(tables["fwd_y"][0]) + list(tables["fwd_y"][1])
    fwd = [jnp.asarray(t) for t in fwd]
    inv = list(tables["inv_x"]) + list(tables["inv_kx"]) + list(tables["inv_y"][0]) + list(tables["inv_y"][1])
    inv = [jnp.asarray(t) for t in inv]
    params = pltpu.CompilerParams(
        dimension_semantics=("arbitrary",), vmem_limit_bytes=56 * 1024 * 1024
    )
    send_shape = (4, phys * chunk, 128)
    fixed = (interleave, field_count, plus)
    modes_shape = [
        jax.ShapeDtypeStruct((field_count, count, 2 * width), F32),
        jax.ShapeDtypeStruct(send_shape, F32),
    ]
    if row_count == 32 and phys == 8 and group_fields % 32 == 0:
        groups = field_count // 4
        fields = pl.pallas_call(
            rows_kernel,
            grid=(group_fields // 32,),
            in_specs=[pl.BlockSpec((32, row_count, width), lambda n: (n, 0, 0))]
            + [whole_spec(t.shape) for t in fwd[:2]],
            out_specs=pl.BlockSpec((8, 2 * count, 128), lambda n: (n, 0, 0)),
            out_shape=jax.ShapeDtypeStruct((group_fields // 4, 2 * count, 128), F32),
            compiler_params=params,
            name="rows",
        )(fields, *fwd[:2])
        fields = fields.reshape(phys, groups * 2 * count, 128)
        fields = lax.all_to_all(fields, "phys", split_axis=0, concat_axis=0, tiled=True)
        start_modes, start_send = pl.pallas_call(
            functools.partial(columns_kernel, *fixed),
            grid=(groups,),
            in_specs=[pl.BlockSpec((phys, 1, 2 * count, 128), lambda g: (0, g, 0, 0))]
            + [whole_spec(t.shape) for t in fwd[2:]],
            out_specs=[
                pl.BlockSpec((4, count, 2 * width), lambda g: (g, 0, 0)),
                whole_spec(send_shape),
            ],
            out_shape=modes_shape,
            compiler_params=params,
            name="columns",
        )(fields.reshape(phys, groups, 2 * count, 128), *fwd[2:])
    else:
        extra = field_count * phys - group_fields
        fields = jnp.pad(fields, ((0, extra), (0, 0), (0, 0)))
        fields = fields.reshape(phys, field_count, row_count, width)
        fields = lax.all_to_all(fields, "phys", split_axis=0, concat_axis=0, tiled=True)
        start_modes, start_send = pl.pallas_call(
            functools.partial(spectrum_kernel, *fixed),
            grid=(field_count,),
            in_specs=[pl.BlockSpec((phys, 1, row_count, width), lambda f: (0, f, 0, 0))]
            + [whole_spec(t.shape) for t in fwd],
            out_specs=[
                pl.BlockSpec((1, count, 2 * width), lambda f: (f, 0, 0)),
                whole_spec(send_shape),
            ],
            out_shape=modes_shape,
            compiler_params=params,
            name="spectrum",
        )(fields, *fwd)

    def exchange(send):
        rows = chunk
        if interleave:
            send = send.reshape(ang * phys, rows, 128)
        else:
            send = send.reshape(2, 2, phys, rows, 128 // block, block)
            send = send.transpose(1, 4, 2, 3, 0, 5).reshape(ang * phys, rows, 2 * block)
        got = lax.all_to_all(send, ("ang", "phys"), split_axis=0, concat_axis=0, tiled=True)
        return got.reshape(ang * phys * rows, 2 * block)

    start = exchange(start_send)

    stack = 4 if field_count % 4 == 0 else 1
    extra = [force, jnp.asarray(tables["wave_x"]), jnp.asarray(tables["wave_y"])]
    adv_send = pl.pallas_call(
        functools.partial(advance_kernel, *fixed),
        grid=(field_count // stack,),
        in_specs=[
            pl.BlockSpec(memory_space=pltpu.SMEM),
            pl.BlockSpec((stack, count, 2 * width), lambda f: (f, 0, 0)),
        ]
        + [whole_spec(t.shape) for t in extra + fwd + inv],
        out_specs=whole_spec(send_shape),
        out_shape=jax.ShapeDtypeStruct(send_shape, F32),
        cost_estimate=cost(field_count * 24 * count * 6 * width * width),
        compiler_params=params,
        name="advance",
    )(time_step, start_modes, *extra, *fwd, *inv)
    adv_send, start = lax.optimization_barrier((adv_send, start))
    advanced = exchange(adv_send)

    each = field_count // samples if field_count >= samples else field_count
    tables_s = 1 if field_count >= samples else samples
    index = np.arange(field_count)[:, None] + field_count * np.arange(phys)[None, :]
    index = np.broadcast_to(index[:, None, :], (field_count, ang, phys))
    first = np.arange(ang)[None, :, None] * angle_local + index // samples
    turn = 2.0 * math.pi / angle_total * np.mod(
        first[..., None] * np.arange(angle_total), angle_total
    )
    pair = np.concatenate([np.cos(turn), np.sin(turn)], axis=-1) / math.sqrt(angle_total)
    pair = np.where((index < group_fields)[..., None], pair, 0.0)
    matrix = []
    for s in range(tables_s):
        if tables_s == 1:
            rows = pair[::samples]
        else:
            rows = np.where((index % samples == s)[..., None], pair, 0.0)
        matrix.append(rows.reshape(each * ang * phys, 2 * angle_total).T)
    mat_hi, mat_lo = [jnp.asarray(t) for t in split_table(np.stack(matrix))]
    signed_angle = jnp.asarray(signed(np.arange(angle_total), angle_total).astype(np.float32))
    turns = jnp.stack(
        [
            jnp.tile(jnp.cos(signed_angle * rotation[0]), samples),
            jnp.tile(jnp.sin(signed_angle * rotation[0]), samples),
        ]
    )
    merged = samples * angle_total

    def to_angles(got, last):
        return pl.pallas_call(
            functools.partial(angle_kernel, plus, field_count, samples, chunk),
            in_specs=[pl.BlockSpec(memory_space=pltpu.VMEM)] * 4,
            out_specs=pl.BlockSpec(memory_space=pltpu.VMEM),
            out_shape=jax.ShapeDtypeStruct((2, plus, block, merged), F32),
            scratch_shapes=[pltpu.VMEM((plus * 2 * merged // 128, block, 128), F32)],
            cost_estimate=cost(2 * plus * 2 * block * 3 * mat_hi.shape[2] * 2 * merged),
            compiler_params=pltpu.CompilerParams(vmem_limit_bytes=40 * 1024 * 1024),
            name="angle",
        )(got, mat_hi, mat_lo, last)

    return to_angles(advanced, to_angles(start, turns))


def solution(mesh):
    in_specs = (P("ang", None, "phys", None), P(), P(), P())
    out_specs = P(None, "phys", "ang", None)

    def program(vorticity, forcing_mode, time_step, rotation):
        tables = make_tables(vorticity.shape[3], mesh.shape["phys"], mesh.shape["ang"])
        return jax.shard_map(
            functools.partial(local, tables),
            mesh=mesh,
            in_specs=in_specs,
            out_specs=out_specs,
            check_vma=False,
        )(vorticity, forcing_mode, time_step, rotation)

    return program
```

time: 188 us -> 163 us (0.87)
  Pallas kernels: 66 us -> 48.6 us
  blocking collectives: 43.1 us -> 32.6 us
  waiting for transfers between devices: 62.3 us -> 66.5 us
    pallas_call x3 -> x5, Pallas kernels: 66 us -> 48.6 us  [the longest x1 30.5 us: local(): pl.pallas_call(functools.partial(advance_kernel, *fixed), grid=(field_cou...]
    all_to_all x1, blocking collectives: 43.1 us -> 32.6 us  [local(): lax.all_to_all(fields, 'phys', split_axis=0, concat_axis=0, tiled=True)]
    all_to_all x2, waiting for transfers between devices: 62.3 us -> 66.5 us  [exchange(): lax.all_to_all(send, ('ang', 'phys'), split_axis=0, concat_axis=0, tiled=...]
    mul x2 -> x0, local copies, waits for them, and re-layouts: 2.19 us -> none  [local(): jnp.asarray(part.reshape(-1, 2, 1, angle_total)) * pick]
  transfers between devices with their start and end apart: 2 -> 2, of which waited for: 2 -> 2; matrix products, arithmetic and copies ran while one was open for 2% -> 1% of each run, Pallas kernels for 22% -> 20%
where the time goes in v3:
time: 163 us; the launch traced here: 162 us
  waiting for transfers between devices  66.5 us (41%)
  Pallas kernels  48.6 us (30%)
  blocking collectives  32.6 us (20%)
  starting transfers between devices  8.79 us (5%)
  local copies, waits for them, and re-layouts  3.13 us (2%)
  between operations  2.02 us (1%)
    all_to_all x2, waiting for transfers between devices, exchange(): lax.all_to_all(send, ('ang', 'phys'), split_axis=0, concat_axis=0, tiled=...  66.5 us
    all_to_all x1, blocking collectives, local(): lax.all_to_all(fields, 'phys', split_axis=0, concat_axis=0, tiled=True)  32.6 us
    pallas_call x1, Pallas kernels, local(): pl.pallas_call(functools.partial(advance_kernel, *fixed), grid=(field_cou...  30.5 us
    all_to_all x2, starting transfers between devices, exchange(): lax.all_to_all(send, ('ang', 'phys'), split_axis=0, concat_axis=0, tiled=...  8.79 us
    pallas_call x2, Pallas kernels, to_angles(): pl.pallas_call(functools.partial(angle_kernel, plus, field_count, samples...  7.41 us
    pallas_call x1, Pallas kernels, local(): pl.pallas_call(functools.partial(columns_kernel, *fixed), grid=(groups,),...  5.8 us
    pallas_call x1, Pallas kernels, local(): pl.pallas_call(rows_kernel, grid=(group_fields // 32,), in_specs=[pl.Bloc...  4.92 us
  transfers between devices with their start and end apart: 2, of which 2 were waited for; matrix products, arithmetic and copies ran while one was open for 1% of the time, Pallas kernels for 20%

profile of v3, /device:TPU:0, one launch (start us, length us, event | category | flops | bytes accessed | tf_op | source)
XLA Modules:
  0.0 162.2 jit_solution(1290964016644735643)
XLA Ops:
  0.0 4.9 %rows.1 = f32[24,176,128]{2,1,0:T(8,128)} custom-call(f32[96,32,256]{2,1,0:T(8,128)} %bitcast.14, bf16[176,256]{1,0:T(8,128)(2,1)} %constant.44.clone.fx_hi, bf16[176,256]{1,0:T(8,128)(2,1)} %constant.45.clone.fx_lo), custom_call_target="tpu_custom_call" | custom-call | tf_op jit(solution)/shard_map/rows/pallas_call | solution.py:366
  4.9 32.6 %all_to_all.15 = f32[8,528,128]{2,1,0:T(8,128)} all-to-all(f32[8,528,128]{2,1,0:T(8,128)} %bitcast.13), channel_id=1, replica_groups=mesh['phys'=8,'ang'=4] {'phys'}, dimensions={0} | all-to-all | bytes 4325376 | tf_op jit(solution)/shard_map/all_to_all | solution.py:377
  37.5 5.8 %columns.1 = (f32[12,88,512]{2,1,0:T(8,128)}, f32[4,1088,128]{2,1,0:T(8,128)}) custom-call(f32[8,3,176,128]{3,2,1,0:T(8,128)} %bitcast.12, bf16[256,256]{1,0:T(8,128)(2,1)} %constant.46.clone.e_hi, bf16[256,256]{1,0:T(8,128)(2,1)} %constant.47.clone.e_lo, bf16[256,256]{1,0:T(8,128)(2,1)} %constant.48.clone.o_hi, bf16[256,256]{1,0:T(8,128)(2,1)} %constant.49.clone.o_lo), custom_call_target="tpu_custom_call" | custom-call | tf_op jit(solution)/shard_map/columns/pallas_call | solution.py:378
  43.3 4.5 %all-to-all-start.1 = ((f32[32,136,128]{2,1,0:T(8,128)}), f32[32,136,128]{2,1,0:T(8,128)S(1)}, u32[]{:S(2)}, u32[]{:S(2)}) async-start(f32[32,136,128]{2,1,0:T(8,128)} %bitcast.16), calls=%async_computation.1 | async-start | bytes 4456448 | tf_op jit(solution)/shard_map/all_to_all | solution.py:417
  49.1 0.6 cosine_multiply_fusion.force_ref
  49.7 30.5 %advance.1 = f32[4,1088,128]{2,1,0:T(8,128)} custom-call(f32[1]{0:T(128)S(6)} %copy.25.dt_ref, f32[12,88,512]{2,1,0:T(8,128)} %get-tuple-element.9.s_ref, f32[1,256]{1,0:T(1,128)} %cosine_multiply_fusion.force_ref, f32[88,1]{1,0:T(8,128)} %constant.58.clone.wave_x_ref, f32[1,512]{1,0:T(1,128)} %constant.59.clone.wave_y_ref, ...), custom_call_target="tpu_custom_call" | custom-call | flops 9965666304 | bytes 8388608 | tf_op jit(solution)/shard_map/advance/pallas_call | solution.py:424
  80.2 19.3 %all-to-all-done.1 = f32[32,136,128]{2,1,0:T(8,128)S(1)} async-done(((f32[32,136,128]{2,1,0:T(8,128)}), f32[32,136,128]{2,1,0:T(8,128)S(1)}, u32[]{:S(2)}, u32[]{:S(2)}) %all-to-all-start.1) | async-done | bytes 2228256 | tf_op jit(solution)/shard_map/all_to_all | solution.py:417
  99.5 0.0 copy-start.4
  99.5 0.0 copy-start.2
  99.5 0.0 copy-start.3
  99.5 4.3 %all-to-all-start.2 = ((f32[32,136,128]{2,1,0:T(8,128)}), f32[32,136,128]{2,1,0:T(8,128)}, u32[]{:S(2)}, u32[]{:S(2)}) async-start(f32[32,136,128]{2,1,0:T(8,128)} %bitcast.15), calls=%async_computation.2 | async-start | bytes 4456448 | tf_op jit(solution)/shard_map/all_to_all | solution.py:417
  104.5 0.0 copy-done.4
  104.5 0.1 stack_tile.6
  104.6 0.1 stack_tile.7
  104.7 0.0 copy-done.2
  104.7 0.0 copy-done.3
  104.7 2.2 %angle.2.last_ref = f32[2,11,64,384]{3,2,1,0:T(8,128)S(1)} custom-call(f32[4352,128]{1,0:T(8,128)S(1)} %bitcast.11, bf16[1,192,96]{2,1,0:T(8,128)(2,1)S(1)} %copy-done.2, bf16[1,192,96]{2,1,0:T(8,128)(2,1)S(1)} %copy-done.3, f32[2,384]{1,0:T(2,128)S(1)} %pad_maximum_fusion.last_ref), custom_call_target="tpu_custom_call" | custom-call | flops 622854144 | bytes 8388608 | tf_op jit(solution)/shard_map/angle/pallas_call | solution.py:469
  106.9 0.0 copy-start
  107.0 1.3 copy-done
  108.3 47.1 %all-to-all-done.2 = f32[32,136,128]{2,1,0:T(8,128)} async-done(((f32[32,136,128]{2,1,0:T(8,128)}), f32[32,136,128]{2,1,0:T(8,128)}, u32[]{:S(2)}, u32[]{:S(2)}) %all-to-all-start.2) | async-done | bytes 2228256 | tf_op jit(solution)/shard_map/all_to_all | solution.py:417
  155.4 0.0 copy-start.1
  155.4 1.6 copy-done.1
  157.0 5.2 %angle.3 = f32[2,11,64,384]{3,2,1,0:T(8,128)} custom-call(f32[4352,128]{1,0:T(8,128)} %bitcast.8.got_ref, bf16[1,192,96]{2,1,0:T(8,128)(2,1)S(1)} %copy-done.2, bf16[1,192,96]{2,1,0:T(8,128)(2,1)S(1)} %copy-done.3, f32[2,11,64,384]{3,2,1,0:T(8,128)S(1)} %copy-done.1), custom_call_target="tpu_custom_call" | custom-call | flops 622854144 | bytes 8388608 | tf_op jit(solution)/shard_map/angle/pallas_call | solution.py:469
  (4 shorter events, 0.1 us)
Async XLA Ops:
  43.3 56.2 %all-to-all-start.1 = ((f32[32,136,128]{2,1,0:T(8,128)}), f32[32,136,128]{2,1,0:T(8,128)S(1)}, u32[]{:S(2)}, u32[]{:S(2)}) async-start(f32[32,136,128]{2,1,0:T(8,128)} %bitcast.16), calls=%async_computation.1 | async-start | bytes 4456448 | tf_op jit(solution)/shard_map/all_to_all | solution.py:417
  99.5 5.0 %copy-start.4 = (f32[96]{0:T(128)S(1)}, f32[96]{0:T(128)}, u32[]{:S(2)}) copy-start(f32[96]{0:T(128)} %constant.62.clone) | copy-start | bytes 1156
  99.5 5.2 %copy-start.2 = (bf16[1,192,96]{2,1,0:T(8,128)(2,1)S(1)}, bf16[1,192,96]{2,1,0:T(8,128)(2,1)}, u32[]{:S(2)}) copy-start(bf16[1,192,96]{2,1,0:T(8,128)(2,1)} %constant.60.clone.mat_hi) | copy-start | bytes 110596
  99.5 5.2 %copy-start.3 = (bf16[1,192,96]{2,1,0:T(8,128)(2,1)S(1)}, bf16[1,192,96]{2,1,0:T(8,128)(2,1)}, u32[]{:S(2)}) copy-start(bf16[1,192,96]{2,1,0:T(8,128)(2,1)} %constant.61.clone.mat_lo) | copy-start | bytes 110596
  99.5 55.9 %all-to-all-start.2 = ((f32[32,136,128]{2,1,0:T(8,128)}), f32[32,136,128]{2,1,0:T(8,128)}, u32[]{:S(2)}, u32[]{:S(2)}) async-start(f32[32,136,128]{2,1,0:T(8,128)} %bitcast.15), calls=%async_computation.2 | async-start | bytes 4456448 | tf_op jit(solution)/shard_map/all_to_all | solution.py:417
  106.9 1.3 copy-start
  155.4 1.6 copy-start.1

commit v4 on v3

--- a/solution.py
+++ b/solution.py
@@ -173,18 +173,20 @@
     return swap_lanes(left[0], right[0], 32) + swap_lanes(left[1], right[1], 32)
 
 
-def columns_kernel(
-    interleave, field_count, plus, x_ref, e_hi, e_lo, o_hi, o_lo, s_ref, send_ref
-):
+def four_modes(x_ref, e_hi, e_lo, o_hi, o_lo):
     halves = [gather_rows([x_ref[4 * h + q, 0] for q in range(4)]) for h in range(2)]
     fields = [jnp.concatenate([halves[0][i], halves[1][i]], axis=1) for i in range(4)]
     count = fields[0].shape[0] // 2
     rows = jnp.concatenate([f[:count] for f in fields] + [f[count:] for f in fields], axis=0)
     modes = forward_y(rows, (e_hi, e_lo, o_hi, o_lo))
+    return [modes[i * count : (i + 1) * count] for i in range(4)]
+
+
+def columns_kernel(interleave, field_count, plus, x_ref, e_hi, e_lo, o_hi, o_lo, send_ref):
+    modes = four_modes(x_ref, e_hi, e_lo, o_hi, o_lo)
     for i in range(4):
-        own = modes[i * count : (i + 1) * count]
-        s_ref[i] = own
-        store_send(send_ref, own, pl.program_id(0) * 4 + i, field_count, plus, interleave)
+        field = pl.program_id(0) * 4 + i
+        store_send(send_ref, modes[i], field, field_count, plus, interleave)
 
 
 def spectrum_kernel(interleave, field_count, plus, x_ref, fx_hi, fx_lo, e_hi, e_lo, o_hi, o_lo, s_ref, send_ref):
@@ -224,8 +226,12 @@
     yo_lo,
     send_ref,
 ):
-    stack, count = s_ref.shape[:2]
-    width = s_ref.shape[2] // 2
+    if len(s_ref.shape) == 4:
+        spectra = four_modes(s_ref, e_hi, e_lo, o_hi, o_lo)
+    else:
+        spectra = [s_ref[i] for i in range(s_ref.shape[0])]
+    stack = len(spectra)
+    count, width = spectra[0].shape[0], spectra[0].shape[1] // 2
     half = width // 2
     wave_x, wave_y = wave_x_ref[...], wave_y_ref[...]
     wave_sq = wave_x * wave_x + wave_y * wave_y
@@ -264,7 +270,6 @@
         return [out[i * count : (i + 1) * count] - damping * modes[i] for i in range(stack)]
 
     step = dt_ref[0]
-    spectra = [s_ref[i] for i in range(stack)]
     middle = [s + (0.5 * step) * t for s, t in zip(spectra, tendency(spectra))]
     second = tendency(middle)
     for i in range(stack):
@@ -274,16 +279,49 @@
 
 
 def angle_kernel(
-    plus, field_count, samples, chunk, got_ref, mat_hi, mat_lo, last_ref, out_ref, rows_ref
+    plus,
+    field_count,
+    samples,
+    turning,
+    got_hbm,
+    mat_hi,
+    mat_lo,
+    last_ref,
+    out_hbm,
+    got_ref,
+    last_buf,
+    out_buf,
+    rows_ref,
+    got_sem,
+    last_sem,
+    out_sem,
 ):
-    sources = got_ref.shape[0] // chunk
-    lanes = got_ref.shape[1]
+    sources, chunk, lanes = got_hbm.shape
     modes = mat_hi.shape[1] // 2
     quarter = lanes // 4
     merged = samples * modes
     blocks = merged // 128
-    turning = len(last_ref.shape) == 2
+    parts = input_parts(plus, field_count, chunk)
+    loads = []
+    for n, (first_k, first, size) in enumerate(parts):
+        place = (slice(None), slice(first, first + size))
+        copies = [pltpu.make_async_copy(got_hbm.at[place], got_ref.at[place], got_sem.at[n])]
+        if not turning:
+            last_k = parts[n + 1][0] if n + 1 < len(parts) else plus
+            place = (slice(None), slice(first_k, last_k))
+            copies.append(
+                pltpu.make_async_copy(last_ref.at[place], last_buf.at[place], last_sem.at[n])
+            )
+        for copy in copies:
+            copy.start()
+        loads.append((first_k, copies))
+    flat = got_ref.reshape(sources * chunk, lanes)
+    stores = []
     for k in range(plus):
+        for first_k, copies in loads:
+            if first_k == k:
+                for copy in copies:
+                    copy.wait()
         cos_rows, sin_rows = [], []
         for s in range(samples):
             if field_count < samples:
@@ -291,7 +329,7 @@
             else:
                 picks, table = range(s, field_count, samples), 0
             values = jnp.concatenate(
-                [got_ref[pl.ds(k * field_count + f, sources, stride=chunk), :] for f in picks],
+                [flat[pl.ds(k * field_count + f, sources, stride=chunk), :] for f in picks],
                 axis=0,
             )
             result = left_mul(mat_hi.at[table], mat_lo.at[table], values)
@@ -318,11 +356,27 @@
         for part in range(2):
             place = (k * 2 + part) * blocks
             joined = jnp.concatenate([rows_ref[place + b] for b in range(blocks)], axis=1)
-            out_ref[part, k] = joined if turning else joined + last_ref[part, k]
+            out_buf[part, k] = joined if turning else joined + last_buf[part, k]
+        copy = pltpu.make_async_copy(out_buf.at[:, k], out_hbm.at[:, k], out_sem.at[k])
+        copy.start()
+        stores.append(copy)
+    for copy in stores:
+        copy.wait()
+
+
+def input_parts(plus, field_count, chunk):
+    cuts = [k for k in range(1, plus) if k % 4 == 0 and k * field_count % 8 == 0]
+    firsts = [0] + cuts
+    rows = [k * field_count for k in firsts] + [chunk]
+    return [(k, rows[n], rows[n + 1] - rows[n]) for n, k in enumerate(firsts)]
 
 
 def cost(flops):
     return pl.CostEstimate(flops=int(flops), bytes_accessed=8 * 1024 * 1024, transcendentals=0)
+
+
+def in_hbm(values):
+    return pltpu.with_memory_space_constraint(values, pltpu.HBM)
 
 
 def whole_spec(shape):
@@ -351,16 +405,15 @@
     fwd = list(tables["fwd_x"]) + list(tables["fwd_y"][0]) + list(tables["fwd_y"][1])
     fwd = [jnp.asarray(t) for t in fwd]
     inv = list(tables["inv_x"]) + list(tables["inv_kx"]) + list(tables["inv_y"][0]) + list(tables["inv_y"][1])
-    inv = [jnp.asarray(t) for t in inv]
-    params = pltpu.CompilerParams(
-        dimension_semantics=("arbitrary",), vmem_limit_bytes=56 * 1024 * 1024
-    )
+    inv = [in_hbm(jnp.asarray(t)) for t in inv]
+    def params(megabytes):
+        return pltpu.CompilerParams(
+            dimension_semantics=("arbitrary",), vmem_limit_bytes=megabytes * 1024 * 1024
+        )
+
     send_shape = (4, phys * chunk, 128)
     fixed = (interleave, field_count, plus)
-    modes_shape = [
-        jax.ShapeDtypeStruct((field_count, count, 2 * width), F32),
-        jax.ShapeDtypeStruct(send_shape, F32),
-    ]
+    send_out = pltpu.HBM(send_shape, F32)
     if row_count == 32 and phys == 8 and group_fields % 32 == 0:
         groups = field_count // 4
         fields = pl.pallas_call(
@@ -370,30 +423,29 @@
             + [whole_spec(t.shape) for t in fwd[:2]],
             out_specs=pl.BlockSpec((8, 2 * count, 128), lambda n: (n, 0, 0)),
             out_shape=jax.ShapeDtypeStruct((group_fields // 4, 2 * count, 128), F32),
-            compiler_params=params,
+            compiler_params=params(20),
             name="rows",
-        )(fields, *fwd[:2])
+        )(in_hbm(fields), *map(in_hbm, fwd[:2]))
         fields = fields.reshape(phys, groups * 2 * count, 128)
         fields = lax.all_to_all(fields, "phys", split_axis=0, concat_axis=0, tiled=True)
-        start_modes, start_send = pl.pallas_call(
+        spectra = fields.reshape(phys, groups, 2 * count, 128)
+        spectra_spec = pl.BlockSpec((phys, 1, 2 * count, 128), lambda g: (0, g, 0, 0))
+        start_send = pl.pallas_call(
             functools.partial(columns_kernel, *fixed),
             grid=(groups,),
-            in_specs=[pl.BlockSpec((phys, 1, 2 * count, 128), lambda g: (0, g, 0, 0))]
-            + [whole_spec(t.shape) for t in fwd[2:]],
-            out_specs=[
-                pl.BlockSpec((4, count, 2 * width), lambda g: (g, 0, 0)),
-                whole_spec(send_shape),
-            ],
-            out_shape=modes_shape,
-            compiler_params=params,
+            in_specs=[spectra_spec] + [whole_spec(t.shape) for t in fwd[2:]],
+            out_specs=whole_spec(send_shape),
+            out_shape=jax.ShapeDtypeStruct(send_shape, F32),
+            compiler_params=params(20),
             name="columns",
-        )(fields.reshape(phys, groups, 2 * count, 128), *fwd[2:])
+        )(spectra, *fwd[2:])
+        stack = 4
     else:
         extra = field_count * phys - group_fields
         fields = jnp.pad(fields, ((0, extra), (0, 0), (0, 0)))
         fields = fields.reshape(phys, field_count, row_count, width)
         fields = lax.all_to_all(fields, "phys", split_axis=0, concat_axis=0, tiled=True)
-        start_modes, start_send = pl.pallas_call(
+        spectra, start_send = pl.pallas_call(
             functools.partial(spectrum_kernel, *fixed),
             grid=(field_count,),
             in_specs=[pl.BlockSpec((phys, 1, row_count, width), lambda f: (0, f, 0, 0))]
@@ -402,10 +454,15 @@
                 pl.BlockSpec((1, count, 2 * width), lambda f: (f, 0, 0)),
                 whole_spec(send_shape),
             ],
-            out_shape=modes_shape,
-            compiler_params=params,
+            out_shape=[
+                jax.ShapeDtypeStruct((field_count, count, 2 * width), F32),
+                jax.ShapeDtypeStruct(send_shape, F32),
+            ],
+            compiler_params=params(24),
             name="spectrum",
         )(fields, *fwd)
+        spectra_spec = pl.BlockSpec((1, count, 2 * width), lambda f: (f, 0, 0))
+        stack = 1
 
     def exchange(send):
         rows = chunk
@@ -415,26 +472,25 @@
             send = send.reshape(2, 2, phys, rows, 128 // block, block)
             send = send.transpose(1, 4, 2, 3, 0, 5).reshape(ang * phys, rows, 2 * block)
         got = lax.all_to_all(send, ("ang", "phys"), split_axis=0, concat_axis=0, tiled=True)
-        return got.reshape(ang * phys * rows, 2 * block)
+        return got
 
     start = exchange(start_send)
 
-    stack = 4 if field_count % 4 == 0 else 1
     extra = [force, jnp.asarray(tables["wave_x"]), jnp.asarray(tables["wave_y"])]
     adv_send = pl.pallas_call(
         functools.partial(advance_kernel, *fixed),
         grid=(field_count // stack,),
         in_specs=[
             pl.BlockSpec(memory_space=pltpu.SMEM),
-            pl.BlockSpec((stack, count, 2 * width), lambda f: (f, 0, 0)),
+            spectra_spec,
         ]
         + [whole_spec(t.shape) for t in extra + fwd + inv],
         out_specs=whole_spec(send_shape),
-        out_shape=jax.ShapeDtypeStruct(send_shape, F32),
+        out_shape=send_out,
         cost_estimate=cost(field_count * 24 * count * 6 * width * width),
-        compiler_params=params,
+        compiler_params=params(36),
         name="advance",
-    )(time_step, start_modes, *extra, *fwd, *inv)
+    )(time_step, spectra, *extra, *map(in_hbm, fwd), *inv)
     adv_send, start = lax.optimization_barrier((adv_send, start))
     advanced = exchange(adv_send)
 
@@ -465,19 +521,33 @@
     )
     merged = samples * angle_total
 
-    def to_angles(got, last):
+    parts = len(input_parts(plus, field_count, chunk))
+    out_shape = (2, plus, block, merged)
+    vmem = pl.BlockSpec(memory_space=pltpu.VMEM)
+    hbm = pl.BlockSpec(memory_space=pltpu.HBM)
+
+    def to_angles(got, last, turning):
         return pl.pallas_call(
-            functools.partial(angle_kernel, plus, field_count, samples, chunk),
-            in_specs=[pl.BlockSpec(memory_space=pltpu.VMEM)] * 4,
-            out_specs=pl.BlockSpec(memory_space=pltpu.VMEM),
-            out_shape=jax.ShapeDtypeStruct((2, plus, block, merged), F32),
-            scratch_shapes=[pltpu.VMEM((plus * 2 * merged // 128, block, 128), F32)],
+            functools.partial(angle_kernel, plus, field_count, samples, turning),
+            in_specs=[hbm, vmem, vmem, vmem if turning else hbm],
+            out_specs=hbm,
+            out_shape=pltpu.HBM(out_shape, F32),
+            scratch_shapes=[
+                pltpu.VMEM(got.shape, F32),
+                pltpu.VMEM((8, 128) if turning else out_shape, F32),
+                pltpu.VMEM(out_shape, F32),
+                pltpu.VMEM((plus * 2 * merged // 128, block, 128), F32),
+                pltpu.SemaphoreType.DMA((parts,)),
+                pltpu.SemaphoreType.DMA((parts,)),
+                pltpu.SemaphoreType.DMA((plus,)),
+            ],
             cost_estimate=cost(2 * plus * 2 * block * 3 * mat_hi.shape[2] * 2 * merged),
-            compiler_params=pltpu.CompilerParams(vmem_limit_bytes=40 * 1024 * 1024),
+            compiler_params=pltpu.CompilerParams(vmem_limit_bytes=20 * 1024 * 1024),
             name="angle",
         )(got, mat_hi, mat_lo, last)
 
-    return to_angles(advanced, to_angles(start, turns))
+    start_part = in_hbm(to_angles(start, turns, True))
+    return to_angles(advanced, start_part, False)
 
 
 def solution(mesh):

time: 163 us -> 158 us (0.969)
  waiting for transfers between devices: 66.5 us -> 63.3 us
    all_to_all x2, waiting for transfers between devices: 66.5 us -> 63.3 us  [exchange(): lax.all_to_all(send, ('ang', 'phys'), split_axis=0, concat_axis=0, tiled=...]
    pallas_call x1, Pallas kernels: 5.8 us -> 3.04 us  [local(): pl.pallas_call(functools.partial(columns_kernel, *fixed), grid=(groups,),...]
    pallas_call x1, Pallas kernels: 30.5 us -> 32.3 us  [local(): pl.pallas_call(functools.partial(advance_kernel, *fixed), grid=(field_cou...]
  transfers between devices with their start and end apart: 2 -> 2, of which waited for: 2 -> 2; matrix products, arithmetic and copies ran while one was open for 1% -> 0% of each run, Pallas kernels for 20% -> 23%
where the time goes in v4:
time: 158 us
  waiting for transfers between devices  63.3 us (40%)
  Pallas kernels  48 us (30%)
  blocking collectives  32.4 us (21%)
  starting transfers between devices  8.27 us (5%)
  local copies, waits for them, and re-layouts  3.2 us (2%)
  between operations  2.27 us (1%)
    all_to_all x2, waiting for transfers between devices, exchange(): lax.all_to_all(send, ('ang', 'phys'), split_axis=0, concat_axis=0, tiled=...  63.3 us
    all_to_all x1, blocking collectives, local(): lax.all_to_all(fields, 'phys', split_axis=0, concat_axis=0, tiled=True)  32.4 us
    pallas_call x1, Pallas kernels, local(): pl.pallas_call(functools.partial(advance_kernel, *fixed), grid=(field_cou...  32.3 us
    pallas_call x2, Pallas kernels, to_angles(): pl.pallas_call(functools.partial(angle_kernel, plus, field_count, samples...  8.88 us
    all_to_all x2, starting transfers between devices, exchange(): lax.all_to_all(send, ('ang', 'phys'), split_axis=0, concat_axis=0, tiled=...  8.27 us
    pallas_call x1, Pallas kernels, local(): pl.pallas_call(rows_kernel, grid=(group_fields // 32,), in_specs=[pl.Bloc...  3.81 us
  transfers between devices with their start and end apart: 2, of which 2 were waited for; matrix products, arithmetic and copies ran while one was open for 0% of the time, Pallas kernels for 23%

profile of v4, /device:TPU:0, one launch (start us, length us, event | category | flops | bytes accessed | tf_op | source)
XLA Modules:
  0.0 157.6 jit_solution(11980507418027309654)
XLA Ops:
  0.0 3.8 %rows.1 = f32[24,176,128]{2,1,0:T(8,128)S(1)} custom-call(f32[96,32,256]{2,1,0:T(8,128)} %bitcast.13, bf16[176,256]{1,0:T(8,128)(2,1)} %constant.44.clone.fx_hi, bf16[176,256]{1,0:T(8,128)(2,1)} %constant.45.clone.fx_lo), custom_call_target="tpu_custom_call" | custom-call | tf_op jit(solution)/shard_map/rows/pallas_call | solution.py:419
  3.8 0.0 copy-start.5
  3.8 0.0 copy-start.6
  3.8 0.0 copy-start.7
  3.9 0.0 copy-start.8
  3.9 32.4 %all_to_all.15 = f32[8,528,128]{2,1,0:T(8,128)S(1)} all-to-all(f32[8,528,128]{2,1,0:T(8,128)S(1)} %bitcast.12), channel_id=1, replica_groups=mesh['phys'=8,'ang'=4] {'phys'}, dimensions={0} | all-to-all | bytes 4325376 | tf_op jit(solution)/shard_map/all_to_all | solution.py:430
  36.3 0.0 copy-start.1
  36.3 0.0 copy-done.5
  36.3 0.0 copy-done.6
  36.3 0.0 copy-done.7
  36.3 0.0 copy-done.8
  36.3 3.0 %columns.1 = f32[4,1088,128]{2,1,0:T(8,128)S(1)} custom-call(f32[8,3,176,128]{3,2,1,0:T(8,128)S(1)} %bitcast.10, bf16[256,256]{1,0:T(8,128)(2,1)S(1)} %copy-done.5, bf16[256,256]{1,0:T(8,128)(2,1)S(1)} %copy-done.6, bf16[256,256]{1,0:T(8,128)(2,1)S(1)} %copy-done.7, bf16[256,256]{1,0:T(8,128)(2,1)S(1)} %copy-done.8), custom_call_target="tpu_custom_call" | custom-call | tf_op jit(solution)/shard_map/columns/pallas_call | solution.py:433
  39.3 0.0 copy-done.1
  39.4 0.0 copy-start
  39.4 1.4 copy-done
  40.7 0.0 copy-start.9
  40.7 0.0 copy-start.10
  40.7 4.0 %all-to-all-start.1 = ((f32[32,136,128]{2,1,0:T(8,128)}), f32[32,136,128]{2,1,0:T(8,128)S(1)}, u32[]{:S(2)}, u32[]{:S(2)}) async-start(f32[32,136,128]{2,1,0:T(8,128)} %bitcast.9), calls=%async_computation.1 | async-start | bytes 4456448 | tf_op jit(solution)/shard_map/all_to_all | solution.py:474
  46.0 0.1 cosine_multiply_fusion.force_ref
  46.1 0.0 copy-done.9
  46.1 0.0 copy-done.10
  46.1 0.0 copy-start.2
  46.1 1.6 %copy-done.2 = f32[8,528,128]{2,1,0:T(8,128)S(1)} copy-done((f32[8,528,128]{2,1,0:T(8,128)S(1)}, f32[8,528,128]{2,1,0:T(8,128)}, u32[]{:S(2)}) %copy-start.2) | copy-done | bytes 2162712
  47.7 32.3 %advance.1 = f32[4,1088,128]{2,1,0:T(8,128)} custom-call(f32[1]{0:T(128)S(6)} %copy.25.dt_ref, f32[8,3,176,128]{3,2,1,0:T(8,128)S(1)} %bitcast.11, f32[1,256]{1,0:T(1,128)S(1)} %cosine_multiply_fusion.force_ref, f32[88,1]{1,0:T(8,128)S(1)} %copy-done.9, f32[1,512]{1,0:T(1,128)S(1)} %copy-done.10, bf16[176,256]{1,0:T(8,128)(2,1)} %constant.44.clone.fx_hi, ...), custom_call_target="tpu_custom_call" | custom-call | flops 9965666304 | bytes 8388608 | tf_op jit(solution)/shard_map/advance/pallas_call | solution.py:480
  80.0 16.5 %all-to-all-done.1.got_hbm = f32[32,136,128]{2,1,0:T(8,128)S(1)} async-done(((f32[32,136,128]{2,1,0:T(8,128)}), f32[32,136,128]{2,1,0:T(8,128)S(1)}, u32[]{:S(2)}, u32[]{:S(2)}) %all-to-all-start.1) | async-done | bytes 2228256 | tf_op jit(solution)/shard_map/all_to_all | solution.py:474
  96.4 0.0 copy-start.11
  96.4 0.0 copy-start.3
  96.4 0.0 copy-start.4
  96.4 4.3 %all-to-all-start.2 = ((f32[32,136,128]{2,1,0:T(8,128)}), f32[32,136,128]{2,1,0:T(8,128)}, u32[]{:S(2)}, u32[]{:S(2)}) async-start(f32[32,136,128]{2,1,0:T(8,128)} %bitcast.14), calls=%async_computation.2 | async-start | bytes 4456448 | tf_op jit(solution)/shard_map/all_to_all | solution.py:474
  101.4 0.0 copy-done.11
  101.5 0.1 stack_tile.6
  101.5 0.1 stack_tile.7
  101.6 0.0 copy-done.3
  101.7 0.0 copy-done.4
  101.7 3.8 %angle.2.last_ref = f32[2,11,64,384]{3,2,1,0:T(8,128)} custom-call(f32[32,136,128]{2,1,0:T(8,128)S(1)} %all-to-all-done.1.got_hbm, bf16[1,192,96]{2,1,0:T(8,128)(2,1)S(1)} %copy-done.3, bf16[1,192,96]{2,1,0:T(8,128)(2,1)S(1)} %copy-done.4, f32[2,384]{1,0:T(2,128)S(1)} %pad_maximum_fusion.last_ref), custom_call_target="tpu_custom_call" | custom-call | flops 622854144 | bytes 8388608 | tf_op jit(solution)/shard_map/angle/pallas_call | solution.py:530
  105.5 46.9 %all-to-all-done.2.got_hbm = f32[32,136,128]{2,1,0:T(8,128)} async-done(((f32[32,136,128]{2,1,0:T(8,128)}), f32[32,136,128]{2,1,0:T(8,128)}, u32[]{:S(2)}, u32[]{:S(2)}) %all-to-all-start.2) | async-done | bytes 2228256 | tf_op jit(solution)/shard_map/all_to_all | solution.py:474
  152.3 5.1 %angle.3 = f32[2,11,64,384]{3,2,1,0:T(8,128)} custom-call(f32[32,136,128]{2,1,0:T(8,128)} %all-to-all-done.2.got_hbm, bf16[1,192,96]{2,1,0:T(8,128)(2,1)S(1)} %copy-done.3, bf16[1,192,96]{2,1,0:T(8,128)(2,1)S(1)} %copy-done.4, f32[2,11,64,384]{3,2,1,0:T(8,128)} %angle.2.last_ref), custom_call_target="tpu_custom_call" | custom-call | flops 622854144 | bytes 8388608 | tf_op jit(solution)/shard_map/angle/pallas_call | solution.py:530
  (4 shorter events, 0.1 us)
Async XLA Ops:
  3.8 32.5 %copy-start.5 = (bf16[256,256]{1,0:T(8,128)(2,1)S(1)}, bf16[256,256]{1,0:T(8,128)(2,1)}, u32[]{:S(2)}) copy-start(bf16[256,256]{1,0:T(8,128)(2,1)} %constant.46.clone.e_hi) | copy-start | bytes 393220
  3.8 32.4 %copy-start.6 = (bf16[256,256]{1,0:T(8,128)(2,1)S(1)}, bf16[256,256]{1,0:T(8,128)(2,1)}, u32[]{:S(2)}) copy-start(bf16[256,256]{1,0:T(8,128)(2,1)} %constant.47.clone.e_lo) | copy-start | bytes 393220
  3.8 32.4 %copy-start.7 = (bf16[256,256]{1,0:T(8,128)(2,1)S(1)}, bf16[256,256]{1,0:T(8,128)(2,1)}, u32[]{:S(2)}) copy-start(bf16[256,256]{1,0:T(8,128)(2,1)} %constant.48.clone.o_hi) | copy-start | bytes 393220
  3.9 32.4 %copy-start.8 = (bf16[256,256]{1,0:T(8,128)(2,1)S(1)}, bf16[256,256]{1,0:T(8,128)(2,1)}, u32[]{:S(2)}) copy-start(bf16[256,256]{1,0:T(8,128)(2,1)} %constant.49.clone.o_lo) | copy-start | bytes 393220
  36.3 3.1 %copy-start.1 = (f32[8,528,128]{2,1,0:T(8,128)}, f32[8,528,128]{2,1,0:T(8,128)S(1)}, u32[]{:S(2)}) copy-start(f32[8,528,128]{2,1,0:T(8,128)S(1)} %all_to_all.15) | copy-start | bytes 6488068
  39.4 1.4 copy-start
  40.7 5.3 %copy-start.9 = (f32[88,1]{1,0:T(8,128)S(1)}, f32[88,1]{1,0:T(8,128)}, u32[]{:S(2)}) copy-start(f32[88,1]{1,0:T(8,128)} %constant.58.clone.wave_x_ref) | copy-start | bytes 1060
  40.7 5.3 %copy-start.10 = (f32[1,512]{1,0:T(1,128)S(1)}, f32[1,512]{1,0:T(1,128)}, u32[]{:S(2)}) copy-start(f32[1,512]{1,0:T(1,128)} %constant.59.clone.wave_y_ref) | copy-start | bytes 6148
  40.7 55.7 %all-to-all-start.1 = ((f32[32,136,128]{2,1,0:T(8,128)}), f32[32,136,128]{2,1,0:T(8,128)S(1)}, u32[]{:S(2)}, u32[]{:S(2)}) async-start(f32[32,136,128]{2,1,0:T(8,128)} %bitcast.9), calls=%async_computation.1 | async-start | bytes 4456448 | tf_op jit(solution)/shard_map/all_to_all | solution.py:474
  46.1 1.6 %copy-start.2 = (f32[8,528,128]{2,1,0:T(8,128)S(1)}, f32[8,528,128]{2,1,0:T(8,128)}, u32[]{:S(2)}) copy-start(f32[8,528,128]{2,1,0:T(8,128)} %copy-done.1) | copy-start | bytes 6488068
  96.4 5.0 %copy-start.11 = (f32[96]{0:T(128)S(1)}, f32[96]{0:T(128)}, u32[]{:S(2)}) copy-start(f32[96]{0:T(128)} %constant.62.clone) | copy-start | bytes 1156
  96.4 5.2 %copy-start.3 = (bf16[1,192,96]{2,1,0:T(8,128)(2,1)S(1)}, bf16[1,192,96]{2,1,0:T(8,128)(2,1)}, u32[]{:S(2)}) copy-start(bf16[1,192,96]{2,1,0:T(8,128)(2,1)} %constant.60.clone.mat_hi) | copy-start | bytes 110596
  96.4 5.2 %copy-start.4 = (bf16[1,192,96]{2,1,0:T(8,128)(2,1)S(1)}, bf16[1,192,96]{2,1,0:T(8,128)(2,1)}, u32[]{:S(2)}) copy-start(bf16[1,192,96]{2,1,0:T(8,128)(2,1)} %constant.61.clone.mat_lo) | copy-start | bytes 110596
  96.4 55.9 %all-to-all-start.2 = ((f32[32,136,128]{2,1,0:T(8,128)}), f32[32,136,128]{2,1,0:T(8,128)}, u32[]{:S(2)}, u32[]{:S(2)}) async-start(f32[32,136,128]{2,1,0:T(8,128)} %bitcast.14), calls=%async_computation.2 | async-start | bytes 4456448 | tf_op jit(solution)/shard_map/all_to_all | solution.py:474

commit v5 on v4

--- a/solution.py
+++ b/solution.py
@@ -137,6 +137,9 @@
         pieces = out
     phys = modes.shape[0] // plus
     chunk = send_ref.shape[1] // phys
+    if chunk < plus * field_count:
+        store_levelled(send_ref, pieces, field, field_count)
+        return
     whole, rest = 8 * (plus // 8), plus % 8
     for owner in range(phys):
         parts = [(owner * whole, whole, 0), (phys * whole + owner * rest, rest, whole)]
@@ -146,6 +149,36 @@
             place = pl.ds(owner * chunk + first * field_count + field, size, stride=field_count)
             for b in range(4):
                 send_ref[b, place, :] = pieces[b][start : start + size]
+
+
+def store_levelled(send_ref, pieces, field, field_count):
+    phys = 8
+    chunk = send_ref.shape[1] // phys
+    lane = lax.broadcasted_iota(jnp.int32, pieces[0].shape, 1)
+    low = lane % 32 < 16
+
+    def pair(values, other, upper):
+        if upper:
+            return jnp.where(low, pltpu.roll(values, 128 - 16, 1), other)
+        return jnp.where(low, values, pltpu.roll(other, 16, 1))
+
+    def put(owner, p, unit, rows):
+        place = pl.ds(p * chunk + unit * field_count + field, rows.shape[0], stride=field_count)
+        send_ref[owner, place, :] = rows
+
+    count = pieces[0].shape[0]
+    for end, middle in ((0, 1), (3, 2)):
+        whole, part = pieces[end], pieces[middle]
+        fours = pair(part, pltpu.roll(part, count - 4, 0), middle == 2)
+        ones = pair(part, pltpu.roll(part, count - 1, 0), middle == 2)
+        for p in range(phys):
+            tail = 64 + 3 * p
+            put(end, p, 0, whole[8 * p : 8 * p + 8])
+            put(end, p, 8, whole[tail : tail + 1])
+            put(middle, p, 0, whole[tail + 1 : tail + 3])
+            put(middle, p, 2, fours[8 * p : 8 * p + 4])
+            put(middle, p, 6, ones[tail : tail + 1])
+            put(middle, p, 7, ones[tail + 2 : tail + 3])
 
 
 def rows_kernel(x_ref, fx_hi, fx_lo, out_ref):
@@ -357,17 +390,50 @@
             place = (k * 2 + part) * blocks
             joined = jnp.concatenate([rows_ref[place + b] for b in range(blocks)], axis=1)
             out_buf[part, k] = joined if turning else joined + last_buf[part, k]
-        copy = pltpu.make_async_copy(out_buf.at[:, k], out_hbm.at[:, k], out_sem.at[k])
-        copy.start()
-        stores.append(copy)
+        if out_hbm is not None:
+            copy = pltpu.make_async_copy(out_buf.at[:, k], out_hbm.at[:, k], out_sem.at[k])
+            copy.start()
+            stores.append(copy)
     for copy in stores:
         copy.wait()
+
+
+def place_kernel(field_count, samples, kind_ref, got_hbm, mat_hi, mat_lo, last_ref, out_ref, *scratch):
+    kind = kind_ref[0]
+    result_buf = scratch[2]
+    units = result_buf.shape[1]
+    angle_kernel(
+        units, field_count, samples, False, got_hbm, mat_hi, mat_lo, last_ref, None, *scratch
+    )
+    half = out_ref.shape[2] // 2
+    zeros = jnp.zeros((2, 1) + out_ref.shape[2:], F32)
+
+    @pl.when(kind == 0)
+    def _():
+        out_ref[:, :units] = result_buf[...]
+        for k in range(units, out_ref.shape[1]):
+            out_ref[:, k : k + 1] = zeros
+
+    @pl.when(kind > 0)
+    def _():
+        first = pl.multiple_of((kind - 1) * half, half)
+        other = pl.multiple_of(half - first, half)
+        pairs = [(2 + k, 0, k) for k in range(4)] + [(2 + k, 1, 4 + k) for k in range(4)]
+        pairs += [(6, 0, 8), (6, 1, 9), (7, 0, 10)]
+        for unit, which, k in pairs:
+            rows = result_buf[:, unit, which * half : (which + 1) * half]
+            out_ref[:, k, pl.ds(first, half), :] = rows
+            out_ref[:, k, pl.ds(other, half), :] = jnp.zeros_like(rows)
+
+
+def add_kernel(out_in, moved_ref, out_ref):
+    out_ref[...] = out_in[...] + moved_ref[...]
 
 
 def input_parts(plus, field_count, chunk):
     cuts = [k for k in range(1, plus) if k % 4 == 0 and k * field_count % 8 == 0]
     firsts = [0] + cuts
-    rows = [k * field_count for k in firsts] + [chunk]
+    rows = [k * field_count for k in firsts] + [min(chunk, -(-plus * field_count // 8) * 8)]
     return [(k, rows[n], rows[n + 1] - rows[n]) for n, k in enumerate(firsts)]
 
 
@@ -393,7 +459,10 @@
     field_count = -(-group_fields // phys)
     plus = tables["plus"]
     count = plus * phys
-    chunk = -(-plus * field_count // 8) * 8
+    direct = row_count == 32 and phys == 8 and group_fields % 32 == 0
+    levelled = direct and width // ang == 64 and plus == 11
+    units = 9 if levelled else plus
+    chunk = -(-units * field_count // 8) * 8
     block = width // ang
     interleave = block == 64
 
@@ -414,7 +483,7 @@
     send_shape = (4, phys * chunk, 128)
     fixed = (interleave, field_count, plus)
     send_out = pltpu.HBM(send_shape, F32)
-    if row_count == 32 and phys == 8 and group_fields % 32 == 0:
+    if direct:
         groups = field_count // 4
         fields = pl.pallas_call(
             rows_kernel,
@@ -521,33 +590,61 @@
     )
     merged = samples * angle_total
 
-    parts = len(input_parts(plus, field_count, chunk))
-    out_shape = (2, plus, block, merged)
     vmem = pl.BlockSpec(memory_space=pltpu.VMEM)
     hbm = pl.BlockSpec(memory_space=pltpu.HBM)
 
-    def to_angles(got, last, turning):
+    def to_angles(got, last, turning, count, place=None):
+        shape = (2, count, block, merged)
+        parts = len(input_parts(count, field_count, chunk))
+        kernel, first = functools.partial(angle_kernel, count), []
+        out_spec, out_shape = hbm, pltpu.HBM(shape, F32)
+        if place is not None:
+            kernel, first = place_kernel, [pl.BlockSpec(memory_space=pltpu.SMEM)]
+            out_spec = vmem
+            out_shape = jax.ShapeDtypeStruct((2, plus, block, merged), F32)
+            kernel = functools.partial(kernel, field_count, samples)
+        else:
+            kernel = functools.partial(kernel, field_count, samples, turning)
         return pl.pallas_call(
-            functools.partial(angle_kernel, plus, field_count, samples, turning),
-            in_specs=[hbm, vmem, vmem, vmem if turning else hbm],
-            out_specs=hbm,
-            out_shape=pltpu.HBM(out_shape, F32),
+            kernel,
+            in_specs=first + [hbm, vmem, vmem, vmem if turning else hbm],
+            out_specs=out_spec,
+            out_shape=out_shape,
             scratch_shapes=[
                 pltpu.VMEM(got.shape, F32),
-                pltpu.VMEM((8, 128) if turning else out_shape, F32),
-                pltpu.VMEM(out_shape, F32),
-                pltpu.VMEM((plus * 2 * merged // 128, block, 128), F32),
+                pltpu.VMEM((8, 128) if turning else shape, F32),
+                pltpu.VMEM(shape, F32),
+                pltpu.VMEM((count * 2 * merged // 128, block, 128), F32),
                 pltpu.SemaphoreType.DMA((parts,)),
                 pltpu.SemaphoreType.DMA((parts,)),
-                pltpu.SemaphoreType.DMA((plus,)),
+                pltpu.SemaphoreType.DMA((count,)),
             ],
-            cost_estimate=cost(2 * plus * 2 * block * 3 * mat_hi.shape[2] * 2 * merged),
+            cost_estimate=cost(2 * count * 2 * block * 3 * mat_hi.shape[2] * 2 * merged),
             compiler_params=pltpu.CompilerParams(vmem_limit_bytes=20 * 1024 * 1024),
             name="angle",
-        )(got, mat_hi, mat_lo, last)
-
-    start_part = in_hbm(to_angles(start, turns, True))
-    return to_angles(advanced, start_part, False)
+        )(*([] if place is None else [place]), got, mat_hi, mat_lo, last)
+
+    start_part = in_hbm(to_angles(start, turns, True, units))
+    if not levelled:
+        return to_angles(advanced, start_part, False, units)
+    extra = plus - units
+    moved = lax.ppermute(
+        to_angles(advanced, start_part, False, extra), "ang", [(1, 0), (2, 3)]
+    )
+    ang_index = lax.axis_index("ang")
+    kind = jnp.where((ang_index == 0) | (ang_index == 3), 0, ang_index).astype(jnp.int32)
+    out = to_angles(advanced, start_part, False, units, kind.reshape(1))
+    spec = pl.BlockSpec((2, 1, block, merged), lambda k: (0, units + k, 0, 0))
+    return pl.pallas_call(
+        add_kernel,
+        grid=(extra,),
+        in_specs=[spec, pl.BlockSpec((2, 1, block, merged), lambda k: (0, k, 0, 0))],
+        out_specs=spec,
+        out_shape=jax.ShapeDtypeStruct(out.shape, F32),
+        input_output_aliases={0: 0},
+        compiler_params=params(20),
+        name="add",
+    )(out, moved)
 
 
 def solution(mesh):

time: 158 us -> 153 us (0.968)
  waiting for transfers between devices: 63.3 us -> 53.2 us
  Pallas kernels: 48 us -> 53.7 us
  local copies, waits for them, and re-layouts: 3.2 us -> 1.46 us
    all_to_all x2, waiting for transfers between devices: 63.3 us -> 47.1 us  [exchange(): lax.all_to_all(send, ('ang', 'phys'), split_axis=0, concat_axis=0, tiled=...]
    ppermute x0 -> x1, waiting for transfers between devices: none -> 6.12 us  [local(): lax.ppermute(to_angles(advanced, start_part, False, extra), 'ang', [(1, 0...]
    pallas_call x2 -> x4, Pallas kernels: 8.88 us -> 13.9 us  [the longest x3 12.2 us: to_angles(): pl.pallas_call(kernel, in_specs=first + [hbm, vmem, vmem, vmem if turning...]
    unnamed x24 -> x20, local copies, waits for them, and re-layouts: 3.02 us -> 1.28 us
  transfers between devices with their start and end apart: 2 -> 3, of which waited for: 2 -> 3; matrix products, arithmetic and copies ran while one was open for 0% -> 0% of each run, Pallas kernels for 23% -> 28%
where the time goes in v5:
time: 153 us
  Pallas kernels  53.7 us (35%)
  waiting for transfers between devices  53.2 us (35%)
  blocking collectives  32.4 us (21%)
  starting transfers between devices  9.58 us (6%)
  between operations  2.14 us (1%)
    all_to_all x2, waiting for transfers between devices, exchange(): lax.all_to_all(send, ('ang', 'phys'), split_axis=0, concat_axis=0, tiled=...  47.1 us
    pallas_call x1, Pallas kernels, local(): pl.pallas_call(functools.partial(advance_kernel, *fixed), grid=(field_cou...  32.5 us
    all_to_all x1, blocking collectives, local(): lax.all_to_all(fields, 'phys', split_axis=0, concat_axis=0, tiled=True)  32.4 us
    pallas_call x3, Pallas kernels, to_angles(): pl.pallas_call(kernel, in_specs=first + [hbm, vmem, vmem, vmem if turning...  12.2 us
    all_to_all x2, starting transfers between devices, exchange(): lax.all_to_all(send, ('ang', 'phys'), split_axis=0, concat_axis=0, tiled=...  8.29 us
    ppermute x1, waiting for transfers between devices, local(): lax.ppermute(to_angles(advanced, start_part, False, extra), 'ang', [(1, 0...  6.12 us
    pallas_call x1, Pallas kernels, local(): pl.pallas_call(rows_kernel, grid=(group_fields // 32,), in_specs=[pl.Bloc...  3.81 us
    pallas_call x1, Pallas kernels, local(): pl.pallas_call(functools.partial(columns_kernel, *fixed), grid=(groups,),...  3.53 us
  transfers between devices with their start and end apart: 3, of which 3 were waited for; matrix products, arithmetic and copies ran while one was open for 0% of the time, Pallas kernels for 28%

profile of v5, /device:TPU:0, one launch (start us, length us, event | category | flops | bytes accessed | tf_op | source)
XLA Modules:
  0.0 152.6 jit_solution(8168935433826117218)
XLA Ops:
  0.0 3.8 %rows.1 = f32[24,176,128]{2,1,0:T(8,128)S(1)} custom-call(f32[96,32,256]{2,1,0:T(8,128)} %bitcast.14, bf16[176,256]{1,0:T(8,128)(2,1)} %constant.52.clone.fx_hi, bf16[176,256]{1,0:T(8,128)(2,1)} %constant.53.clone.fx_lo), custom_call_target="tpu_custom_call" | custom-call | tf_op jit(solution)/shard_map/rows/pallas_call | solution.py:488
  3.8 0.0 copy-start.3
  3.8 0.0 copy-start.4
  3.8 0.0 copy-start.5
  3.9 0.0 copy-start.6
  3.9 32.4 %all_to_all.15 = f32[8,528,128]{2,1,0:T(8,128)S(1)} all-to-all(f32[8,528,128]{2,1,0:T(8,128)S(1)} %bitcast.12), channel_id=1, replica_groups=mesh['phys'=8,'ang'=4] {'phys'}, dimensions={0} | all-to-all | bytes 4325376 | tf_op jit(solution)/shard_map/all_to_all | solution.py:499
  36.3 0.0 copy-done.3
  36.3 0.0 copy-done.4
  36.3 0.0 copy-done.5
  36.3 0.0 copy-done.6
  36.3 3.5 %columns.1 = f32[4,896,128]{2,1,0:T(8,128)S(1)} custom-call(f32[8,3,176,128]{3,2,1,0:T(8,128)S(1)} %bitcast.10, bf16[256,256]{1,0:T(8,128)(2,1)S(1)} %copy-done.3, bf16[256,256]{1,0:T(8,128)(2,1)S(1)} %copy-done.4, bf16[256,256]{1,0:T(8,128)(2,1)S(1)} %copy-done.5, bf16[256,256]{1,0:T(8,128)(2,1)S(1)} %copy-done.6), custom_call_target="tpu_custom_call" | custom-call | tf_op jit(solution)/shard_map/columns/pallas_call | solution.py:502
  39.8 0.0 copy-start
  39.8 1.2 copy-done
  41.1 0.0 copy-start.7
  41.1 0.0 copy-start.8
  41.1 4.1 %all-to-all-start.1 = ((f32[32,112,128]{2,1,0:T(8,128)}), f32[32,112,128]{2,1,0:T(8,128)}, u32[]{:S(2)}, u32[]{:S(2)}) async-start(f32[32,112,128]{2,1,0:T(8,128)} %bitcast.13), calls=%async_computation.1 | async-start | bytes 3670016 | tf_op jit(solution)/shard_map/all_to_all | solution.py:543
  46.5 0.1 cosine_multiply_fusion.force_ref
  46.5 0.0 copy-done.7
  46.5 0.0 copy-done.8
  46.5 32.5 %advance.1 = f32[4,896,128]{2,1,0:T(8,128)} custom-call(f32[1]{0:T(128)S(6)} %copy.27.dt_ref, f32[8,3,176,128]{3,2,1,0:T(8,128)S(1)} %bitcast.11, f32[1,256]{1,0:T(1,128)S(1)} %cosine_multiply_fusion.force_ref, f32[88,1]{1,0:T(8,128)S(1)} %copy-done.7, f32[1,512]{1,0:T(1,128)S(1)} %copy-done.8, bf16[176,256]{1,0:T(8,128)(2,1)} %constant.52.clone.fx_hi, ...), custom_call_target="tpu_custom_call" | custom-call | flops 9965666304 | bytes 8388608 | tf_op jit(solution)/shard_map/advance/pallas_call | solution.py:549
  79.0 0.0 copy-start.9
  79.0 0.0 copy-start.1
  79.0 0.0 copy-start.2
  79.0 9.3 %all-to-all-done.1.got_hbm = f32[32,112,128]{2,1,0:T(8,128)} async-done(((f32[32,112,128]{2,1,0:T(8,128)}), f32[32,112,128]{2,1,0:T(8,128)}, u32[]{:S(2)}, u32[]{:S(2)}) %all-to-all-start.1) | async-done | bytes 1835040 | tf_op jit(solution)/shard_map/all_to_all | solution.py:543
  88.4 4.2 %all-to-all-start.2 = ((f32[32,112,128]{2,1,0:T(8,128)}), f32[32,112,128]{2,1,0:T(8,128)S(1)}, u32[]{:S(2)}, u32[]{:S(2)}) async-start(f32[32,112,128]{2,1,0:T(8,128)} %bitcast.15), calls=%async_computation.2 | async-start | bytes 3670016 | tf_op jit(solution)/shard_map/all_to_all | solution.py:543
  93.2 0.0 copy-done.9
  93.3 0.1 stack_tile.6
  93.4 0.1 stack_tile.7
  93.5 0.0 copy-done.1
  93.5 0.0 copy-done.2
  93.5 4.4 %angle.3.last_ref = f32[2,9,64,384]{3,2,1,0:T(8,128)} custom-call(f32[32,112,128]{2,1,0:T(8,128)} %all-to-all-done.1.got_hbm, bf16[1,192,96]{2,1,0:T(8,128)(2,1)S(1)} %copy-done.1, bf16[1,192,96]{2,1,0:T(8,128)(2,1)S(1)} %copy-done.2, f32[2,384]{1,0:T(2,128)S(1)} %pad_maximum_fusion.last_ref), custom_call_target="tpu_custom_call" | custom-call | flops 509607936 | bytes 8388608 | tf_op jit(solution)/shard_map/angle/pallas_call | solution.py:608
  98.0 37.8 %all-to-all-done.2.got_hbm = f32[32,112,128]{2,1,0:T(8,128)S(1)} async-done(((f32[32,112,128]{2,1,0:T(8,128)}), f32[32,112,128]{2,1,0:T(8,128)S(1)}, u32[]{:S(2)}, u32[]{:S(2)}) %all-to-all-start.2) | async-done | bytes 1835040 | tf_op jit(solution)/shard_map/all_to_all | solution.py:543
  135.7 2.4 %angle.5 = f32[2,2,64,384]{3,2,1,0:T(8,128)} custom-call(f32[32,112,128]{2,1,0:T(8,128)S(1)} %all-to-all-done.2.got_hbm, bf16[1,192,96]{2,1,0:T(8,128)(2,1)S(1)} %copy-done.1, bf16[1,192,96]{2,1,0:T(8,128)(2,1)S(1)} %copy-done.2, f32[2,9,64,384]{3,2,1,0:T(8,128)} %angle.3.last_ref), custom_call_target="tpu_custom_call" | custom-call | flops 113246208 | bytes 8388608 | tf_op jit(solution)/shard_map/angle/pallas_call | solution.py:608
  138.1 1.3 collective-permute-start
  139.4 5.3 %angle.4.out_in = f32[2,11,64,384]{3,2,1,0:T(8,128)} custom-call(s32[1]{0:T(128)} %bitcast.kind_ref, f32[32,112,128]{2,1,0:T(8,128)S(1)} %all-to-all-done.2.got_hbm, bf16[1,192,96]{2,1,0:T(8,128)(2,1)S(1)} %copy-done.1, bf16[1,192,96]{2,1,0:T(8,128)(2,1)S(1)} %copy-done.2, f32[2,9,64,384]{3,2,1,0:T(8,128)} %angle.3.last_ref), custom_call_target="tpu_custom_call" | custom-call | flops 509607936 | bytes 8388608 | tf_op jit(solution)/shard_map/angle/pallas_call | solution.py:608
  144.8 6.1 %collective-permute-done.moved_ref = f32[2,2,64,384]{3,2,1,0:T(8,128)S(1)} collective-permute-done((f32[2,2,64,384]{3,2,1,0:T(8,128)}, f32[2,2,64,384]{3,2,1,0:T(8,128)S(1)}, u32[]{:S(2)}, u32[]{:S(2)}) %collective-permute-start) | collective-permute-done | bytes 393248 | tf_op jit(solution)/shard_map/ppermute | solution.py:631
  150.9 1.7 %add.1 = f32[2,11,64,384]{3,2,1,0:T(8,128)} custom-call(f32[2,11,64,384]{3,2,1,0:T(8,128)} %angle.4.out_in, f32[2,2,64,384]{3,2,1,0:T(8,128)S(1)} %collective-permute-done.moved_ref), custom_call_target="tpu_custom_call", output_to_operand_aliasing={{}: (0, {})} | custom-call | tf_op jit(solution)/shard_map/add/pallas_call | solution.py:638
  (4 shorter events, 0.1 us)
Async XLA Ops:
  3.8 32.5 %copy-start.3 = (bf16[256,256]{1,0:T(8,128)(2,1)S(1)}, bf16[256,256]{1,0:T(8,128)(2,1)}, u32[]{:S(2)}) copy-start(bf16[256,256]{1,0:T(8,128)(2,1)} %constant.54.clone.e_hi) | copy-start | bytes 393220
  3.8 32.4 %copy-start.4 = (bf16[256,256]{1,0:T(8,128)(2,1)S(1)}, bf16[256,256]{1,0:T(8,128)(2,1)}, u32[]{:S(2)}) copy-start(bf16[256,256]{1,0:T(8,128)(2,1)} %constant.55.clone.e_lo) | copy-start | bytes 393220
  3.8 32.4 %copy-start.5 = (bf16[256,256]{1,0:T(8,128)(2,1)S(1)}, bf16[256,256]{1,0:T(8,128)(2,1)}, u32[]{:S(2)}) copy-start(bf16[256,256]{1,0:T(8,128)(2,1)} %constant.56.clone.o_hi) | copy-start | bytes 393220
  3.9 32.4 %copy-start.6 = (bf16[256,256]{1,0:T(8,128)(2,1)S(1)}, bf16[256,256]{1,0:T(8,128)(2,1)}, u32[]{:S(2)}) copy-start(bf16[256,256]{1,0:T(8,128)(2,1)} %constant.57.clone.o_lo) | copy-start | bytes 393220
  39.8 1.2 copy-start
  41.1 5.4 %copy-start.7 = (f32[88,1]{1,0:T(8,128)S(1)}, f32[88,1]{1,0:T(8,128)}, u32[]{:S(2)}) copy-start(f32[88,1]{1,0:T(8,128)} %constant.66.clone.wave_x_ref) | copy-start | bytes 1060
  41.1 5.5 %copy-start.8 = (f32[1,512]{1,0:T(1,128)S(1)}, f32[1,512]{1,0:T(1,128)}, u32[]{:S(2)}) copy-start(f32[1,512]{1,0:T(1,128)} %constant.67.clone.wave_y_ref) | copy-start | bytes 6148
  41.1 47.3 %all-to-all-start.1 = ((f32[32,112,128]{2,1,0:T(8,128)}), f32[32,112,128]{2,1,0:T(8,128)}, u32[]{:S(2)}, u32[]{:S(2)}) async-start(f32[32,112,128]{2,1,0:T(8,128)} %bitcast.13), calls=%async_computation.1 | async-start | bytes 3670016 | tf_op jit(solution)/shard_map/all_to_all | solution.py:543
  79.0 14.2 %copy-start.9 = (f32[96]{0:T(128)S(1)}, f32[96]{0:T(128)}, u32[]{:S(2)}) copy-start(f32[96]{0:T(128)} %constant.70.clone) | copy-start | bytes 1156
  79.0 14.5 %copy-start.1 = (bf16[1,192,96]{2,1,0:T(8,128)(2,1)S(1)}, bf16[1,192,96]{2,1,0:T(8,128)(2,1)}, u32[]{:S(2)}) copy-start(bf16[1,192,96]{2,1,0:T(8,128)(2,1)} %constant.68.clone.mat_hi) | copy-start | bytes 110596
  79.0 14.5 %copy-start.2 = (bf16[1,192,96]{2,1,0:T(8,128)(2,1)S(1)}, bf16[1,192,96]{2,1,0:T(8,128)(2,1)}, u32[]{:S(2)}) copy-start(bf16[1,192,96]{2,1,0:T(8,128)(2,1)} %constant.69.clone.mat_lo) | copy-start | bytes 110596
  88.4 47.3 %all-to-all-start.2 = ((f32[32,112,128]{2,1,0:T(8,128)}), f32[32,112,128]{2,1,0:T(8,128)S(1)}, u32[]{:S(2)}, u32[]{:S(2)}) async-start(f32[32,112,128]{2,1,0:T(8,128)} %bitcast.15), calls=%async_computation.2 | async-start | bytes 3670016 | tf_op jit(solution)/shard_map/all_to_all | solution.py:543
  138.1 12.8 %collective-permute-start = (f32[2,2,64,384]{3,2,1,0:T(8,128)}, f32[2,2,64,384]{3,2,1,0:T(8,128)S(1)}, u32[]{:S(2)}, u32[]{:S(2)}) collective-permute-start(f32[2,2,64,384]{3,2,1,0:T(8,128)} %angle.5), channel_id=1, source_target_pairs={{1,0},{2,3},{5,4},{6,7},{9,8},{10,11},{13,12},{14,15},{17,16},{18,... | collective-permute-start | bytes 1179656 | tf_op jit(solution)/shard_map/ppermute | solution.py:631

commit v6 on v5

--- a/solution.py
+++ b/solution.py
@@ -338,7 +338,9 @@
     loads = []
     for n, (first_k, first, size) in enumerate(parts):
         place = (slice(None), slice(first, first + size))
-        copies = [pltpu.make_async_copy(got_hbm.at[place], got_ref.at[place], got_sem.at[n])]
+        copies = []
+        if turning:
+            copies = [pltpu.make_async_copy(got_hbm.at[place], got_ref.at[place], got_sem.at[n])]
         if not turning:
             last_k = parts[n + 1][0] if n + 1 < len(parts) else plus
             place = (slice(None), slice(first_k, last_k))
@@ -348,7 +350,7 @@
         for copy in copies:
             copy.start()
         loads.append((first_k, copies))
-    flat = got_ref.reshape(sources * chunk, lanes)
+    flat = (got_ref if turning else got_hbm).reshape(sources * chunk, lanes)
     stores = []
     for k in range(plus):
         for first_k, copies in loads:
@@ -390,29 +392,22 @@
             place = (k * 2 + part) * blocks
             joined = jnp.concatenate([rows_ref[place + b] for b in range(blocks)], axis=1)
             out_buf[part, k] = joined if turning else joined + last_buf[part, k]
-        if out_hbm is not None:
-            copy = pltpu.make_async_copy(out_buf.at[:, k], out_hbm.at[:, k], out_sem.at[k])
-            copy.start()
-            stores.append(copy)
+        copy = pltpu.make_async_copy(out_buf.at[:, k], out_hbm.at[:, k], out_sem.at[k])
+        copy.start()
+        stores.append(copy)
     for copy in stores:
         copy.wait()
 
 
-def place_kernel(field_count, samples, kind_ref, got_hbm, mat_hi, mat_lo, last_ref, out_ref, *scratch):
+def place_kernel(kind_ref, units_ref, moved_ref, out_ref):
     kind = kind_ref[0]
-    result_buf = scratch[2]
-    units = result_buf.shape[1]
-    angle_kernel(
-        units, field_count, samples, False, got_hbm, mat_hi, mat_lo, last_ref, None, *scratch
-    )
+    units = units_ref.shape[1]
     half = out_ref.shape[2] // 2
-    zeros = jnp.zeros((2, 1) + out_ref.shape[2:], F32)
 
     @pl.when(kind == 0)
     def _():
-        out_ref[:, :units] = result_buf[...]
-        for k in range(units, out_ref.shape[1]):
-            out_ref[:, k : k + 1] = zeros
+        out_ref[:, :units] = units_ref[...]
+        out_ref[:, units:] = moved_ref[...]
 
     @pl.when(kind > 0)
     def _():
@@ -421,13 +416,9 @@
         pairs = [(2 + k, 0, k) for k in range(4)] + [(2 + k, 1, 4 + k) for k in range(4)]
         pairs += [(6, 0, 8), (6, 1, 9), (7, 0, 10)]
         for unit, which, k in pairs:
-            rows = result_buf[:, unit, which * half : (which + 1) * half]
+            rows = units_ref[:, unit, which * half : (which + 1) * half]
             out_ref[:, k, pl.ds(first, half), :] = rows
             out_ref[:, k, pl.ds(other, half), :] = jnp.zeros_like(rows)
-
-
-def add_kernel(out_in, moved_ref, out_ref):
-    out_ref[...] = out_in[...] + moved_ref[...]
 
 
 def input_parts(plus, field_count, chunk):
@@ -462,7 +453,8 @@
     direct = row_count == 32 and phys == 8 and group_fields % 32 == 0
     levelled = direct and width // ang == 64 and plus == 11
     units = 9 if levelled else plus
-    chunk = -(-units * field_count // 8) * 8
+    start_chunk = -(-units * field_count // 8) * 8
+    chunk = -(-plus * field_count // 8) * 8
     block = width // ang
     interleave = block == 64
 
@@ -481,16 +473,18 @@
         )
 
     send_shape = (4, phys * chunk, 128)
+    start_shape = (4, phys * start_chunk, 128)
     fixed = (interleave, field_count, plus)
     send_out = pltpu.HBM(send_shape, F32)
     if direct:
         groups = field_count // 4
+        step_fields = 48 if group_fields % 48 == 0 else 32
         fields = pl.pallas_call(
             rows_kernel,
-            grid=(group_fields // 32,),
-            in_specs=[pl.BlockSpec((32, row_count, width), lambda n: (n, 0, 0))]
+            grid=(group_fields // step_fields,),
+            in_specs=[pl.BlockSpec((step_fields, row_count, width), lambda n: (n, 0, 0))]
             + [whole_spec(t.shape) for t in fwd[:2]],
-            out_specs=pl.BlockSpec((8, 2 * count, 128), lambda n: (n, 0, 0)),
+            out_specs=pl.BlockSpec((step_fields // 4, 2 * count, 128), lambda n: (n, 0, 0)),
             out_shape=jax.ShapeDtypeStruct((group_fields // 4, 2 * count, 128), F32),
             compiler_params=params(20),
             name="rows",
@@ -503,8 +497,8 @@
             functools.partial(columns_kernel, *fixed),
             grid=(groups,),
             in_specs=[spectra_spec] + [whole_spec(t.shape) for t in fwd[2:]],
-            out_specs=whole_spec(send_shape),
-            out_shape=jax.ShapeDtypeStruct(send_shape, F32),
+            out_specs=whole_spec(start_shape),
+            out_shape=jax.ShapeDtypeStruct(start_shape, F32),
             compiler_params=params(20),
             name="columns",
         )(spectra, *fwd[2:])
@@ -534,7 +528,7 @@
         stack = 1
 
     def exchange(send):
-        rows = chunk
+        rows = send.shape[1] // phys
         if interleave:
             send = send.reshape(ang * phys, rows, 128)
         else:
@@ -593,25 +587,16 @@
     vmem = pl.BlockSpec(memory_space=pltpu.VMEM)
     hbm = pl.BlockSpec(memory_space=pltpu.HBM)
 
-    def to_angles(got, last, turning, count, place=None):
+    def to_angles(got, last, turning, count):
         shape = (2, count, block, merged)
-        parts = len(input_parts(count, field_count, chunk))
-        kernel, first = functools.partial(angle_kernel, count), []
-        out_spec, out_shape = hbm, pltpu.HBM(shape, F32)
-        if place is not None:
-            kernel, first = place_kernel, [pl.BlockSpec(memory_space=pltpu.SMEM)]
-            out_spec = vmem
-            out_shape = jax.ShapeDtypeStruct((2, plus, block, merged), F32)
-            kernel = functools.partial(kernel, field_count, samples)
-        else:
-            kernel = functools.partial(kernel, field_count, samples, turning)
+        parts = len(input_parts(count, field_count, got.shape[1]))
         return pl.pallas_call(
-            kernel,
-            in_specs=first + [hbm, vmem, vmem, vmem if turning else hbm],
-            out_specs=out_spec,
-            out_shape=out_shape,
+            functools.partial(angle_kernel, count, field_count, samples, turning),
+            in_specs=[hbm if turning else vmem, vmem, vmem, vmem if turning else hbm],
+            out_specs=hbm,
+            out_shape=pltpu.HBM(shape, F32),
             scratch_shapes=[
-                pltpu.VMEM(got.shape, F32),
+                pltpu.VMEM(got.shape if turning else (8, 128), F32),
                 pltpu.VMEM((8, 128) if turning else shape, F32),
                 pltpu.VMEM(shape, F32),
                 pltpu.VMEM((count * 2 * merged // 128, block, 128), F32),
@@ -622,29 +607,22 @@
             cost_estimate=cost(2 * count * 2 * block * 3 * mat_hi.shape[2] * 2 * merged),
             compiler_params=pltpu.CompilerParams(vmem_limit_bytes=20 * 1024 * 1024),
             name="angle",
-        )(*([] if place is None else [place]), got, mat_hi, mat_lo, last)
-
-    start_part = in_hbm(to_angles(start, turns, True, units))
-    if not levelled:
-        return to_angles(advanced, start_part, False, units)
-    extra = plus - units
-    moved = lax.ppermute(
-        to_angles(advanced, start_part, False, extra), "ang", [(1, 0), (2, 3)]
-    )
-    ang_index = lax.axis_index("ang")
-    kind = jnp.where((ang_index == 0) | (ang_index == 3), 0, ang_index).astype(jnp.int32)
-    out = to_angles(advanced, start_part, False, units, kind.reshape(1))
-    spec = pl.BlockSpec((2, 1, block, merged), lambda k: (0, units + k, 0, 0))
-    return pl.pallas_call(
-        add_kernel,
-        grid=(extra,),
-        in_specs=[spec, pl.BlockSpec((2, 1, block, merged), lambda k: (0, k, 0, 0))],
-        out_specs=spec,
-        out_shape=jax.ShapeDtypeStruct(out.shape, F32),
-        input_output_aliases={0: 0},
-        compiler_params=params(20),
-        name="add",
-    )(out, moved)
+        )(got, mat_hi, mat_lo, last)
+
+    start_part = to_angles(start, turns, True, units)
+    if levelled:
+        moved = lax.ppermute(start_part[:, : plus - units], "ang", [(1, 0), (2, 3)])
+        ang_index = lax.axis_index("ang")
+        kind = jnp.where((ang_index == 0) | (ang_index == 3), 0, ang_index).astype(jnp.int32)
+        start_part = pl.pallas_call(
+            place_kernel,
+            in_specs=[pl.BlockSpec(memory_space=pltpu.SMEM), vmem, vmem],
+            out_specs=vmem,
+            out_shape=jax.ShapeDtypeStruct((2, plus, block, merged), F32),
+            compiler_params=pltpu.CompilerParams(vmem_limit_bytes=20 * 1024 * 1024),
+            name="place",
+        )(kind.reshape(1), start_part, moved)
+    return to_angles(advanced, in_hbm(start_part), False, plus)
 
 
 def solution(mesh):

time: 153 us -> 149 us (0.974)
  Pallas kernels: 53.7 us -> 48.5 us
  local copies, waits for them, and re-layouts: 1.46 us -> 5.26 us
  waiting for transfers between devices: 53.2 us -> 50.5 us
    all_to_all x2, waiting for transfers between devices: 47.1 us -> 17.7 us  [exchange(): lax.all_to_all(send, ('ang', 'phys'), split_axis=0, concat_axis=0, tiled=...]
    ppermute x1, waiting for transfers between devices: 6.12 us -> 32.7 us  [local(): moved = lax.ppermute(start_part[:, :plus - units], 'ang', [(1, 0), (2, 3)])]
    pallas_call x5 -> x4, Pallas kernels: 17.7 us -> 12.7 us  [the longest x2 9.25 us: to_angles(): pl.pallas_call(functools.partial(angle_kernel, count, field_count, sample...]
    unnamed x20 -> x24, local copies, waits for them, and re-layouts: 1.28 us -> 4.06 us
  transfers between devices with their start and end apart: 3 -> 3, of which waited for: 3 -> 3; matrix products, arithmetic and copies ran while one was open for 0% -> 1% of each run, Pallas kernels for 28% -> 25%
where the time goes in v6:
time: 149 us
  waiting for transfers between devices  50.5 us (34%)
  Pallas kernels  48.5 us (33%)
  blocking collectives  32.4 us (22%)
  starting transfers between devices  9.58 us (6%)
  local copies, waits for them, and re-layouts  5.26 us (4%)
  between operations  2.3 us (2%)
    ppermute x1, waiting for transfers between devices, local(): moved = lax.ppermute(start_part[:, :plus - units], 'ang', [(1, 0), (2, 3)])  32.7 us
    all_to_all x1, blocking collectives, local(): lax.all_to_all(fields, 'phys', split_axis=0, concat_axis=0, tiled=True)  32.4 us
    pallas_call x1, Pallas kernels, local(): pl.pallas_call(functools.partial(advance_kernel, *fixed), grid=(field_cou...  32.3 us
    all_to_all x2, waiting for transfers between devices, exchange(): lax.all_to_all(send, ('ang', 'phys'), split_axis=0, concat_axis=0, tiled=...  17.7 us
    pallas_call x2, Pallas kernels, to_angles(): pl.pallas_call(functools.partial(angle_kernel, count, field_count, sample...  9.25 us
    all_to_all x2, starting transfers between devices, exchange(): lax.all_to_all(send, ('ang', 'phys'), split_axis=0, concat_axis=0, tiled=...  8.29 us
    unnamed x24, local copies, waits for them, and re-layouts  4.06 us
    pallas_call x1, Pallas kernels, local(): pl.pallas_call(functools.partial(columns_kernel, *fixed), grid=(groups,),...  3.54 us
  transfers between devices with their start and end apart: 3, of which 3 were waited for; matrix products, arithmetic and copies ran while one was open for 1% of the time, Pallas kernels for 25%

profile of v6, /device:TPU:0, one launch (start us, length us, event | category | flops | bytes accessed | tf_op | source)
XLA Modules:
  0.0 148.6 jit_solution(18150596970658724602)
XLA Ops:
  0.0 3.3 %rows.1 = f32[24,176,128]{2,1,0:T(8,128)S(1)} custom-call(f32[96,32,256]{2,1,0:T(8,128)} %bitcast.14, bf16[176,256]{1,0:T(8,128)(2,1)} %constant.52.clone.fx_hi, bf16[176,256]{1,0:T(8,128)(2,1)} %constant.53.clone.fx_lo), custom_call_target="tpu_custom_call" | custom-call | tf_op jit(solution)/shard_map/rows/pallas_call | solution.py:482
  3.3 0.0 copy-start.5
  3.3 0.0 copy-start.6
  3.3 0.0 copy-start.7
  3.3 0.0 copy-start.8
  3.3 32.4 %all_to_all.15 = f32[8,528,128]{2,1,0:T(8,128)S(1)} all-to-all(f32[8,528,128]{2,1,0:T(8,128)S(1)} %bitcast.12), channel_id=1, replica_groups=mesh['phys'=8,'ang'=4] {'phys'}, dimensions={0} | all-to-all | bytes 4325376 | tf_op jit(solution)/shard_map/all_to_all | solution.py:493
  35.7 0.0 copy-done.5
  35.7 0.0 copy-done.6
  35.7 0.0 copy-done.7
  35.7 0.0 copy-done.8
  35.8 3.5 %columns.1 = f32[4,896,128]{2,1,0:T(8,128)S(1)} custom-call(f32[8,3,176,128]{3,2,1,0:T(8,128)S(1)} %bitcast.10, bf16[256,256]{1,0:T(8,128)(2,1)S(1)} %copy-done.8, bf16[256,256]{1,0:T(8,128)(2,1)S(1)} %copy-done.7, bf16[256,256]{1,0:T(8,128)(2,1)S(1)} %copy-done.6, bf16[256,256]{1,0:T(8,128)(2,1)S(1)} %copy-done.5), custom_call_target="tpu_custom_call" | custom-call | tf_op jit(solution)/shard_map/columns/pallas_call | solution.py:496
  39.3 0.0 copy-start.2
  39.3 1.2 copy-done.2
  40.5 0.0 copy-start.9
  40.5 0.0 copy-start.10
  40.5 4.1 %all-to-all-start.1 = ((f32[32,112,128]{2,1,0:T(8,128)}), f32[32,112,128]{2,1,0:T(8,128)}, u32[]{:S(2)}, u32[]{:S(2)}) async-start(f32[32,112,128]{2,1,0:T(8,128)} %bitcast.13), calls=%async_computation.1 | async-start | bytes 3670016 | tf_op jit(solution)/shard_map/all_to_all | solution.py:537
  45.9 0.1 cosine_multiply_fusion.force_ref
  46.0 0.0 copy-done.9
  46.0 0.0 copy-done.10
  46.0 32.3 %advance.1 = f32[4,1088,128]{2,1,0:T(8,128)} custom-call(f32[1]{0:T(128)S(6)} %copy.25.dt_ref, f32[8,3,176,128]{3,2,1,0:T(8,128)S(1)} %bitcast.11, f32[1,256]{1,0:T(1,128)S(1)} %cosine_multiply_fusion.force_ref, f32[88,1]{1,0:T(8,128)S(1)} %copy-done.9, f32[1,512]{1,0:T(1,128)S(1)} %copy-done.10, bf16[176,256]{1,0:T(8,128)(2,1)} %constant.52.clone.fx_hi, ...), custom_call_target="tpu_custom_call" | custom-call | flops 9965666304 | bytes 8388608 | tf_op jit(solution)/shard_map/advance/pallas_call | solution.py:543
  78.3 9.5 %all-to-all-done.1.got_hbm = f32[32,112,128]{2,1,0:T(8,128)} async-done(((f32[32,112,128]{2,1,0:T(8,128)}), f32[32,112,128]{2,1,0:T(8,128)}, u32[]{:S(2)}, u32[]{:S(2)}) %all-to-all-start.1) | async-done | bytes 1835040 | tf_op jit(solution)/shard_map/all_to_all | solution.py:537
  87.8 0.0 copy-start.11
  87.8 0.0 copy-start.3
  87.8 0.0 copy-start.4
  87.8 4.2 %all-to-all-start.2 = ((f32[32,136,128]{2,1,0:T(8,128)}), f32[32,136,128]{2,1,0:T(8,128)S(1)}, u32[]{:S(2)}, u32[]{:S(2)}) async-start(f32[32,136,128]{2,1,0:T(8,128)} %bitcast.15), calls=%async_computation.2 | async-start | bytes 4456448 | tf_op jit(solution)/shard_map/all_to_all | solution.py:537
  92.7 0.0 copy-done.11
  92.8 0.1 stack_tile.6
  92.8 0.1 stack_tile.7
  93.0 0.0 copy-done.3
  93.0 0.0 copy-done.4
  93.0 4.4 %angle.2.units_ref = f32[2,9,64,384]{3,2,1,0:T(8,128)} custom-call(f32[32,112,128]{2,1,0:T(8,128)} %all-to-all-done.1.got_hbm, bf16[1,192,96]{2,1,0:T(8,128)(2,1)S(1)} %copy-done.4, bf16[1,192,96]{2,1,0:T(8,128)(2,1)S(1)} %copy-done.3, f32[2,384]{1,0:T(2,128)S(1)} %pad_maximum_fusion.last_ref), custom_call_target="tpu_custom_call" | custom-call | flops 509607936 | bytes 8388608 | tf_op jit(solution)/shard_map/angle/pallas_call | solution.py:593
  97.4 1.0 slice.4
  98.4 1.3 collective-permute-start
  99.7 32.7 %collective-permute-done.moved_ref = f32[2,2,64,384]{3,2,1,0:T(8,128)S(1)} collective-permute-done((f32[2,2,64,384]{3,2,1,0:T(8,128)S(1)}, f32[2,2,64,384]{3,2,1,0:T(8,128)S(1)}, u32[]{:S(2)}, u32[]{:S(2)}) %collective-permute-start) | collective-permute-done | bytes 393248 | tf_op jit(solution)/shard_map/ppermute | solution.py:614
  132.5 0.0 copy-start
  132.5 1.5 copy-done
  134.0 0.1 place.1.last_ref
  134.1 0.0 copy-start.1
  134.1 1.3 copy-done.1
  135.4 8.2 %all-to-all-done.2.got_hbm = f32[32,136,128]{2,1,0:T(8,128)S(1)} async-done(((f32[32,136,128]{2,1,0:T(8,128)}), f32[32,136,128]{2,1,0:T(8,128)S(1)}, u32[]{:S(2)}, u32[]{:S(2)}) %all-to-all-start.2) | async-done | bytes 2228256 | tf_op jit(solution)/shard_map/all_to_all | solution.py:537
  143.6 4.8 %angle.3 = f32[2,11,64,384]{3,2,1,0:T(8,128)} custom-call(f32[32,136,128]{2,1,0:T(8,128)S(1)} %all-to-all-done.2.got_hbm, bf16[1,192,96]{2,1,0:T(8,128)(2,1)S(1)} %copy-done.4, bf16[1,192,96]{2,1,0:T(8,128)(2,1)S(1)} %copy-done.3, f32[2,11,64,384]{3,2,1,0:T(8,128)} %copy-done.1), custom_call_target="tpu_custom_call" | custom-call | flops 622854144 | bytes 8388608 | tf_op jit(solution)/shard_map/angle/pallas_call | solution.py:593
  (4 shorter events, 0.1 us)
Async XLA Ops:
  3.3 32.5 %copy-start.5 = (bf16[256,256]{1,0:T(8,128)(2,1)S(1)}, bf16[256,256]{1,0:T(8,128)(2,1)}, u32[]{:S(2)}) copy-start(bf16[256,256]{1,0:T(8,128)(2,1)} %constant.57.clone.o_lo) | copy-start | bytes 393220
  3.3 32.4 %copy-start.6 = (bf16[256,256]{1,0:T(8,128)(2,1)S(1)}, bf16[256,256]{1,0:T(8,128)(2,1)}, u32[]{:S(2)}) copy-start(bf16[256,256]{1,0:T(8,128)(2,1)} %constant.56.clone.o_hi) | copy-start | bytes 393220
  3.3 32.4 %copy-start.7 = (bf16[256,256]{1,0:T(8,128)(2,1)S(1)}, bf16[256,256]{1,0:T(8,128)(2,1)}, u32[]{:S(2)}) copy-start(bf16[256,256]{1,0:T(8,128)(2,1)} %constant.55.clone.e_lo) | copy-start | bytes 393220
  3.3 32.4 %copy-start.8 = (bf16[256,256]{1,0:T(8,128)(2,1)S(1)}, bf16[256,256]{1,0:T(8,128)(2,1)}, u32[]{:S(2)}) copy-start(bf16[256,256]{1,0:T(8,128)(2,1)} %constant.54.clone.e_hi) | copy-start | bytes 393220
  39.3 1.2 copy-start.2
  40.5 5.5 %copy-start.9 = (f32[88,1]{1,0:T(8,128)S(1)}, f32[88,1]{1,0:T(8,128)}, u32[]{:S(2)}) copy-start(f32[88,1]{1,0:T(8,128)} %constant.66.clone.wave_x_ref) | copy-start | bytes 1060
  40.5 5.5 %copy-start.10 = (f32[1,512]{1,0:T(1,128)S(1)}, f32[1,512]{1,0:T(1,128)}, u32[]{:S(2)}) copy-start(f32[1,512]{1,0:T(1,128)} %constant.67.clone.wave_y_ref) | copy-start | bytes 6148
  40.5 47.3 %all-to-all-start.1 = ((f32[32,112,128]{2,1,0:T(8,128)}), f32[32,112,128]{2,1,0:T(8,128)}, u32[]{:S(2)}, u32[]{:S(2)}) async-start(f32[32,112,128]{2,1,0:T(8,128)} %bitcast.13), calls=%async_computation.1 | async-start | bytes 3670016 | tf_op jit(solution)/shard_map/all_to_all | solution.py:537
  87.8 4.9 %copy-start.11 = (f32[96]{0:T(128)S(1)}, f32[96]{0:T(128)}, u32[]{:S(2)}) copy-start(f32[96]{0:T(128)} %constant.70.clone) | copy-start | bytes 1156
  87.8 5.1 %copy-start.3 = (bf16[1,192,96]{2,1,0:T(8,128)(2,1)S(1)}, bf16[1,192,96]{2,1,0:T(8,128)(2,1)}, u32[]{:S(2)}) copy-start(bf16[1,192,96]{2,1,0:T(8,128)(2,1)} %constant.69.clone.mat_lo) | copy-start | bytes 110596
  87.8 5.1 %copy-start.4 = (bf16[1,192,96]{2,1,0:T(8,128)(2,1)S(1)}, bf16[1,192,96]{2,1,0:T(8,128)(2,1)}, u32[]{:S(2)}) copy-start(bf16[1,192,96]{2,1,0:T(8,128)(2,1)} %constant.68.clone.mat_hi) | copy-start | bytes 110596
  87.8 55.8 %all-to-all-start.2 = ((f32[32,136,128]{2,1,0:T(8,128)}), f32[32,136,128]{2,1,0:T(8,128)S(1)}, u32[]{:S(2)}, u32[]{:S(2)}) async-start(f32[32,136,128]{2,1,0:T(8,128)} %bitcast.15), calls=%async_computation.2 | async-start | bytes 4456448 | tf_op jit(solution)/shard_map/all_to_all | solution.py:537
  98.4 34.0 %collective-permute-start = (f32[2,2,64,384]{3,2,1,0:T(8,128)S(1)}, f32[2,2,64,384]{3,2,1,0:T(8,128)S(1)}, u32[]{:S(2)}, u32[]{:S(2)}) collective-permute-start(f32[2,2,64,384]{3,2,1,0:T(8,128)S(1)} %slice.4), channel_id=1, source_target_pairs={{1,0},{2,3},{5,4},{6,7},{9,8},{10,11},{13,12},{14,15},{17,16},{18,... | collective-permute-start | bytes 1179656 | tf_op jit(solution)/shard_map/ppermute | solution.py:614
  132.5 1.5 copy-start
  134.1 1.3 copy-start.1

commit v7 on v6

--- a/solution.py
+++ b/solution.py
@@ -125,16 +125,24 @@
     )
 
 
-def store_send(send_ref, modes, field, field_count, plus, interleave):
-    pieces = [modes[:, 128 * b : 128 * (b + 1)] for b in range(4)]
-    if interleave:
+def store_send(send_ref, modes, field, field_count, plus, interleave, start=None):
+    def owners(values):
+        pieces = [values[:, 128 * b : 128 * (b + 1)] for b in range(4)]
+        if not interleave:
+            return pieces
         low_lane = lax.broadcasted_iota(jnp.int32, pieces[0].shape, 1) < 64
         out = []
         for b in range(2):
             even, odd = pieces[b], pieces[b + 2]
             out.append(jnp.where(low_lane, even, pltpu.roll(odd, 64, 1)))
             out.append(jnp.where(low_lane, pltpu.roll(even, 64, 1), odd))
-        pieces = out
+        return out
+
+    pieces = owners(modes)
+    if start is not None:
+        start = owners(start)
+        pieces[1] = pair_lanes(pieces[1], start[1], False)
+        pieces[2] = pair_lanes(pieces[2], start[2], True)
     phys = modes.shape[0] // plus
     chunk = send_ref.shape[1] // phys
     if chunk < plus * field_count:
@@ -151,34 +159,29 @@
                 send_ref[b, place, :] = pieces[b][start : start + size]
 
 
+def pair_lanes(values, other, upper):
+    lane = lax.broadcasted_iota(jnp.int32, values.shape, 1)
+    if upper:
+        return jnp.where(lane % 32 < 16, pltpu.roll(values, 128 - 16, 1), other)
+    return jnp.where(lane % 32 < 16, values, pltpu.roll(other, 16, 1))
+
+
 def store_levelled(send_ref, pieces, field, field_count):
     phys = 8
     chunk = send_ref.shape[1] // phys
-    lane = lax.broadcasted_iota(jnp.int32, pieces[0].shape, 1)
-    low = lane % 32 < 16
-
-    def pair(values, other, upper):
-        if upper:
-            return jnp.where(low, pltpu.roll(values, 128 - 16, 1), other)
-        return jnp.where(low, values, pltpu.roll(other, 16, 1))
+    own = chunk // field_count
 
     def put(owner, p, unit, rows):
         place = pl.ds(p * chunk + unit * field_count + field, rows.shape[0], stride=field_count)
         send_ref[owner, place, :] = rows
 
-    count = pieces[0].shape[0]
     for end, middle in ((0, 1), (3, 2)):
-        whole, part = pieces[end], pieces[middle]
-        fours = pair(part, pltpu.roll(part, count - 4, 0), middle == 2)
-        ones = pair(part, pltpu.roll(part, count - 1, 0), middle == 2)
+        whole = pieces[end]
         for p in range(phys):
-            tail = 64 + 3 * p
-            put(end, p, 0, whole[8 * p : 8 * p + 8])
-            put(end, p, 8, whole[tail : tail + 1])
-            put(middle, p, 0, whole[tail + 1 : tail + 3])
-            put(middle, p, 2, fours[8 * p : 8 * p + 4])
-            put(middle, p, 6, ones[tail : tail + 1])
-            put(middle, p, 7, ones[tail + 2 : tail + 3])
+            put(end, p, 0, whole[8 * p : 8 * p + own])
+            if own < 8:
+                put(middle, p, 0, whole[8 * p + own : 8 * p + 8])
+            put(middle, p, 8 - own, whole[64 + 3 * p : 67 + 3 * p])
 
 
 def rows_kernel(x_ref, fx_hi, fx_lo, out_ref):
@@ -235,6 +238,7 @@
 
 
 def advance_kernel(
+    levelled,
     interleave,
     field_count,
     plus,
@@ -308,7 +312,8 @@
     for i in range(stack):
         field = pl.program_id(0) * stack + i
         advanced = spectra[i] + step * second[i]
-        store_send(send_ref, advanced, field, field_count, plus, interleave)
+        start = spectra[i] if levelled else None
+        store_send(send_ref, advanced, field, field_count, plus, interleave, start)
 
 
 def angle_kernel(
@@ -316,6 +321,8 @@
     field_count,
     samples,
     turning,
+    kind_ref,
+    turn_ref,
     got_hbm,
     mat_hi,
     mat_lo,
@@ -350,6 +357,12 @@
         for copy in copies:
             copy.start()
         loads.append((first_k, copies))
+    turn_cos, turn_sin = turn_ref[0:1], turn_ref[1:2]
+    kind = None if kind_ref is None else kind_ref[0]
+
+    def turned_back(real, imag):
+        return [turn_sin * imag - turn_cos * real, -(turn_sin * real + turn_cos * imag)]
+
     flat = (got_ref if turning else got_hbm).reshape(sources * chunk, lanes)
     stores = []
     for k in range(plus):
@@ -377,11 +390,22 @@
             near, far = slice(row, row + quarter), slice(row + quarter, row + 2 * quarter)
             real = cosine[near] + sine[far]
             imag = cosine[far] - sine[near]
+            pair = (real, imag)
             if turning:
-                turn_cos, turn_sin = last_ref[0:1], last_ref[1:2]
-                pair = (turn_sin * imag - turn_cos * real, -(turn_sin * real + turn_cos * imag))
-            else:
-                pair = (real, imag)
+                pair = turned_back(real, imag)
+            elif kind_ref is not None:
+                half = quarter // 2
+                late = turned_back(real[half:], imag[half:])
+                for part in range(2):
+                    own = pair[part][:half] + late[part]
+                    none = jnp.zeros_like(own)
+                    own = jnp.where(
+                        kind == 1,
+                        jnp.concatenate([own, none], axis=0),
+                        jnp.concatenate([none, own], axis=0),
+                    )
+                    late[part] = jnp.where(kind == 0, pair[part], own)
+                pair = late
             for part in range(2):
                 for b in range(blocks):
                     place = (k * 2 + part) * blocks + b
@@ -402,23 +426,16 @@
 def place_kernel(kind_ref, units_ref, moved_ref, out_ref):
     kind = kind_ref[0]
     units = units_ref.shape[1]
-    half = out_ref.shape[2] // 2
+    rest = out_ref.shape[1] - units
 
     @pl.when(kind == 0)
     def _():
         out_ref[:, :units] = units_ref[...]
-        out_ref[:, units:] = moved_ref[...]
+        out_ref[:, units:] = moved_ref[:, :rest]
 
     @pl.when(kind > 0)
     def _():
-        first = pl.multiple_of((kind - 1) * half, half)
-        other = pl.multiple_of(half - first, half)
-        pairs = [(2 + k, 0, k) for k in range(4)] + [(2 + k, 1, 4 + k) for k in range(4)]
-        pairs += [(6, 0, 8), (6, 1, 9), (7, 0, 10)]
-        for unit, which, k in pairs:
-            rows = units_ref[:, unit, which * half : (which + 1) * half]
-            out_ref[:, k, pl.ds(first, half), :] = rows
-            out_ref[:, k, pl.ds(other, half), :] = jnp.zeros_like(rows)
+        out_ref[...] = jnp.zeros_like(out_ref)
 
 
 def input_parts(plus, field_count, chunk):
@@ -452,7 +469,7 @@
     count = plus * phys
     direct = row_count == 32 and phys == 8 and group_fields % 32 == 0
     levelled = direct and width // ang == 64 and plus == 11
-    units = 9 if levelled else plus
+    units = 8 if levelled else plus
     start_chunk = -(-units * field_count // 8) * 8
     chunk = -(-plus * field_count // 8) * 8
     block = width // ang
@@ -541,7 +558,7 @@
 
     extra = [force, jnp.asarray(tables["wave_x"]), jnp.asarray(tables["wave_y"])]
     adv_send = pl.pallas_call(
-        functools.partial(advance_kernel, *fixed),
+        functools.partial(advance_kernel, levelled, *fixed),
         grid=(field_count // stack,),
         in_specs=[
             pl.BlockSpec(memory_space=pltpu.SMEM),
@@ -587,12 +604,29 @@
     vmem = pl.BlockSpec(memory_space=pltpu.VMEM)
     hbm = pl.BlockSpec(memory_space=pltpu.HBM)
 
-    def to_angles(got, last, turning, count):
+    ang_index = lax.axis_index("ang")
+    kind = jnp.where((ang_index == 0) | (ang_index == 3), 0, ang_index).astype(jnp.int32)
+    kind = kind.reshape(1)
+    smem = pl.BlockSpec(memory_space=pltpu.SMEM)
+
+    def to_angles(got, last, count):
+        turning = last is None
         shape = (2, count, block, merged)
         parts = len(input_parts(count, field_count, got.shape[1]))
+        kernel = functools.partial(angle_kernel, count, field_count, samples, turning)
+        operands = [(turns, vmem), (got, hbm if turning else vmem), (mat_hi, vmem), (mat_lo, vmem)]
+        if turning:
+            body = lambda turn, got, hi, lo, *rest: kernel(None, turn, got, hi, lo, None, *rest)
+        else:
+            operands.append((last, hbm))
+            if levelled:
+                operands.insert(0, (kind, smem))
+                body = kernel
+            else:
+                body = functools.partial(kernel, None)
         return pl.pallas_call(
-            functools.partial(angle_kernel, count, field_count, samples, turning),
-            in_specs=[hbm if turning else vmem, vmem, vmem, vmem if turning else hbm],
+            body,
+            in_specs=[spec for _, spec in operands],
             out_specs=hbm,
             out_shape=pltpu.HBM(shape, F32),
             scratch_shapes=[
@@ -607,22 +641,20 @@
             cost_estimate=cost(2 * count * 2 * block * 3 * mat_hi.shape[2] * 2 * merged),
             compiler_params=pltpu.CompilerParams(vmem_limit_bytes=20 * 1024 * 1024),
             name="angle",
-        )(got, mat_hi, mat_lo, last)
-
-    start_part = to_angles(start, turns, True, units)
+        )(*[value for value, _ in operands])
+
+    start_part = to_angles(start, None, units)
     if levelled:
         moved = lax.ppermute(start_part[:, : plus - units], "ang", [(1, 0), (2, 3)])
-        ang_index = lax.axis_index("ang")
-        kind = jnp.where((ang_index == 0) | (ang_index == 3), 0, ang_index).astype(jnp.int32)
         start_part = pl.pallas_call(
             place_kernel,
-            in_specs=[pl.BlockSpec(memory_space=pltpu.SMEM), vmem, vmem],
+            in_specs=[smem, vmem, vmem],
             out_specs=vmem,
             out_shape=jax.ShapeDtypeStruct((2, plus, block, merged), F32),
             compiler_params=pltpu.CompilerParams(vmem_limit_bytes=20 * 1024 * 1024),
             name="place",
-        )(kind.reshape(1), start_part, moved)
-    return to_angles(advanced, in_hbm(start_part), False, plus)
+        )(kind, start_part, moved)
+    return to_angles(advanced, in_hbm(start_part), plus)
 
 
 def solution(mesh):

time: 149 us -> 144 us (0.966); the launches traced: 149 us -> 142 us
  waiting for transfers between devices: 50.5 us -> 45.2 us
    all_to_all x2, waiting for transfers between devices: 17.7 us -> 4.43 us  [exchange(): lax.all_to_all(send, ('ang', 'phys'), split_axis=0, concat_axis=0, tiled=...]
    ppermute x1, waiting for transfers between devices: 32.7 us -> 40.8 us  [local(): moved = lax.ppermute(start_part[:, :plus - units], 'ang', [(1, 0), (2, 3)])]
  transfers between devices with their start and end apart: 3 -> 3, of which waited for: 3 -> 3; matrix products, arithmetic and copies ran while one was open for 1% -> 1% of each run, Pallas kernels for 25% -> 26%
where the time goes in v7:
time: 144 us; the launch traced here: 142 us
  Pallas kernels  47.5 us (33%)
  waiting for transfers between devices  45.2 us (31%)
  blocking collectives  32.4 us (22%)
  starting transfers between devices  9.33 us (6%)
  local copies, waits for them, and re-layouts  5.19 us (4%)
  between operations  2.3 us (2%)
    ppermute x1, waiting for transfers between devices, local(): moved = lax.ppermute(start_part[:, :plus - units], 'ang', [(1, 0), (2, 3)])  40.8 us
    pallas_call x1, Pallas kernels, local(): pl.pallas_call(functools.partial(advance_kernel, levelled, *fixed), grid=...  32.6 us
    all_to_all x1, blocking collectives, local(): lax.all_to_all(fields, 'phys', split_axis=0, concat_axis=0, tiled=True)  32.4 us
    pallas_call x2, Pallas kernels, to_angles(): pl.pallas_call(body, in_specs=[spec for _, spec in operands], out_specs=h...  8.76 us
    all_to_all x2, starting transfers between devices, exchange(): lax.all_to_all(send, ('ang', 'phys'), split_axis=0, concat_axis=0, tiled=...  8.04 us
    all_to_all x2, waiting for transfers between devices, exchange(): lax.all_to_all(send, ('ang', 'phys'), split_axis=0, concat_axis=0, tiled=...  4.43 us
    unnamed x24, local copies, waits for them, and re-layouts  3.91 us
    pallas_call x1, Pallas kernels, local(): pl.pallas_call(rows_kernel, grid=(group_fields // step_fields,), in_specs...  3.28 us
  transfers between devices with their start and end apart: 3, of which 3 were waited for; matrix products, arithmetic and copies ran while one was open for 1% of the time, Pallas kernels for 26%

profile of v7, /device:TPU:0, one launch (start us, length us, event | category | flops | bytes accessed | tf_op | source)
XLA Modules:
  0.0 142.0 jit_solution(68770362284575383)
XLA Ops:
  0.0 3.3 %rows.1 = f32[24,176,128]{2,1,0:T(8,128)S(1)} custom-call(f32[96,32,256]{2,1,0:T(8,128)} %bitcast.14, bf16[176,256]{1,0:T(8,128)(2,1)} %constant.52.clone.fx_hi, bf16[176,256]{1,0:T(8,128)(2,1)} %constant.53.clone.fx_lo), custom_call_target="tpu_custom_call" | custom-call | tf_op jit(solution)/shard_map/rows/pallas_call | solution.py:499
  3.3 0.0 copy-start.5
  3.3 0.0 copy-start.6
  3.3 0.0 copy-start.7
  3.3 0.0 copy-start.8
  3.3 32.4 %all_to_all.15 = f32[8,528,128]{2,1,0:T(8,128)S(1)} all-to-all(f32[8,528,128]{2,1,0:T(8,128)S(1)} %bitcast.12), channel_id=1, replica_groups=mesh['phys'=8,'ang'=4] {'phys'}, dimensions={0} | all-to-all | bytes 4325376 | tf_op jit(solution)/shard_map/all_to_all | solution.py:510
  35.7 0.0 copy-done.5
  35.7 0.0 copy-done.6
  35.7 0.0 copy-done.7
  35.7 0.0 copy-done.8
  35.8 2.7 %columns.1 = f32[4,768,128]{2,1,0:T(8,128)S(1)} custom-call(f32[8,3,176,128]{3,2,1,0:T(8,128)S(1)} %bitcast.10, bf16[256,256]{1,0:T(8,128)(2,1)S(1)} %copy-done.8, bf16[256,256]{1,0:T(8,128)(2,1)S(1)} %copy-done.7, bf16[256,256]{1,0:T(8,128)(2,1)S(1)} %copy-done.6, bf16[256,256]{1,0:T(8,128)(2,1)S(1)} %copy-done.5), custom_call_target="tpu_custom_call" | custom-call | tf_op jit(solution)/shard_map/columns/pallas_call | solution.py:513
  38.5 0.0 copy-start.2
  38.5 1.1 copy-done.2
  39.6 0.0 copy-start.9
  39.6 0.0 copy-start.10
  39.6 4.1 %all-to-all-start.1 = ((f32[32,96,128]{2,1,0:T(8,128)}), f32[32,96,128]{2,1,0:T(8,128)}, u32[]{:S(2)}, u32[]{:S(2)}) async-start(f32[32,96,128]{2,1,0:T(8,128)} %bitcast.13), calls=%async_computation.1 | async-start | bytes 3145728 | tf_op jit(solution)/shard_map/all_to_all | solution.py:554
  45.0 0.1 cosine_multiply_fusion.force_ref
  45.1 0.0 copy-done.9
  45.1 0.0 copy-done.10
  45.1 32.6 %advance.1 = f32[4,1088,128]{2,1,0:T(8,128)} custom-call(f32[1]{0:T(128)S(6)} %copy.25.dt_ref, f32[8,3,176,128]{3,2,1,0:T(8,128)S(1)} %bitcast.11, f32[1,256]{1,0:T(1,128)S(1)} %cosine_multiply_fusion.force_ref, f32[88,1]{1,0:T(8,128)S(1)} %copy-done.9, f32[1,512]{1,0:T(1,128)S(1)} %copy-done.10, bf16[176,256]{1,0:T(8,128)(2,1)} %constant.52.clone.fx_hi, ...), custom_call_target="tpu_custom_call" | custom-call | flops 9965666304 | bytes 8388608 | tf_op jit(solution)/shard_map/advance/pallas_call | solution.py:560
  77.7 3.8 %all-to-all-done.1.got = f32[32,96,128]{2,1,0:T(8,128)} async-done(((f32[32,96,128]{2,1,0:T(8,128)}), f32[32,96,128]{2,1,0:T(8,128)}, u32[]{:S(2)}, u32[]{:S(2)}) %all-to-all-start.1) | async-done | bytes 1572896 | tf_op jit(solution)/shard_map/all_to_all | solution.py:554
  81.5 0.0 copy-start.11
  81.5 0.0 copy-start.3
  81.5 0.0 copy-start.4
  81.5 4.0 %all-to-all-start.2 = ((f32[32,136,128]{2,1,0:T(8,128)}), f32[32,136,128]{2,1,0:T(8,128)S(1)}, u32[]{:S(2)}, u32[]{:S(2)}) async-start(f32[32,136,128]{2,1,0:T(8,128)} %bitcast.15), calls=%async_computation.2 | async-start | bytes 4456448 | tf_op jit(solution)/shard_map/all_to_all | solution.py:554
  86.1 0.0 copy-done.11
  86.1 0.1 stack_tile.6
  86.2 0.1 stack_tile.7
  86.3 0.0 copy-done.3
  86.3 0.0 copy-done.4
  86.4 4.0 %angle.2.units_ref = f32[2,8,64,384]{3,2,1,0:T(8,128)} custom-call(f32[2,384]{1,0:T(2,128)S(1)} %pad_maximum_fusion.turn.turn_ref, f32[32,96,128]{2,1,0:T(8,128)} %all-to-all-done.1.got, bf16[1,192,96]{2,1,0:T(8,128)(2,1)S(1)} %copy-done.4, bf16[1,192,96]{2,1,0:T(8,128)(2,1)S(1)} %copy-done.3), custom_call_target="tpu_custom_call" | custom-call | flops 452984832 | bytes 8388608 | tf_op jit(solution)/shard_map/angle/pallas_call | solution.py:627
  90.4 1.1 slice.4
  91.5 1.3 collective-permute-start
  92.8 40.8 %collective-permute-done.moved_ref = f32[2,3,64,384]{3,2,1,0:T(8,128)S(1)} collective-permute-done((f32[2,3,64,384]{3,2,1,0:T(8,128)S(1)}, f32[2,3,64,384]{3,2,1,0:T(8,128)S(1)}, u32[]{:S(2)}, u32[]{:S(2)}) %collective-permute-start) | collective-permute-done | bytes 589856 | tf_op jit(solution)/shard_map/ppermute | solution.py:648
  133.6 0.0 copy-start
  133.6 1.4 copy-done
  135.0 0.1 place.1.last_ref
  135.1 0.0 copy-start.1
  135.2 1.3 copy-done.1
  136.5 0.6 all-to-all-done.2.got_hbm
  137.1 4.7 %angle.3 = f32[2,11,64,384]{3,2,1,0:T(8,128)} custom-call(s32[1]{0:T(128)} %bitcast.kind_ref, f32[2,384]{1,0:T(2,128)S(1)} %pad_maximum_fusion.turn.turn_ref, f32[32,136,128]{2,1,0:T(8,128)S(1)} %all-to-all-done.2.got_hbm, bf16[1,192,96]{2,1,0:T(8,128)(2,1)S(1)} %copy-done.4, bf16[1,192,96]{2,1,0:T(8,128)(2,1)S(1)} %copy-done.3, f32[2,11,64,384]{3,2,1,0:T(8,128)} %copy-done.1), custom_call_target="tpu_custom_call" | custom-call | flops 622854144 | bytes 8388608 | tf_op jit(solution)/shard_map/angle/pallas_call | solution.py:627
  (4 shorter events, 0.1 us)
Async XLA Ops:
  3.3 32.5 %copy-start.5 = (bf16[256,256]{1,0:T(8,128)(2,1)S(1)}, bf16[256,256]{1,0:T(8,128)(2,1)}, u32[]{:S(2)}) copy-start(bf16[256,256]{1,0:T(8,128)(2,1)} %constant.57.clone.o_lo) | copy-start | bytes 393220
  3.3 32.4 %copy-start.6 = (bf16[256,256]{1,0:T(8,128)(2,1)S(1)}, bf16[256,256]{1,0:T(8,128)(2,1)}, u32[]{:S(2)}) copy-start(bf16[256,256]{1,0:T(8,128)(2,1)} %constant.56.clone.o_hi) | copy-start | bytes 393220
  3.3 32.4 %copy-start.7 = (bf16[256,256]{1,0:T(8,128)(2,1)S(1)}, bf16[256,256]{1,0:T(8,128)(2,1)}, u32[]{:S(2)}) copy-start(bf16[256,256]{1,0:T(8,128)(2,1)} %constant.55.clone.e_lo) | copy-start | bytes 393220
  3.3 32.4 %copy-start.8 = (bf16[256,256]{1,0:T(8,128)(2,1)S(1)}, bf16[256,256]{1,0:T(8,128)(2,1)}, u32[]{:S(2)}) copy-start(bf16[256,256]{1,0:T(8,128)(2,1)} %constant.54.clone.e_hi) | copy-start | bytes 393220
  38.5 1.1 copy-start.2
  39.6 5.5 %copy-start.9 = (f32[88,1]{1,0:T(8,128)S(1)}, f32[88,1]{1,0:T(8,128)}, u32[]{:S(2)}) copy-start(f32[88,1]{1,0:T(8,128)} %constant.66.clone.wave_x_ref) | copy-start | bytes 1060
  39.6 5.5 %copy-start.10 = (f32[1,512]{1,0:T(1,128)S(1)}, f32[1,512]{1,0:T(1,128)}, u32[]{:S(2)}) copy-start(f32[1,512]{1,0:T(1,128)} %constant.67.clone.wave_y_ref) | copy-start | bytes 6148
  39.6 41.8 %all-to-all-start.1 = ((f32[32,96,128]{2,1,0:T(8,128)}), f32[32,96,128]{2,1,0:T(8,128)}, u32[]{:S(2)}, u32[]{:S(2)}) async-start(f32[32,96,128]{2,1,0:T(8,128)} %bitcast.13), calls=%async_computation.1 | async-start | bytes 3145728 | tf_op jit(solution)/shard_map/all_to_all | solution.py:554
  81.5 4.6 %copy-start.11 = (f32[96]{0:T(128)S(1)}, f32[96]{0:T(128)}, u32[]{:S(2)}) copy-start(f32[96]{0:T(128)} %constant.70.clone) | copy-start | bytes 1156
  81.5 4.9 %copy-start.3 = (bf16[1,192,96]{2,1,0:T(8,128)(2,1)S(1)}, bf16[1,192,96]{2,1,0:T(8,128)(2,1)}, u32[]{:S(2)}) copy-start(bf16[1,192,96]{2,1,0:T(8,128)(2,1)} %constant.69.clone.lo.mat_lo) | copy-start | bytes 110596
  81.5 4.9 %copy-start.4 = (bf16[1,192,96]{2,1,0:T(8,128)(2,1)S(1)}, bf16[1,192,96]{2,1,0:T(8,128)(2,1)}, u32[]{:S(2)}) copy-start(bf16[1,192,96]{2,1,0:T(8,128)(2,1)} %constant.68.clone.hi.mat_hi) | copy-start | bytes 110596
  81.5 55.6 %all-to-all-start.2 = ((f32[32,136,128]{2,1,0:T(8,128)}), f32[32,136,128]{2,1,0:T(8,128)S(1)}, u32[]{:S(2)}, u32[]{:S(2)}) async-start(f32[32,136,128]{2,1,0:T(8,128)} %bitcast.15), calls=%async_computation.2 | async-start | bytes 4456448 | tf_op jit(solution)/shard_map/all_to_all | solution.py:554
  91.5 42.1 %collective-permute-start = (f32[2,3,64,384]{3,2,1,0:T(8,128)S(1)}, f32[2,3,64,384]{3,2,1,0:T(8,128)S(1)}, u32[]{:S(2)}, u32[]{:S(2)}) collective-permute-start(f32[2,3,64,384]{3,2,1,0:T(8,128)S(1)} %slice.4), channel_id=1, source_target_pairs={{1,0},{2,3},{5,4},{6,7},{9,8},{10,11},{13,12},{14,15},{17,16},{18,... | collective-permute-start | bytes 1769480 | tf_op jit(solution)/shard_map/ppermute | solution.py:648
  133.6 1.4 copy-start
  135.1 1.3 copy-start.1
